TPU v7x, 512 devices: a whole 4x4x16 slice. The times are simulated.
512 devices in a mesh: grp: 64 (over z, x), own: 8 (over y, core).
Axes of the slice: x: 4, y: 4, z: 16, core: 2. Of those that a mesh axis runs over, the one named last changes fastest.
Arguments:
- excitation: bfloat16 [4, 8192, 256], P(None, ('grp', 'own')), may hold values from -6 to 6
- cur_hist: bfloat16 [4, 8192, 256], P(None, ('grp', 'own')), may hold values from -6 to 6
- ret_hist: bfloat16 [4, 8192, 256], P(None, ('grp', 'own')), may hold values from -6 to 6
- pole_state: float32 [16, 8192, 256], P(None, ('grp', 'own')), may hold values from -12 to 12
- self_inverse: bfloat16 [8192, 256, 256], P(('grp', 'own')), may hold values from -0.375 to 0.375
- near_mats: bfloat16 [2, 256, 256], replicated, may hold values from -0.09375 to 0.09375
- far_mats: bfloat16 [16, 256, 256], replicated, may hold values from -0.0234375 to 0.0234375
- poles: float32 [16], replicated, may hold values from 0.3 to 0.97
- residues: float32 [16], replicated, may hold values from -0.3 to 0.3
- near_src: int32 [2, 8192, 2], P(None, ('grp', 'own')), may hold values from 0 to 15
- near_delay: int32 [2, 8192, 2], P(None, ('grp', 'own')), may hold values from 1 to 4
- far_dest: int32 [8192, 4], P(('grp', 'own')), may hold values from 0 to 63, all different within a row; in each aligned block of 16 rows (0 to 15, 16 to 31, ...) at most 2 rows name the same one
- far_delay: int32 [8192, 4], P(('grp', 'own')), may hold values from 1 to 4
- far_reader: int32 [64, 64, 8, 2, 16], P('grp', None, 'own'), may hold values from 0 to 127
Outputs:
- currents: bfloat16 [4, 8192, 256], P(None, ('grp', 'own'))
- pole_final: float32 [16, 8192, 256], P(None, ('grp', 'own'))
Inputs may be any that keep to these rules, and one draw needn't show every extreme that they name: `far_dest`: each source tile names 4 different groups; among the tiles of one aligned block of 16 tiles no group is named by more than 2 tiles.
All inputs are finite; a program needn't handle non-finite values.
Results may differ from a plain program's by a relative error of at most 0.018.
Values may be sent and summed in bfloat16 or wider, within the bound.
No kernel may reach another device: no remote copies, remote signals or barrier semaphores. Data moves between devices by JAX's collectives and lax.ppermute only.
A program may use at most 64 MiB of HBM per device.

v0:
```python
import jax
import jax.numpy as jnp
from jax import lax
from jax.sharding import PartitionSpec as P

STEPS = 4


def body(
    excitation,
    cur_hist,
    ret_hist,
    pole_state,
    self_inverse,
    near_mats,
    far_mats,
    poles,
    residues,
    near_src,
    near_delay,
    far_dest,
    far_delay,
    far_reader,
):
    group_count = far_reader.shape[1]
    slot_count = far_reader.shape[3]
    class_count = far_reader.shape[4]
    tile_count = excitation.shape[1]
    group_tiles = tile_count * lax.axis_size("own")
    readers = far_reader.reshape(group_count * slot_count, class_count)
    reader_hits = (
        readers.T[:, None, :] == jnp.arange(group_tiles, dtype=jnp.int32)[None, :, None]
    ).astype(jnp.bfloat16)
    named_by = (far_dest[:, :, None] == jnp.arange(group_count, dtype=jnp.int32)).astype(jnp.int32)
    per_tile = named_by.sum(1)
    before = jnp.cumsum(per_tile, axis=0) - per_tile
    slot_rank = jnp.take_along_axis(before, far_dest, axis=1)
    local_ids = jnp.broadcast_to(jnp.arange(tile_count, dtype=jnp.int32)[:, None], far_dest.shape)
    basis_width = excitation.shape[2]
    history_cur = cur_hist
    history_ret = ret_hist
    pole_now = pole_state
    outputs = []
    for time_step in range(STEPS):
        blocks = history_ret[far_delay - 1, local_ids]
        outgoing = (
            jnp.zeros((group_count, slot_count, basis_width), jnp.bfloat16)
            .at[far_dest, slot_rank]
            .set(blocks)
        )
        far_terms = jnp.einsum(
            "gcb,kab->gcka",
            lax.all_to_all(outgoing, "grp", split_axis=0, concat_axis=0, tiled=True),
            far_mats,
            preferred_element_type=jnp.float32,
        ).astype(jnp.bfloat16)
        far_terms = far_terms.reshape(group_count * slot_count, class_count, basis_width)
        group_part = jnp.einsum(
            "kqs,ska->qa", reader_hits, far_terms, preferred_element_type=jnp.float32
        )
        near_rows = history_cur[near_delay - 1, near_src]
        near_field = jnp.einsum(
            "ktmb,kab->ta", near_rows, near_mats, preferred_element_type=jnp.float32
        )
        group_total = lax.psum(group_part, "own")
        far_field = lax.dynamic_slice_in_dim(
            group_total, lax.axis_index("own") * tile_count, tile_count, 0
        )
        right_side = (excitation[time_step].astype(jnp.float32) - near_field - far_field).astype(
            jnp.bfloat16
        )
        current_now = jnp.einsum(
            "tab,tb->ta", self_inverse, right_side, preferred_element_type=jnp.float32
        ).astype(jnp.bfloat16)
        current_now = lax.optimization_barrier(current_now)
        outputs.append(current_now)
        current_wide = current_now.astype(jnp.float32)
        pole_now = poles[:, None, None] * pole_now + current_wide[None]
        retarded_now = (current_wide + jnp.einsum("p,ptb->tb", residues, pole_now)).astype(
            jnp.bfloat16
        )
        history_cur = jnp.concatenate([current_now[None], history_cur[:-1]], axis=0)
        history_ret = jnp.concatenate([retarded_now[None], history_ret[:-1]], axis=0)
    return (jnp.stack(outputs), pole_now)


def solution(mesh):
    in_specs = (
        P(None, ("grp", "own"), None),
        P(None, ("grp", "own"), None),
        P(None, ("grp", "own"), None),
        P(None, ("grp", "own"), None),
        P(("grp", "own"), None, None),
        P(),
        P(),
        P(),
        P(),
        P(None, ("grp", "own"), None),
        P(None, ("grp", "own"), None),
        P(("grp", "own"), None),
        P(("grp", "own"), None),
        P("grp", None, "own", None, None),
    )
    out_specs = (P(None, ("grp", "own"), None), P(None, ("grp", "own"), None))
    return jax.shard_map(body, mesh=mesh, in_specs=in_specs, out_specs=out_specs, check_vma=False)
```

profile of v0, /device:TPU:1, one launch (start us, length us, event | category | flops | bytes accessed | tf_op | source)
XLA Modules:
  0.0 459.1 jit_solution(701371521254957817)
XLA Ops:
  7.2 0.9 convert_reduce_fusion
  10.8 0.8 gather_fusion.1
  12.3 7.7 %scatter_fusion = bf16[64,2,256]{2,1,0:T(2,128)(2,1)} fusion(bf16[64,2,256]{2,1,0:T(2,128)(2,1)} %broadcast.68.clone, s32[64]{0:T(128)S(1)} %reshape.120, bf16[64,256]{1,0:T(8,128)(2,1)S(1)} %gather_fusion.1), kind=kCustom, calls=%fused_computation.9 | custom fusion | bytes 98816 | tf_op jit(solution)/shard_map/scatter | solution.py:49
  20.0 19.1 %all-to-all-start = ((bf16[64,2,256]{2,1,0:T(2,128)(2,1)}), bf16[64,2,256]{2,1,0:T(2,128)(2,1)S(1)}, u32[]{:S(2)}, u32[]{:S(2)}) async-start(bf16[64,2,256]{2,1,0:T(2,128)(2,1)} %scatter_fusion), calls=%async_computation | async-start | bytes 131072 | tf_op jit(solution)/shard_map/all_to_all | solution.py:53
  39.3 13.8 %all-to-all-done = bf16[64,2,256]{2,1,0:T(2,128)(2,1)S(1)} async-done(((bf16[64,2,256]{2,1,0:T(2,128)(2,1)}), bf16[64,2,256]{2,1,0:T(2,128)(2,1)S(1)}, u32[]{:S(2)}, u32[]{:S(2)}) %all-to-all-start) | async-done | bytes 65568 | tf_op jit(solution)/shard_map/all_to_all | solution.py:53
  54.6 1.4 convolution_bitcast_fusion.3
  56.3 0.8 gather_fusion
  57.3 63.4 %all-reduce.5.cloned.1.call-done = f32[128,256]{1,0:T(8,128)} async-done(((f32[128,256]{1,0:T(8,128)}), f32[128,256]{1,0:T(8,128)}) %all-reduce.5.cloned.1.call-update) | async-done | bytes 131088 | tf_op jit(solution)/shard_map/psum | solution.py:65
  120.7 0.9 fusion.35
  121.5 2.2 fusion.69
  125.7 7.7 %scatter_fusion.1 = bf16[64,2,256]{2,1,0:T(2,128)(2,1)} fusion(bf16[64,2,256]{2,1,0:T(2,128)(2,1)} %broadcast.68.clone.1, s32[64]{0:T(128)S(1)} %reshape.120, bf16[64,256]{1,0:T(8,128)(2,1)S(1)} %gather_fusion.3), kind=kCustom, calls=%fused_computation.10 | custom fusion | bytes 98816 | tf_op jit(solution)/shard_map/scatter | solution.py:49
  133.4 14.7 %all-to-all-start.1 = ((bf16[64,2,256]{2,1,0:T(2,128)(2,1)}), bf16[64,2,256]{2,1,0:T(2,128)(2,1)S(1)}, u32[]{:S(2)}, u32[]{:S(2)}) async-start(bf16[64,2,256]{2,1,0:T(2,128)(2,1)} %scatter_fusion.1), calls=%async_computation.1 | async-start | bytes 131072 | tf_op jit(solution)/shard_map/all_to_all | solution.py:53
  149.3 12.9 %all-to-all-done.1 = bf16[64,2,256]{2,1,0:T(2,128)(2,1)S(1)} async-done(((bf16[64,2,256]{2,1,0:T(2,128)(2,1)}), bf16[64,2,256]{2,1,0:T(2,128)(2,1)S(1)}, u32[]{:S(2)}, u32[]{:S(2)}) %all-to-all-start.1) | async-done | bytes 65568 | tf_op jit(solution)/shard_map/all_to_all | solution.py:53
  163.6 1.4 convolution_bitcast_fusion.2
  165.0 64.7 %all-reduce.7.cloned.1.call-done = f32[128,256]{1,0:T(8,128)} async-done(((f32[128,256]{1,0:T(8,128)}), f32[128,256]{1,0:T(8,128)}) %all-reduce.7.cloned.1.call-update) | async-done | bytes 131088 | tf_op jit(solution)/shard_map/psum | solution.py:65
  229.7 0.9 fusion.34
  230.6 2.2 fusion.67
  234.8 7.7 %scatter_fusion.2 = bf16[64,2,256]{2,1,0:T(2,128)(2,1)} fusion(bf16[64,2,256]{2,1,0:T(2,128)(2,1)} %broadcast.68.clone.2, s32[64]{0:T(128)S(1)} %reshape.120, bf16[64,256]{1,0:T(8,128)(2,1)S(1)} %gather_fusion.5), kind=kCustom, calls=%fused_computation.11 | custom fusion | bytes 98816 | tf_op jit(solution)/shard_map/scatter | solution.py:49
  242.5 14.7 %all-to-all-start.2 = ((bf16[64,2,256]{2,1,0:T(2,128)(2,1)}), bf16[64,2,256]{2,1,0:T(2,128)(2,1)S(1)}, u32[]{:S(2)}, u32[]{:S(2)}) async-start(bf16[64,2,256]{2,1,0:T(2,128)(2,1)} %scatter_fusion.2), calls=%async_computation.2 | async-start | bytes 131072 | tf_op jit(solution)/shard_map/all_to_all | solution.py:53
  258.2 13.1 %all-to-all-done.2 = bf16[64,2,256]{2,1,0:T(2,128)(2,1)S(1)} async-done(((bf16[64,2,256]{2,1,0:T(2,128)(2,1)}), bf16[64,2,256]{2,1,0:T(2,128)(2,1)S(1)}, u32[]{:S(2)}, u32[]{:S(2)}) %all-to-all-start.2) | async-done | bytes 65568 | tf_op jit(solution)/shard_map/all_to_all | solution.py:53
  272.7 1.4 convolution_bitcast_fusion.1
  274.1 64.7 %all-reduce.9.cloned.1.call-done = f32[128,256]{1,0:T(8,128)} async-done(((f32[128,256]{1,0:T(8,128)}), f32[128,256]{1,0:T(8,128)}) %all-reduce.9.cloned.1.call-update) | async-done | bytes 131088 | tf_op jit(solution)/shard_map/psum | solution.py:65
  338.8 0.9 fusion.33
  339.7 2.2 fusion.65
  343.9 7.7 %scatter_fusion.3 = bf16[64,2,256]{2,1,0:T(2,128)(2,1)} fusion(bf16[64,2,256]{2,1,0:T(2,128)(2,1)} %broadcast.68, s32[64]{0:T(128)S(1)} %reshape.120, bf16[64,256]{1,0:T(8,128)(2,1)S(1)} %gather_fusion.7), kind=kCustom, calls=%fused_computation.12 | custom fusion | bytes 98816 | tf_op jit(solution)/shard_map/scatter | solution.py:49
  351.6 14.7 %all-to-all-start.3 = ((bf16[64,2,256]{2,1,0:T(2,128)(2,1)}), bf16[64,2,256]{2,1,0:T(2,128)(2,1)S(1)}, u32[]{:S(2)}, u32[]{:S(2)}) async-start(bf16[64,2,256]{2,1,0:T(2,128)(2,1)} %scatter_fusion.3), calls=%async_computation.3 | async-start | bytes 131072 | tf_op jit(solution)/shard_map/all_to_all | solution.py:53
  366.5 13.8 %all-to-all-done.3 = bf16[64,2,256]{2,1,0:T(2,128)(2,1)S(1)} async-done(((bf16[64,2,256]{2,1,0:T(2,128)(2,1)}), bf16[64,2,256]{2,1,0:T(2,128)(2,1)S(1)}, u32[]{:S(2)}, u32[]{:S(2)}) %all-to-all-start.3) | async-done | bytes 65568 | tf_op jit(solution)/shard_map/all_to_all | solution.py:53
  381.8 1.4 convolution_bitcast_fusion
  384.2 63.7 %all-reduce.11.cloned.1.call-done = f32[128,256]{1,0:T(8,128)} async-done(((f32[128,256]{1,0:T(8,128)}), f32[128,256]{1,0:T(8,128)}) %all-reduce.11.cloned.1.call-update) | async-done | bytes 131088 | tf_op jit(solution)/shard_map/psum | solution.py:65
  447.9 0.9 fusion.32
  448.8 2.2 fusion.63
  451.1 0.8 multiply_add_fusion
  (114 shorter events, 19.3 us)
Async XLA Ops:
  7.2 45.9 %copy-start = (bf16[16,256,256]{2,1,0:T(8,128)(2,1)S(1)}, bf16[16,256,256]{2,1,0:T(8,128)(2,1)}, u32[]{:S(2)}) copy-start(bf16[16,256,256]{2,1,0:T(8,128)(2,1)} %param.20) | copy-start | bytes 6291460
  9.2 1.2 copy-start.8
  9.2 1.6 copy-start.3
  9.2 30.0 %copy-start.6 = (s32[1,64,1,2,16]{1,4,3,2,0:T(8,128)S(1)}, s32[1,64,1,2,16]{1,4,3,2,0:T(8,128)}, u32[]{:S(2)}) copy-start(s32[1,64,1,2,16]{1,4,3,2,0:T(8,128)} %param.27) | copy-start | bytes 24580
  20.0 33.1 %all-to-all-start = ((bf16[64,2,256]{2,1,0:T(2,128)(2,1)}), bf16[64,2,256]{2,1,0:T(2,128)(2,1)S(1)}, u32[]{:S(2)}, u32[]{:S(2)}) async-start(bf16[64,2,256]{2,1,0:T(2,128)(2,1)} %scatter_fusion), calls=%async_computation | async-start | bytes 131072 | tf_op jit(solution)/shard_map/all_to_all | solution.py:53
  39.1 81.6 %all-reduce.5.cloned.1.call-start = ((), (), s32[]{:S(2)}) async-start(), calls=%async_computation.4 | async-start | bytes 262144 | tf_op jit(solution)/shard_map/psum | solution.py:65
  53.9 2.1 copy-start.9
  53.9 2.1 copy-start.10
  53.9 2.4 copy-start.4
  54.0 66.7 %copy-start.1 = (bf16[2,256,256]{2,1,0:T(8,128)(2,1)S(1)}, bf16[2,256,256]{2,1,0:T(8,128)(2,1)}, u32[]{:S(2)}) copy-start(bf16[2,256,256]{2,1,0:T(8,128)(2,1)} %param.19) | copy-start | bytes 786436
  54.0 66.7 %copy-start.5 = (bf16[4,16,256]{2,1,0:T(8,128)(2,1)S(1)}, bf16[4,16,256]{2,1,0:T(8,128)(2,1)}, u32[]{:S(2)}) copy-start(bf16[4,16,256]{2,1,0:T(8,128)(2,1)} %param.14) | copy-start | bytes 98308
  54.6 69.2 %copy-start.2 = (f32[16,16,256]{2,1,0:T(8,128)S(1)}, f32[16,16,256]{2,1,0:T(8,128)}, u32[]{:S(2)}) copy-start(f32[16,16,256]{2,1,0:T(8,128)} %param.17) | copy-start | bytes 786436
  54.6 69.2 %copy-start.7 = (f32[16]{0:T(128)S(1)}, f32[16]{0:T(128)}, u32[]{:S(2)}) copy-start(f32[16]{0:T(128)} %param.21) | copy-start | bytes 196
  56.0 67.9 %copy-start.11 = (f32[16]{0:T(128)S(1)}, f32[16]{0:T(128)}, u32[]{:S(2)}) copy-start(f32[16]{0:T(128)} %param.22) | copy-start | bytes 196
  133.4 28.8 %all-to-all-start.1 = ((bf16[64,2,256]{2,1,0:T(2,128)(2,1)}), bf16[64,2,256]{2,1,0:T(2,128)(2,1)S(1)}, u32[]{:S(2)}, u32[]{:S(2)}) async-start(bf16[64,2,256]{2,1,0:T(2,128)(2,1)} %scatter_fusion.1), calls=%async_computation.1 | async-start | bytes 131072 | tf_op jit(solution)/shard_map/all_to_all | solution.py:53
  148.1 81.6 %all-reduce.7.cloned.1.call-start = ((), (), s32[]{:S(2)}) async-start(), calls=%async_computation.5 | async-start | bytes 262144 | tf_op jit(solution)/shard_map/psum | solution.py:65
  242.5 28.8 %all-to-all-start.2 = ((bf16[64,2,256]{2,1,0:T(2,128)(2,1)}), bf16[64,2,256]{2,1,0:T(2,128)(2,1)S(1)}, u32[]{:S(2)}, u32[]{:S(2)}) async-start(bf16[64,2,256]{2,1,0:T(2,128)(2,1)} %scatter_fusion.2), calls=%async_computation.2 | async-start | bytes 131072 | tf_op jit(solution)/shard_map/all_to_all | solution.py:53
  257.1 81.7 %all-reduce.9.cloned.1.call-start = ((), (), s32[]{:S(2)}) async-start(), calls=%async_computation.6 | async-start | bytes 262144 | tf_op jit(solution)/shard_map/psum | solution.py:65
  351.6 28.8 %all-to-all-start.3 = ((bf16[64,2,256]{2,1,0:T(2,128)(2,1)}), bf16[64,2,256]{2,1,0:T(2,128)(2,1)S(1)}, u32[]{:S(2)}, u32[]{:S(2)}) async-start(bf16[64,2,256]{2,1,0:T(2,128)(2,1)} %scatter_fusion.3), calls=%async_computation.3 | async-start | bytes 131072 | tf_op jit(solution)/shard_map/all_to_all | solution.py:53
  366.3 81.6 %all-reduce.11.cloned.1.call-start = ((), (), s32[]{:S(2)}) async-start(), calls=%async_computation.7 | async-start | bytes 262144 | tf_op jit(solution)/shard_map/psum | solution.py:65
Sparse Core Ops, SparseCore 0:
  56.2 64.4 all-reduce.4
  165.2 64.5 all-reduce.6
  274.2 64.5 all-reduce.8
  383.3 64.5 all-reduce.10
where the time goes:
time: 461 us; the launch traced here: 459 us
  waiting for transfers between devices  310 us (67%)
  starting transfers between devices  63.7 us (14%)
  local copies, waits for them, and re-layouts  45.6 us (10%)
  matrix products  22.2 us (5%)
  between operations  14.2 us (3%)
    psum x4, waiting for transfers between devices, body(): group_total = lax.psum(group_part, 'own')  256 us
    all_to_all x4, starting transfers between devices, body(): lax.all_to_all(outgoing, 'grp', split_axis=0, concat_axis=0, tiled=True)  63.1 us
    all_to_all x4, waiting for transfers between devices, body(): lax.all_to_all(outgoing, 'grp', split_axis=0, concat_axis=0, tiled=True)  53.6 us
    scatter x4, local copies, waits for them, and re-layouts, body(): outgoing = jnp.zeros((group_count, slot_count, basis_width), jnp.bfloat16...  30.8 us
  transfers between devices with their start and end apart: 8, of which 8 were waited for; matrix products, arithmetic and copies ran while one was open for 1% of the time, Pallas kernels for 0%

commit v1 on v0

v1 whole, which is shorter than its diff:
```python
import jax
import jax.numpy as jnp
from jax import lax
from jax.sharding import PartitionSpec as P

STEPS = 4
HIST = 4
F32 = jnp.float32
BF16 = jnp.bfloat16


def body(
    excitation,
    cur_hist,
    ret_hist,
    pole_state,
    self_inverse,
    near_mats,
    far_mats,
    poles,
    residues,
    near_src,
    near_delay,
    far_dest,
    far_delay,
    far_reader,
):
    groups = far_reader.shape[1]
    cap = far_reader.shape[3]
    classes = far_reader.shape[4]
    tiles = excitation.shape[1]
    width = excitation.shape[2]
    owners = lax.axis_size("own")
    group_tiles = tiles * owners
    slots = groups * cap

    named_by = far_dest[:, :, None] == jnp.arange(groups, dtype=jnp.int32)
    named = named_by.any(1)
    named_int = named.astype(jnp.int32)
    rank = jnp.cumsum(named_int, axis=0) - named_int
    delay_of = jnp.sum(jnp.where(named_by, far_delay[:, :, None], 0), axis=1)
    send_pick = (
        named.T[:, None, None, :]
        & (rank.T[:, None, None, :] == jnp.arange(cap, dtype=jnp.int32)[None, :, None, None])
        & (
            delay_of.T[:, None, None, :]
            == jnp.arange(1, HIST + 1, dtype=jnp.int32)[None, None, :, None]
        )
    )
    send_pick = send_pick.reshape(slots, HIST * tiles).astype(BF16)

    readers = far_reader.reshape(slots, classes)
    reader_hits = (
        readers.T[None, :, :] == jnp.arange(group_tiles, dtype=jnp.int32)[:, None, None]
    ).astype(BF16)
    reader_hits = reader_hits.reshape(group_tiles, classes * slots)

    near_row = (near_delay - 1) * tiles + near_src
    near_pick = (
        near_row[..., None] == jnp.arange(HIST * tiles, dtype=jnp.int32)
    ).astype(BF16)
    near_pick = near_pick.transpose(0, 2, 1, 3)

    power = [jnp.ones_like(poles)]
    for _ in range(STEPS):
        power.append(power[-1] * poles)
    tail = [
        jnp.sum((residues * power[n + 1])[:, None, None] * pole_state, axis=0)
        for n in range(STEPS)
    ]
    weight = [jnp.sum(residues * power[j]) for j in range(STEPS)]

    history_cur = cur_hist
    history_ret = ret_hist
    outputs = []
    for step in range(STEPS):
        outgoing = jnp.dot(send_pick, history_ret.reshape(HIST * tiles, width))
        incoming = lax.all_to_all(
            outgoing.reshape(groups, cap, width), "grp", split_axis=0, concat_axis=0, tiled=True
        ).reshape(slots, width)
        near_rows = jnp.einsum(
            "kmth,hb->kmtb", near_pick, history_cur.reshape(HIST * tiles, width)
        )
        near_field = jnp.einsum(
            "kmtb,kab->ta", near_rows, near_mats, preferred_element_type=F32
        )
        far_terms = jnp.einsum(
            "sb,kab->ksa", incoming, far_mats, preferred_element_type=F32
        ).astype(BF16)
        group_part = jnp.dot(
            reader_hits, far_terms.reshape(classes * slots, width), preferred_element_type=F32
        ).astype(BF16)
        parts = lax.all_to_all(
            group_part.reshape(owners, tiles, width), "own", split_axis=0, concat_axis=0, tiled=True
        )
        far_field = jnp.sum(parts.astype(F32), axis=0)
        right_side = (excitation[step].astype(F32) - near_field - far_field).astype(BF16)
        current_now = jnp.einsum(
            "tab,tb->ta", self_inverse, right_side, preferred_element_type=F32
        ).astype(BF16)
        current_now = lax.optimization_barrier(current_now)
        outputs.append(current_now)
        if step + 1 < STEPS:
            retarded = current_now.astype(F32) + tail[step]
            for back in range(step + 1):
                retarded = retarded + weight[back] * outputs[step - back].astype(F32)
            history_cur = jnp.concatenate([current_now[None], history_cur[:-1]], axis=0)
            history_ret = jnp.concatenate(
                [retarded.astype(BF16)[None], history_ret[:-1]], axis=0
            )
    pole_final = power[STEPS][:, None, None] * pole_state
    for step in range(STEPS):
        pole_final = pole_final + power[STEPS - 1 - step][:, None, None] * outputs[step].astype(
            F32
        )
    return (jnp.stack(outputs), pole_final)


def solution(mesh):
    in_specs = (
        P(None, ("grp", "own"), None),
        P(None, ("grp", "own"), None),
        P(None, ("grp", "own"), None),
        P(None, ("grp", "own"), None),
        P(("grp", "own"), None, None),
        P(),
        P(),
        P(),
        P(),
        P(None, ("grp", "own"), None),
        P(None, ("grp", "own"), None),
        P(("grp", "own"), None),
        P(("grp", "own"), None),
        P("grp", None, "own", None, None),
    )
    out_specs = (P(None, ("grp", "own"), None), P(None, ("grp", "own"), None))
    return jax.shard_map(body, mesh=mesh, in_specs=in_specs, out_specs=out_specs, check_vma=False)
```

time: 461 us -> 162 us (0.35)
  waiting for transfers between devices: 310 us -> 70.6 us
  local copies, waits for them, and re-layouts: 45.6 us -> 3.89 us
  between operations: 14.2 us -> 0.93 us
  starting transfers between devices: 63.7 us -> 56 us
  other arithmetic: 3.28 us -> 10.3 us
    psum x4 -> x0, waiting for transfers between devices: 256 us -> none  [body(): group_total = lax.psum(group_part, 'own')]
    scatter x4 -> x0, local copies, waits for them, and re-layouts: 30.8 us -> none  [body(): outgoing = jnp.zeros((group_count, slot_count, basis_width), jnp.bfloat16...]
    all_to_all x4 -> x8, waiting for transfers between devices: 53.6 us -> 70.6 us  [the longest x4 51.5 us: body(): lax.all_to_all(outgoing.reshape(groups, cap, width), 'grp', split_axis=0,...]
    gather x12 -> x0, local copies, waits for them, and re-layouts: 7.73 us -> none  [the longest x4 3.33 us: body(): near_rows = history_cur[near_delay - 1, near_src]]
    all_to_all x4 -> x8, starting transfers between devices: 63.1 us -> 56 us  [the longest x4 33 us: body(): lax.all_to_all(outgoing.reshape(groups, cap, width), 'grp', split_axis=0,...]
    dot_general x15 -> x16, matrix products: 13.2 us -> 9.93 us  [the longest x4 6.89 us: body(): jnp.dot(reader_hits, far_terms.reshape(classes * slots, width), preferred...]
  transfers between devices with their start and end apart: 8 -> 8, of which waited for: 8 -> 8; matrix products, arithmetic and copies ran while one was open for 1% -> 3% of each run, Pallas kernels for 0% -> 0%
where the time goes in v1:
time: 162 us; the launch traced here: 161 us
  waiting for transfers between devices  70.6 us (44%)
  starting transfers between devices  56 us (35%)
  matrix products  18.9 us (12%)
  other arithmetic  10.3 us (6%)
  local copies, waits for them, and re-layouts  3.89 us (2%)
    all_to_all x4, waiting for transfers between devices, body(): lax.all_to_all(outgoing.reshape(groups, cap, width), 'grp', split_axis=0,...  51.5 us
    all_to_all x4, starting transfers between devices, body(): lax.all_to_all(outgoing.reshape(groups, cap, width), 'grp', split_axis=0,...  33 us
    all_to_all x4, starting transfers between devices, body(): lax.all_to_all(group_part.reshape(owners, tiles, width), 'own', split_axi...  23.1 us
    all_to_all x4, waiting for transfers between devices, body(): lax.all_to_all(group_part.reshape(owners, tiles, width), 'own', split_axi...  19 us
    dot_general x4, matrix products, body(): jnp.einsum('tab,tb->ta', self_inverse, right_side, preferred_element_type...  9 us
    dot_general x4, matrix products, body(): jnp.dot(reader_hits, far_terms.reshape(classes * slots, width), preferred...  6.89 us
    broadcast_in_dim x3, other arithmetic, body(): retarded.astype(BF16)[None]  3.77 us
  transfers between devices with their start and end apart: 8, of which 8 were waited for; matrix products, arithmetic and copies ran while one was open for 3% of the time, Pallas kernels for 0%

profile of v1, /device:TPU:1, one launch (start us, length us, event | category | flops | bytes accessed | tf_op | source)
XLA Modules:
  0.0 160.7 jit_solution(8632475689925775157)
XLA Ops:
  0.7 0.9 fusion.53
  2.5 1.0 convolution_bitcast_fusion.3
  4.2 19.1 %all-to-all-start = ((bf16[64,2,256]{2,1,0:T(2,128)(2,1)}), bf16[64,2,256]{2,1,0:T(2,128)(2,1)S(1)}, u32[]{:S(2)}, u32[]{:S(2)}) async-start(bf16[64,2,256]{2,1,0:T(2,128)(2,1)} %copy.36), calls=%async_computation | async-start | bytes 131072 | tf_op jit(solution)/shard_map/all_to_all | solution.py:78
  23.3 1.4 fusion.85
  24.7 1.1 multiply_reduce_fusion
  25.8 0.8 copy.34
  27.4 10.0 %all-to-all-done = bf16[64,2,256]{2,1,0:T(2,128)(2,1)S(1)} async-done(((bf16[64,2,256]{2,1,0:T(2,128)(2,1)}), bf16[64,2,256]{2,1,0:T(2,128)(2,1)S(1)}, u32[]{:S(2)}, u32[]{:S(2)}) %all-to-all-start) | async-done | bytes 65568 | tf_op jit(solution)/shard_map/all_to_all | solution.py:78
  37.4 1.7 %fusion.15 = bf16[128,256]{1,0:T(8,128)(2,1)} fusion(bf16[128,256,1]{1,0,2:T(8,128)(2,1)S(1)} %reshape.150, bf16[16,256,256]{2,1,0:T(8,128)(2,1)S(1)} %copy-done, s32[16,128]{1,0:T(8,128)S(1)} %copy.35), kind=kOutput, calls=%fused_computation.19 | convolution fusion | flops 403472384 | bytes 2236416 | tf_op jit(solution)/shard_map/dot_general | solution.py:90
  39.1 6.6 %all-to-all-start.1 = ((bf16[8,16,256]{2,1,0:T(8,128)(2,1)}), bf16[8,16,256]{2,1,0:T(8,128)(2,1)S(1)}, u32[]{:S(2)}, u32[]{:S(2)}) async-start(bf16[8,16,256]{2,1,0:T(8,128)(2,1)} %bitcast.16), calls=%async_computation.1 | async-start | bytes 131072 | tf_op jit(solution)/shard_map/all_to_all | solution.py:93
  45.9 4.6 %all-to-all-done.1 = bf16[8,16,256]{2,1,0:T(8,128)(2,1)S(1)} async-done(((bf16[8,16,256]{2,1,0:T(8,128)(2,1)}), bf16[8,16,256]{2,1,0:T(8,128)(2,1)S(1)}, u32[]{:S(2)}, u32[]{:S(2)}) %all-to-all-start.1) | async-done | bytes 65568 | tf_op jit(solution)/shard_map/all_to_all | solution.py:93
  50.8 2.2 %fusion.72 = bf16[16,1,256]{2,1,0:T(2,128)(2,1)S(1)} fusion(bf16[16,256,256]{2,1,0:T(8,128)(2,1)} %param.18, bf16[16,256,1]{1,0,2:T(8,128)(2,1)S(1)} %fusion.35), kind=kOutput, calls=%fused_computation.117 | convolution fusion | flops 2097152 | bytes 2113536 | tf_op jit(solution)/shard_map/tab,tb->ta/dot_general | solution.py:98
  54.5 4.6 %all-to-all-start.2 = ((bf16[64,2,256]{2,1,0:T(2,128)(2,1)}), bf16[64,2,256]{2,1,0:T(2,128)(2,1)S(1)}, u32[]{:S(2)}, u32[]{:S(2)}) async-start(bf16[64,2,256]{2,1,0:T(2,128)(2,1)} %copy.37), calls=%async_computation.2 | async-start | bytes 131072 | tf_op jit(solution)/shard_map/all_to_all | solution.py:78
  59.4 13.8 %all-to-all-done.2 = bf16[64,2,256]{2,1,0:T(2,128)(2,1)S(1)} async-done(((bf16[64,2,256]{2,1,0:T(2,128)(2,1)}), bf16[64,2,256]{2,1,0:T(2,128)(2,1)S(1)}, u32[]{:S(2)}, u32[]{:S(2)}) %all-to-all-start.2) | async-done | bytes 65568 | tf_op jit(solution)/shard_map/all_to_all | solution.py:78
  73.2 1.7 %fusion.14 = bf16[128,256]{1,0:T(8,128)(2,1)} fusion(bf16[128,256,1]{1,0,2:T(8,128)(2,1)S(1)} %reshape.158, bf16[16,256,256]{2,1,0:T(8,128)(2,1)S(1)} %copy-done, s32[16,128]{1,0:T(8,128)S(1)} %copy.35), kind=kOutput, calls=%fused_computation.18 | convolution fusion | flops 403472384 | bytes 2236416 | tf_op jit(solution)/shard_map/dot_general | solution.py:90
  74.9 5.5 %all-to-all-start.3 = ((bf16[8,16,256]{2,1,0:T(8,128)(2,1)}), bf16[8,16,256]{2,1,0:T(8,128)(2,1)S(1)}, u32[]{:S(2)}, u32[]{:S(2)}) async-start(bf16[8,16,256]{2,1,0:T(8,128)(2,1)} %bitcast.31), calls=%async_computation.3 | async-start | bytes 131072 | tf_op jit(solution)/shard_map/all_to_all | solution.py:93
  80.4 4.9 %all-to-all-done.3 = bf16[8,16,256]{2,1,0:T(8,128)(2,1)S(1)} async-done(((bf16[8,16,256]{2,1,0:T(8,128)(2,1)}), bf16[8,16,256]{2,1,0:T(8,128)(2,1)S(1)}, u32[]{:S(2)}, u32[]{:S(2)}) %all-to-all-start.3) | async-done | bytes 65568 | tf_op jit(solution)/shard_map/all_to_all | solution.py:93
  85.5 2.2 %fusion.70 = bf16[16,1,256]{2,1,0:T(2,128)(2,1)S(1)} fusion(bf16[16,256,256]{2,1,0:T(8,128)(2,1)} %param.18, bf16[16,256,1]{1,0,2:T(8,128)(2,1)S(1)} %fusion.34), kind=kOutput, calls=%fused_computation.115 | convolution fusion | flops 2097152 | bytes 2113536 | tf_op jit(solution)/shard_map/tab,tb->ta/dot_general | solution.py:98
  87.7 1.3 fusion.80
  89.9 4.6 %all-to-all-start.4 = ((bf16[64,2,256]{2,1,0:T(2,128)(2,1)}), bf16[64,2,256]{2,1,0:T(2,128)(2,1)S(1)}, u32[]{:S(2)}, u32[]{:S(2)}) async-start(bf16[64,2,256]{2,1,0:T(2,128)(2,1)} %copy.38), calls=%async_computation.4 | async-start | bytes 131072 | tf_op jit(solution)/shard_map/all_to_all | solution.py:78
  94.8 13.8 %all-to-all-done.4 = bf16[64,2,256]{2,1,0:T(2,128)(2,1)S(1)} async-done(((bf16[64,2,256]{2,1,0:T(2,128)(2,1)}), bf16[64,2,256]{2,1,0:T(2,128)(2,1)S(1)}, u32[]{:S(2)}, u32[]{:S(2)}) %all-to-all-start.4) | async-done | bytes 65568 | tf_op jit(solution)/shard_map/all_to_all | solution.py:78
  108.6 1.7 %fusion.13 = bf16[128,256]{1,0:T(8,128)(2,1)} fusion(bf16[128,256,1]{1,0,2:T(8,128)(2,1)S(1)} %reshape.166, bf16[16,256,256]{2,1,0:T(8,128)(2,1)S(1)} %copy-done, s32[16,128]{1,0:T(8,128)S(1)} %copy.35), kind=kOutput, calls=%fused_computation.17 | convolution fusion | flops 403472384 | bytes 2236416 | tf_op jit(solution)/shard_map/dot_general | solution.py:90
  110.3 5.5 %all-to-all-start.5 = ((bf16[8,16,256]{2,1,0:T(8,128)(2,1)}), bf16[8,16,256]{2,1,0:T(8,128)(2,1)S(1)}, u32[]{:S(2)}, u32[]{:S(2)}) async-start(bf16[8,16,256]{2,1,0:T(8,128)(2,1)} %bitcast.46), calls=%async_computation.5 | async-start | bytes 131072 | tf_op jit(solution)/shard_map/all_to_all | solution.py:93
  115.8 4.9 %all-to-all-done.5 = bf16[8,16,256]{2,1,0:T(8,128)(2,1)S(1)} async-done(((bf16[8,16,256]{2,1,0:T(8,128)(2,1)}), bf16[8,16,256]{2,1,0:T(8,128)(2,1)S(1)}, u32[]{:S(2)}, u32[]{:S(2)}) %all-to-all-start.5) | async-done | bytes 65568 | tf_op jit(solution)/shard_map/all_to_all | solution.py:93
  120.9 2.2 %fusion.68 = bf16[16,1,256]{2,1,0:T(2,128)(2,1)S(1)} fusion(bf16[16,256,256]{2,1,0:T(8,128)(2,1)} %param.18, bf16[16,256,1]{1,0,2:T(8,128)(2,1)S(1)} %fusion.33), kind=kOutput, calls=%fused_computation.113 | convolution fusion | flops 2097152 | bytes 2113536 | tf_op jit(solution)/shard_map/tab,tb->ta/dot_general | solution.py:98
  123.1 1.9 %fusion.81 = bf16[1,16,256]{2,1,0:T(8,128)(2,1)S(1)} fusion(bf16[16,256]{1,0:T(8,128)(2,1)S(1)} %bitcast.216, f32[16,256]{1,0:T(8,128)S(1)} %get-tuple-element.2, f32[]{:T(128)} %get-tuple-element.15, f32[]{:T(128)} %get-tuple-element.18, bf16[16,256]{1,0:T(8,128)(2,1)S(1)} %bitcast.221, f32[]{:T(128)} %get-tuple-element.20, bf16[16,256]{1,0:T(8,128)(2,1)S(1)} %bitcast.226), kind=kLoop, calls=%fused_computation.131 | loop fusion | flops 45056 | bytes 49164 | tf_op jit(solution)/shard_map/broadcast_in_dim | solution.py:109
  126.0 4.6 %all-to-all-start.6 = ((bf16[64,2,256]{2,1,0:T(2,128)(2,1)}), bf16[64,2,256]{2,1,0:T(2,128)(2,1)S(1)}, u32[]{:S(2)}, u32[]{:S(2)}) async-start(bf16[64,2,256]{2,1,0:T(2,128)(2,1)} %copy.39), calls=%async_computation.6 | async-start | bytes 131072 | tf_op jit(solution)/shard_map/all_to_all | solution.py:78
  130.6 14.0 %all-to-all-done.6 = bf16[64,2,256]{2,1,0:T(2,128)(2,1)S(1)} async-done(((bf16[64,2,256]{2,1,0:T(2,128)(2,1)}), bf16[64,2,256]{2,1,0:T(2,128)(2,1)S(1)}, u32[]{:S(2)}, u32[]{:S(2)}) %all-to-all-start.6) | async-done | bytes 65568 | tf_op jit(solution)/shard_map/all_to_all | solution.py:78
  144.7 1.7 %fusion.12 = bf16[128,256]{1,0:T(8,128)(2,1)} fusion(bf16[128,256,1]{1,0,2:T(8,128)(2,1)S(1)} %reshape.174, bf16[16,256,256]{2,1,0:T(8,128)(2,1)S(1)} %copy-done, s32[16,128]{1,0:T(8,128)S(1)} %copy.35), kind=kOutput, calls=%fused_computation.16 | convolution fusion | flops 403472384 | bytes 2236416 | tf_op jit(solution)/shard_map/dot_general | solution.py:90
  146.4 5.5 %all-to-all-start.7 = ((bf16[8,16,256]{2,1,0:T(8,128)(2,1)}), bf16[8,16,256]{2,1,0:T(8,128)(2,1)S(1)}, u32[]{:S(2)}, u32[]{:S(2)}) async-start(bf16[8,16,256]{2,1,0:T(8,128)(2,1)} %bitcast.61), calls=%async_computation.7 | async-start | bytes 131072 | tf_op jit(solution)/shard_map/all_to_all | solution.py:93
  152.1 4.7 %all-to-all-done.7 = bf16[8,16,256]{2,1,0:T(8,128)(2,1)S(1)} async-done(((bf16[8,16,256]{2,1,0:T(8,128)(2,1)}), bf16[8,16,256]{2,1,0:T(8,128)(2,1)S(1)}, u32[]{:S(2)}, u32[]{:S(2)}) %all-to-all-start.7) | async-done | bytes 65568 | tf_op jit(solution)/shard_map/all_to_all | solution.py:93
  156.9 2.2 %fusion.66 = bf16[16,1,256]{2,1,0:T(2,128)(2,1)S(1)} fusion(bf16[16,256,256]{2,1,0:T(8,128)(2,1)} %param.18, bf16[16,256,1]{1,0,2:T(8,128)(2,1)S(1)} %fusion.32), kind=kOutput, calls=%fused_computation.111 | convolution fusion | flops 2097152 | bytes 2113536 | tf_op jit(solution)/shard_map/tab,tb->ta/dot_general | solution.py:98
  159.8 0.8 add_add_fusion
  (65 shorter events, 8.1 us)
Async XLA Ops:
  0.6 36.8 %copy-start = (bf16[16,256,256]{2,1,0:T(8,128)(2,1)S(1)}, bf16[16,256,256]{2,1,0:T(8,128)(2,1)}, u32[]{:S(2)}) copy-start(bf16[16,256,256]{2,1,0:T(8,128)(2,1)} %param.20) | copy-start | bytes 6291460
  0.6 45.3 %copy-start.3 = (bf16[4,16,256]{2,1,0:T(8,128)(2,1)S(1)}, bf16[4,16,256]{2,1,0:T(8,128)(2,1)}, u32[]{:S(2)}) copy-start(bf16[4,16,256]{2,1,0:T(8,128)(2,1)} %param.16) | copy-start | bytes 98308
  0.7 45.1 %copy-start.5 = (bf16[4,16,256]{2,1,0:T(8,128)(2,1)S(1)}, bf16[4,16,256]{2,1,0:T(8,128)(2,1)}, u32[]{:S(2)}) copy-start(bf16[4,16,256]{2,1,0:T(8,128)(2,1)} %param.15) | copy-start | bytes 98308
  0.7 49.9 %copy-start.1 = (bf16[2,256,256]{2,1,0:T(8,128)(2,1)S(1)}, bf16[2,256,256]{2,1,0:T(8,128)(2,1)}, u32[]{:S(2)}) copy-start(bf16[2,256,256]{2,1,0:T(8,128)(2,1)} %param.19) | copy-start | bytes 786436
  0.7 49.9 %copy-start.4 = (bf16[4,16,256]{2,1,0:T(8,128)(2,1)S(1)}, bf16[4,16,256]{2,1,0:T(8,128)(2,1)}, u32[]{:S(2)}) copy-start(bf16[4,16,256]{2,1,0:T(8,128)(2,1)} %param.14) | copy-start | bytes 98308
  4.2 33.1 %all-to-all-start = ((bf16[64,2,256]{2,1,0:T(2,128)(2,1)}), bf16[64,2,256]{2,1,0:T(2,128)(2,1)S(1)}, u32[]{:S(2)}, u32[]{:S(2)}) async-start(bf16[64,2,256]{2,1,0:T(2,128)(2,1)} %copy.36), calls=%async_computation | async-start | bytes 131072 | tf_op jit(solution)/shard_map/all_to_all | solution.py:78
  39.1 11.5 %all-to-all-start.1 = ((bf16[8,16,256]{2,1,0:T(8,128)(2,1)}), bf16[8,16,256]{2,1,0:T(8,128)(2,1)S(1)}, u32[]{:S(2)}, u32[]{:S(2)}) async-start(bf16[8,16,256]{2,1,0:T(8,128)(2,1)} %bitcast.16), calls=%async_computation.1 | async-start | bytes 131072 | tf_op jit(solution)/shard_map/all_to_all | solution.py:93
  54.5 18.6 %all-to-all-start.2 = ((bf16[64,2,256]{2,1,0:T(2,128)(2,1)}), bf16[64,2,256]{2,1,0:T(2,128)(2,1)S(1)}, u32[]{:S(2)}, u32[]{:S(2)}) async-start(bf16[64,2,256]{2,1,0:T(2,128)(2,1)} %copy.37), calls=%async_computation.2 | async-start | bytes 131072 | tf_op jit(solution)/shard_map/all_to_all | solution.py:78
  74.9 10.4 %all-to-all-start.3 = ((bf16[8,16,256]{2,1,0:T(8,128)(2,1)}), bf16[8,16,256]{2,1,0:T(8,128)(2,1)S(1)}, u32[]{:S(2)}, u32[]{:S(2)}) async-start(bf16[8,16,256]{2,1,0:T(8,128)(2,1)} %bitcast.31), calls=%async_computation.3 | async-start | bytes 131072 | tf_op jit(solution)/shard_map/all_to_all | solution.py:93
  89.9 18.6 %all-to-all-start.4 = ((bf16[64,2,256]{2,1,0:T(2,128)(2,1)}), bf16[64,2,256]{2,1,0:T(2,128)(2,1)S(1)}, u32[]{:S(2)}, u32[]{:S(2)}) async-start(bf16[64,2,256]{2,1,0:T(2,128)(2,1)} %copy.38), calls=%async_computation.4 | async-start | bytes 131072 | tf_op jit(solution)/shard_map/all_to_all | solution.py:78
  110.3 10.4 %all-to-all-start.5 = ((bf16[8,16,256]{2,1,0:T(8,128)(2,1)}), bf16[8,16,256]{2,1,0:T(8,128)(2,1)S(1)}, u32[]{:S(2)}, u32[]{:S(2)}) async-start(bf16[8,16,256]{2,1,0:T(8,128)(2,1)} %bitcast.46), calls=%async_computation.5 | async-start | bytes 131072 | tf_op jit(solution)/shard_map/all_to_all | solution.py:93
  126.0 18.6 %all-to-all-start.6 = ((bf16[64,2,256]{2,1,0:T(2,128)(2,1)}), bf16[64,2,256]{2,1,0:T(2,128)(2,1)S(1)}, u32[]{:S(2)}, u32[]{:S(2)}) async-start(bf16[64,2,256]{2,1,0:T(2,128)(2,1)} %copy.39), calls=%async_computation.6 | async-start | bytes 131072 | tf_op jit(solution)/shard_map/all_to_all | solution.py:78
  144.6 15.2 %copy-start.2 = (f32[16,16,256]{2,1,0:T(8,128)S(1)}, f32[16,16,256]{2,1,0:T(8,128)}, u32[]{:S(2)}) copy-start(f32[16,16,256]{2,1,0:T(8,128)} %param.17) | copy-start | bytes 786436
  144.7 15.2 %copy-start.6 = (f32[16]{0:T(128)S(1)}, f32[16]{0:T(128)}, u32[]{:S(2)}) copy-start(f32[16]{0:T(128)} %param.21) | copy-start | bytes 196
  146.4 10.4 %all-to-all-start.7 = ((bf16[8,16,256]{2,1,0:T(8,128)(2,1)}), bf16[8,16,256]{2,1,0:T(8,128)(2,1)S(1)}, u32[]{:S(2)}, u32[]{:S(2)}) async-start(bf16[8,16,256]{2,1,0:T(8,128)(2,1)} %bitcast.61), calls=%async_computation.7 | async-start | bytes 131072 | tf_op jit(solution)/shard_map/all_to_all | solution.py:93

commit v2 on v1

v2 whole, which is shorter than its diff:
```python
import functools

import jax
import jax.numpy as jnp
from jax import lax
from jax.experimental import pallas as pl
from jax.experimental.pallas import tpu as pltpu
from jax.sharding import PartitionSpec as P

STEPS = 4
HIST = 4
F32 = jnp.float32
BF16 = jnp.bfloat16
I32 = jnp.int32
LANES = 128
CONTRACT_LAST = (((1,), (1,)), ((), ()))
VMEM = pl.BlockSpec(memory_space=pltpu.VMEM)
SMEM = pl.BlockSpec(memory_space=pltpu.SMEM)


def halves_stacked(rows):
    return jnp.concatenate([rows[:, :LANES], rows[:, LANES:]], axis=0)


def first_kernel(dest_ref, delay_ref, ret_ref, pick_ref, out_ref):
    hist, tiles, width = ret_ref.shape
    rows = pick_ref.shape[0]
    cols = pick_ref.shape[1]
    repeat = cols // tiles
    dest = jnp.concatenate([dest_ref[...]] * repeat, axis=0)
    delay = jnp.concatenate([delay_ref[...]] * repeat, axis=0)
    shape = (cols, rows)
    at = lax.broadcasted_iota(I32, shape, 1)
    group = at // 4
    col = lax.broadcasted_iota(I32, (cols, 1), 0)
    col_delay = (col // tiles) % hist + 1
    col_half = col // (tiles * hist)
    named = jnp.zeros(shape, F32)
    timed = jnp.zeros(shape, F32)
    for j in range(dest.shape[1]):
        hit = dest[:, j : j + 1] == group
        named = jnp.where(hit, 1.0, named)
        timed = jnp.where(hit & (delay[:, j : j + 1] == col_delay), 1.0, timed)
    to = lax.broadcasted_iota(I32, (cols, cols), 0)
    of = lax.broadcasted_iota(I32, (cols, cols), 1)
    earlier = jnp.where((to // tiles == of // tiles) & (of < to), 1.0, 0.0).astype(BF16)
    before = lax.dot(earlier, named.astype(BF16), preferred_element_type=F32)
    keep = (before == (at % 2).astype(F32)) & (col_half == (at // 2) % 2)
    pick = jnp.where(keep, timed, 0.0).T.astype(BF16)
    pick_ref[...] = pick
    stacked = halves_stacked(ret_ref[...].reshape(hist * tiles, width))
    out_ref[...] = lax.dot(pick, stacked, preferred_element_type=F32).astype(BF16)


def far_kernel(
    in_ref, split_ref, far_ref, hits_ref, near_pick_ref, cur_ref, near_ref, exc_ref,
    part_ref, base_ref, terms_ref,
):
    slots = split_ref.shape[1]
    incoming = in_ref[...]
    entries = jnp.concatenate(
        [
            lax.dot(split_ref[h], incoming, preferred_element_type=F32).astype(BF16)
            for h in range(2)
        ],
        axis=1,
    )
    for k in range(far_ref.shape[0]):
        terms = lax.dot_general(entries, far_ref[k], CONTRACT_LAST, preferred_element_type=F32)
        terms_ref[pl.ds(k * slots, slots), :] = terms.astype(BF16)
    near_rows = lax.dot(near_pick_ref[...], cur_ref[...], preferred_element_type=F32).astype(BF16)
    classes = near_ref.shape[0]
    tiles = exc_ref.shape[0]
    per_class = near_rows.shape[0] // classes
    base = exc_ref[...].astype(F32)
    for k in range(classes):
        near = lax.dot_general(
            near_rows[k * per_class : (k + 1) * per_class],
            near_ref[k],
            CONTRACT_LAST,
            preferred_element_type=F32,
        )
        for m in range(per_class // tiles):
            base = base - near[m * tiles : (m + 1) * tiles]
    base_ref[...] = base
    part_ref[...] = lax.dot(
        hits_ref[...], terms_ref[...], preferred_element_type=F32
    ).astype(BF16)


def solve(parts_ref, base_ref, inverse_ref):
    far_field = parts_ref[0].astype(F32)
    for o in range(1, parts_ref.shape[0]):
        far_field = far_field + parts_ref[o].astype(F32)
    right_side = (base_ref[...] - far_field).astype(BF16)
    tiles = right_side.shape[0]
    row = lax.broadcasted_iota(I32, right_side.shape, 0)
    current = jnp.zeros(right_side.shape, F32)
    for t in range(tiles):
        current = jnp.where(
            row == t, lax.dot(right_side, inverse_ref[t], preferred_element_type=F32), current
        )
    return current.astype(BF16)


def step_kernel(
    step, weight_ref, parts_ref, base_ref, inverse_ref, tail_ref, cur_ref, ret_ref, pick_ref,
    cur_out, ret_out, send_ref,
):
    current = solve(parts_ref, base_ref, inverse_ref)
    tiles = current.shape[0]
    wide = current.astype(F32)
    retarded = wide * (1.0 + weight_ref[0]) + tail_ref[step]
    for back in range(1, step + 1):
        past = cur_ref[pl.ds((back - 1) * tiles, tiles), :]
        retarded = retarded + weight_ref[back] * past.astype(F32)
    kept = cur_ref.shape[0] - tiles
    cur_out[...] = jnp.concatenate([current, cur_ref[:kept, :]], axis=0)
    history = jnp.concatenate([retarded.astype(BF16), ret_ref[:kept, :]], axis=0)
    ret_out[...] = history
    send_ref[...] = lax.dot(
        pick_ref[...], halves_stacked(history), preferred_element_type=F32
    ).astype(BF16)


def last_kernel(pole_ref, parts_ref, base_ref, inverse_ref, cur_ref, state_ref, cur_out, state_out):
    current = solve(parts_ref, base_ref, inverse_ref)
    tiles = current.shape[0]
    past = [cur_ref[pl.ds((STEPS - 2 - n) * tiles, tiles), :] for n in range(STEPS - 1)] + [current]
    for n in range(STEPS):
        cur_out[n] = past[n]
    wide = [c.astype(F32) for c in past]
    for p in range(state_ref.shape[0]):
        pole = pole_ref[p]
        state = state_ref[p]
        for n in range(STEPS):
            state = pole * state + wide[n]
        state_out[p] = state


def call(kernel, name, outs, specs, scratch=()):
    return pl.pallas_call(
        kernel,
        name=name,
        out_shape=outs,
        in_specs=specs,
        out_specs=jax.tree.map(lambda _: VMEM, outs),
        scratch_shapes=scratch,
        compiler_params=pltpu.CompilerParams(vmem_limit_bytes=8 << 20),
    )


def body(
    excitation,
    cur_hist,
    ret_hist,
    pole_state,
    self_inverse,
    near_mats,
    far_mats,
    poles,
    residues,
    near_src,
    near_delay,
    far_dest,
    far_delay,
    far_reader,
):
    groups = far_reader.shape[1]
    cap = far_reader.shape[3]
    classes = far_reader.shape[4]
    tiles = excitation.shape[1]
    width = excitation.shape[2]
    owners = lax.axis_size("own")
    group_tiles = tiles * owners
    slots = groups * cap
    past = HIST * tiles
    shape = jax.ShapeDtypeStruct

    pick, outgoing = call(
        first_kernel,
        "first",
        (shape((2 * slots, 2 * past), BF16), shape((2 * slots, LANES), BF16)),
        [VMEM] * 3,
    )(far_dest, far_delay, ret_hist)

    readers = far_reader.reshape(slots, classes)
    reader_hits = (
        readers.T[None, :, :] == jnp.arange(group_tiles, dtype=I32)[:, None, None]
    ).astype(BF16)
    reader_hits = reader_hits.reshape(group_tiles, classes * slots)
    slot = lax.broadcasted_iota(I32, (2, slots, 2 * slots), 1)
    half = lax.broadcasted_iota(I32, (2, slots, 2 * slots), 0)
    row = lax.broadcasted_iota(I32, (2, slots, 2 * slots), 2)
    split = (row == 4 * (slot // 2) + 2 * half + slot % 2).astype(BF16)
    near_row = ((near_delay - 1) * tiles + near_src).transpose(0, 2, 1).reshape(-1)
    near_pick = (near_row[:, None] == jnp.arange(past, dtype=I32)).astype(BF16)
    scale = [residues]
    for _ in range(STEPS - 1):
        scale.append(scale[-1] * poles)
    scale = jnp.stack(scale)
    weight = jnp.sum(scale, axis=1)
    tail = jnp.sum(scale[1:, :, None, None] * pole_state[None], axis=1)
    inverse = self_inverse.swapaxes(1, 2)

    current = cur_hist.reshape(past, width)
    retarded = ret_hist.reshape(past, width)
    for step in range(STEPS):
        incoming = lax.all_to_all(
            outgoing.reshape(groups, 2 * cap, LANES), "grp", split_axis=0, concat_axis=0, tiled=True
        ).reshape(2 * slots, LANES)
        if step == 0:
            incoming, inverse, tail, weight, reader_hits, near_pick, split = (
                lax.optimization_barrier(
                    (incoming, inverse, tail, weight, reader_hits, near_pick, split)
                )
            )
        part, base = call(
            far_kernel,
            "far",
            (shape((group_tiles, width), BF16), shape((tiles, width), F32)),
            [VMEM] * 8,
            [pltpu.VMEM((classes * slots, width), BF16)],
        )(
            incoming, split, far_mats, reader_hits, near_pick, current, near_mats, excitation[step]
        )
        parts = lax.all_to_all(
            part.reshape(owners, tiles, width), "own", split_axis=0, concat_axis=0, tiled=True
        )
        if step + 1 < STEPS:
            current, retarded, outgoing = call(
                functools.partial(step_kernel, step),
                "step",
                (
                    shape((past, width), BF16),
                    shape((past, width), BF16),
                    shape((2 * slots, LANES), BF16),
                ),
                [SMEM] + [VMEM] * 7,
            )(weight, parts, base, inverse, tail, current, retarded, pick)
    return call(
        last_kernel,
        "last",
        (shape((STEPS, tiles, width), BF16), shape(pole_state.shape, F32)),
        [SMEM] + [VMEM] * 5,
    )(poles, parts, base, inverse, current, pole_state)


def solution(mesh):
    in_specs = (
        P(None, ("grp", "own"), None),
        P(None, ("grp", "own"), None),
        P(None, ("grp", "own"), None),
        P(None, ("grp", "own"), None),
        P(("grp", "own"), None, None),
        P(),
        P(),
        P(),
        P(),
        P(None, ("grp", "own"), None),
        P(None, ("grp", "own"), None),
        P(("grp", "own"), None),
        P(("grp", "own"), None),
        P("grp", None, "own", None, None),
    )
    out_specs = (P(None, ("grp", "own"), None), P(None, ("grp", "own"), None))
    return jax.shard_map(body, mesh=mesh, in_specs=in_specs, out_specs=out_specs, check_vma=False)
```

time: 162 us -> 147 us (0.907)
  blocking collectives: 0 us -> 96.6 us
  waiting for transfers between devices: 70.6 us -> 6.31 us
  starting transfers between devices: 56 us -> 19.1 us
  matrix products: 18.9 us -> 0 us
  Pallas kernels: 0 us -> 12.2 us
  other arithmetic: 10.3 us -> 2.99 us
  local copies, waits for them, and re-layouts: 3.89 us -> 8.5 us
    all_to_all x0 -> x7, blocking collectives: none -> 96.6 us  [the longest x3 56.9 us: body(): lax.all_to_all(outgoing.reshape(groups, 2 * cap, LANES), 'grp', split_axi...]
    all_to_all x8 -> x1, waiting for transfers between devices: 70.6 us -> 6.31 us  [body(): lax.all_to_all(outgoing.reshape(groups, 2 * cap, LANES), 'grp', split_axi...]
    all_to_all x8 -> x1, starting transfers between devices: 56 us -> 19.1 us  [body(): lax.all_to_all(outgoing.reshape(groups, 2 * cap, LANES), 'grp', split_axi...]
    dot_general x20 -> x0, matrix products: 18.9 us -> none  [the longest x4 9 us: body(): jnp.einsum('tab,tb->ta', self_inverse, right_side, preferred_element_type...]
    pallas_call x0 -> x9, Pallas kernels: none -> 12.2 us  [the longest x4 5.74 us: body(): call(far_kernel, 'far', (shape((group_tiles, width), BF16), shape((tiles,...]
    unnamed x15 -> x22, local copies, waits for them, and re-layouts: 0.85 us -> 7.61 us
    broadcast_in_dim x3 -> x0, other arithmetic: 3.77 us -> none  [body(): retarded.astype(BF16)[None]]
    dot_general x8 -> x0, local copies, waits for them, and re-layouts: 2.85 us -> none  [the longest x4 2.82 us: body(): outgoing = jnp.dot(send_pick, history_ret.reshape(HIST * tiles, width))]
  transfers between devices with their start and end apart: 8 -> 1, of which waited for: 8 -> 1; matrix products, arithmetic and copies ran while one was open for 3% -> 5% of each run, Pallas kernels for 0% -> 0%
where the time goes in v2:
time: 147 us
  blocking collectives  96.6 us (66%)
  starting transfers between devices  19.1 us (13%)
  Pallas kernels  12.2 us (8%)
  local copies, waits for them, and re-layouts  8.5 us (6%)
  waiting for transfers between devices  6.31 us (4%)
  other arithmetic  2.99 us (2%)
    all_to_all x3, blocking collectives, body(): lax.all_to_all(outgoing.reshape(groups, 2 * cap, LANES), 'grp', split_axi...  56.9 us
    all_to_all x4, blocking collectives, body(): lax.all_to_all(part.reshape(owners, tiles, width), 'own', split_axis=0, c...  39.7 us
    all_to_all x1, starting transfers between devices, body(): lax.all_to_all(outgoing.reshape(groups, 2 * cap, LANES), 'grp', split_axi...  19.1 us
    unnamed x22, local copies, waits for them, and re-layouts  7.61 us
    all_to_all x1, waiting for transfers between devices, body(): lax.all_to_all(outgoing.reshape(groups, 2 * cap, LANES), 'grp', split_axi...  6.31 us
    pallas_call x4, Pallas kernels, body(): call(far_kernel, 'far', (shape((group_tiles, width), BF16), shape((tiles,...  5.74 us
    pallas_call x3, Pallas kernels, body(): call(functools.partial(step_kernel, step), 'step', (shape((past, width),...  3.71 us
  transfers between devices with their start and end apart: 1, of which 1 were waited for; matrix products, arithmetic and copies ran while one was open for 5% of the time, Pallas kernels for 0%

profile of v2, /device:TPU:1, one launch (start us, length us, event | category | flops | bytes accessed | tf_op | source)
XLA Modules:
  0.0 146.5 jit_solution(10513011421408318375)
XLA Ops:
  0.6 0.8 copy.24.dest_ref
  1.4 0.8 copy.25.delay_ref
  2.1 0.8 copy-done.5
  2.9 1.1 first.1
  4.0 19.1 %all-to-all-start = ((bf16[64,4,128]{2,1,0:T(4,128)(2,1)}), bf16[64,4,128]{2,1,0:T(4,128)(2,1)S(1)}, u32[]{:S(2)}, u32[]{:S(2)}) async-start(bf16[64,4,128]{2,1,0:T(4,128)(2,1)} %bitcast), calls=%async_computation | async-start | bytes 131072 | tf_op jit(solution)/shard_map/all_to_all | solution.py:209
  23.1 0.7 add_bitcast_fusion
  23.8 0.1 eq.40
  24.0 0.8 slice_bitcast_fusion
  24.8 0.8 copy.27
  25.6 0.1 fusion.hits_ref
  25.8 0.7 multiply_bitcast_fusion.2
  26.4 1.1 multiply_reduce_fusion.tail_ref
  27.6 2.9 %copy.26 = bf16[16,256,256]{1,2,0:T(8,128)(2,1)S(1)} copy(bf16[16,256,256]{2,1,0:T(8,128)(2,1)} %param.18) | data formatting | bytes 4194304 | tf_op args[4]
  30.5 0.1 maximum_reduce_fusion.weight_ref
  30.6 0.2 fusion.1.split_ref
  30.8 6.3 %all-to-all-done = bf16[64,4,128]{2,1,0:T(4,128)(2,1)S(1)} async-done(((bf16[64,4,128]{2,1,0:T(4,128)(2,1)}), bf16[64,4,128]{2,1,0:T(4,128)(2,1)S(1)}, u32[]{:S(2)}, u32[]{:S(2)}) %all-to-all-start) | async-done | bytes 65568 | tf_op jit(solution)/shard_map/all_to_all | solution.py:209
  37.1 1.6 %copy-done = bf16[16,256,256]{2,1,0:T(8,128)(2,1)S(1)} copy-done((bf16[16,256,256]{2,1,0:T(8,128)(2,1)S(1)}, bf16[16,256,256]{2,1,0:T(8,128)(2,1)}, u32[]{:S(2)}) %copy-start) | copy-done | bytes 2097176
  38.7 1.4 far.4
  40.2 11.4 %all_to_all.40.parts_ref = bf16[8,16,256]{2,1,0:T(8,128)(2,1)S(1)} all-to-all(bf16[8,16,256]{2,1,0:T(8,128)(2,1)S(1)} %bitcast.51), channel_id=1, replica_groups=mesh['grp'=64,'own'=8] {'own'}, dimensions={0} | all-to-all | bytes 131072 | tf_op jit(solution)/shard_map/all_to_all | solution.py:227
  51.5 1.1 step.3
  52.6 21.2 %all_to_all.41 = bf16[64,4,128]{2,1,0:T(4,128)(2,1)S(1)} all-to-all(bf16[64,4,128]{2,1,0:T(4,128)(2,1)S(1)} %bitcast.50), channel_id=1, replica_groups=mesh['grp'=64,'own'=8] {'grp'}, dimensions={0} | all-to-all | bytes 131072 | tf_op jit(solution)/shard_map/all_to_all | solution.py:209
  73.8 1.4 far.5
  75.3 9.4 %all_to_all.42.parts_ref = bf16[8,16,256]{2,1,0:T(8,128)(2,1)S(1)} all-to-all(bf16[8,16,256]{2,1,0:T(8,128)(2,1)S(1)} %bitcast.52), channel_id=1, replica_groups=mesh['grp'=64,'own'=8] {'own'}, dimensions={0} | all-to-all | bytes 131072 | tf_op jit(solution)/shard_map/all_to_all | solution.py:227
  84.7 1.1 step.4
  85.8 17.8 %all_to_all.43 = bf16[64,4,128]{2,1,0:T(4,128)(2,1)S(1)} all-to-all(bf16[64,4,128]{2,1,0:T(4,128)(2,1)S(1)} %bitcast.48), channel_id=1, replica_groups=mesh['grp'=64,'own'=8] {'grp'}, dimensions={0} | all-to-all | bytes 131072 | tf_op jit(solution)/shard_map/all_to_all | solution.py:209
  103.6 1.4 far.6
  105.0 9.5 %all_to_all.44.parts_ref = bf16[8,16,256]{2,1,0:T(8,128)(2,1)S(1)} all-to-all(bf16[8,16,256]{2,1,0:T(8,128)(2,1)S(1)} %bitcast.53), channel_id=1, replica_groups=mesh['grp'=64,'own'=8] {'own'}, dimensions={0} | all-to-all | bytes 131072 | tf_op jit(solution)/shard_map/all_to_all | solution.py:227
  114.5 1.6 %step.5 = (bf16[64,256]{1,0:T(8,128)(2,1)S(1)}, bf16[64,256]{1,0:T(8,128)(2,1)}, bf16[256,128]{1,0:T(8,128)(2,1)S(1)}) custom-call(f32[4]{0:T(128)S(1)} %maximum_reduce_fusion.weight_ref, bf16[8,16,256]{2,1,0:T(8,128)(2,1)S(1)} %all_to_all.44.parts_ref, f32[16,256]{1,0:T(8,128)S(1)} %get-tuple-element.46.base_ref, bf16[16,256,256]{2,1,0:T(8,128)(2,1)S(1)} %bitcast.38, ...), custom_call_target="tpu_custom_call" | custom-call | tf_op jit(solution)/shard_map/step/pallas_call | solution.py:231
  116.0 17.9 %all_to_all.45 = bf16[64,4,128]{2,1,0:T(4,128)(2,1)S(1)} all-to-all(bf16[64,4,128]{2,1,0:T(4,128)(2,1)S(1)} %bitcast.47), channel_id=1, replica_groups=mesh['grp'=64,'own'=8] {'grp'}, dimensions={0} | all-to-all | bytes 131072 | tf_op jit(solution)/shard_map/all_to_all | solution.py:209
  134.0 1.4 far.7
  135.4 9.5 %all_to_all.46.parts_ref = bf16[8,16,256]{2,1,0:T(8,128)(2,1)S(1)} all-to-all(bf16[8,16,256]{2,1,0:T(8,128)(2,1)S(1)} %bitcast.49), channel_id=1, replica_groups=mesh['grp'=64,'own'=8] {'own'}, dimensions={0} | all-to-all | bytes 131072 | tf_op jit(solution)/shard_map/all_to_all | solution.py:227
  144.9 1.7 %last.1 = (bf16[4,16,256]{2,1,0:T(8,128)(2,1)}, f32[16,16,256]{2,1,0:T(8,128)}) custom-call(f32[16]{0:T(128)S(1)} %copy-done.7, bf16[8,16,256]{2,1,0:T(8,128)(2,1)S(1)} %all_to_all.46.parts_ref, f32[16,256]{1,0:T(8,128)S(1)} %get-tuple-element.51.base_ref, bf16[16,256,256]{2,1,0:T(8,128)(2,1)S(1)} %bitcast.39, ...), custom_call_target="tpu_custom_call" | custom-call | tf_op jit(solution)/shard_map/last/pallas_call | solution.py:241
  (23 shorter events, 0.2 us)
Async XLA Ops:
  2.1 0.8 copy-start.5
  4.0 33.1 %all-to-all-start = ((bf16[64,4,128]{2,1,0:T(4,128)(2,1)}), bf16[64,4,128]{2,1,0:T(4,128)(2,1)S(1)}, u32[]{:S(2)}, u32[]{:S(2)}) async-start(bf16[64,4,128]{2,1,0:T(4,128)(2,1)} %bitcast), calls=%async_computation | async-start | bytes 131072 | tf_op jit(solution)/shard_map/all_to_all | solution.py:209
  27.5 3.0 %copy-start.8 = (f32[16]{0:T(128)S(1)}, f32[16]{0:T(128)}, u32[]{:S(2)}) copy-start(f32[16]{0:T(128)} %param.22) | copy-start | bytes 196
  27.5 9.6 %copy-start.2 = (bf16[2,256,256]{2,1,0:T(8,128)(2,1)S(1)}, bf16[2,256,256]{2,1,0:T(8,128)(2,1)}, u32[]{:S(2)}) copy-start(bf16[2,256,256]{2,1,0:T(8,128)(2,1)} %near_ref.7) | copy-start | bytes 786436
  27.6 9.6 %copy-start.4 = (bf16[4,16,256]{2,1,0:T(8,128)(2,1)S(1)}, bf16[4,16,256]{2,1,0:T(8,128)(2,1)}, u32[]{:S(2)}) copy-start(bf16[4,16,256]{2,1,0:T(8,128)(2,1)} %param.15) | copy-start | bytes 98308
  30.5 21.1 %copy-start.6 = (bf16[4,16,256]{2,1,0:T(8,128)(2,1)S(1)}, bf16[4,16,256]{2,1,0:T(8,128)(2,1)}, u32[]{:S(2)}) copy-start(bf16[4,16,256]{2,1,0:T(8,128)(2,1)} %ret_ref.1) | copy-start | bytes 98308
  37.1 1.6 %copy-start = (bf16[16,256,256]{2,1,0:T(8,128)(2,1)S(1)}, bf16[16,256,256]{2,1,0:T(8,128)(2,1)}, u32[]{:S(2)}) copy-start(bf16[16,256,256]{2,1,0:T(8,128)(2,1)} %far_ref.7) | copy-start | bytes 6291460
  40.1 33.7 %copy-start.1 = (bf16[16,256,256]{2,1,0:T(8,128)(2,1)S(1)}, bf16[16,256,256]{2,1,0:T(8,128)(2,1)}, u32[]{:S(2)}) copy-start(bf16[16,256,256]{2,1,0:T(8,128)(2,1)} %far_ref.7) | copy-start | bytes 6291460
  116.0 28.8 %copy-start.3 = (f32[16,16,256]{2,1,0:T(8,128)S(1)}, f32[16,16,256]{2,1,0:T(8,128)}, u32[]{:S(2)}) copy-start(f32[16,16,256]{2,1,0:T(8,128)} %state_ref.1) | copy-start | bytes 786436
  116.0 28.8 %copy-start.7 = (f32[16]{0:T(128)S(1)}, f32[16]{0:T(128)}, u32[]{:S(2)}) copy-start(f32[16]{0:T(128)} %pole_ref.1) | copy-start | bytes 196

commit v3 on v2

v3 whole, which is shorter than its diff:
```python
import functools

import jax
import jax.numpy as jnp
from jax import lax
from jax.experimental import pallas as pl
from jax.experimental.pallas import tpu as pltpu
from jax.sharding import PartitionSpec as P

STEPS = 4
HIST = 4
F32 = jnp.float32
BF16 = jnp.bfloat16
I32 = jnp.int32
LANES = 128
FAR_PIECES = 4
CONTRACT_LAST = (((1,), (1,)), ((), ()))
VMEM = pl.BlockSpec(memory_space=pltpu.VMEM)
HBM = pl.BlockSpec(memory_space=pltpu.HBM)
SMEM = pl.BlockSpec(memory_space=pltpu.SMEM)


def halves_stacked(rows):
    return jnp.concatenate([rows[:, :LANES], rows[:, LANES:]], axis=0)


def shifted(x, bits):
    return lax.shift_right_logical(x, jnp.full(x.shape, bits, x.dtype))


def first_kernel(
    dest_hbm, delay_hbm, ret_hbm, pick_ref, out_ref, dest_ref, delay_ref, ret_ref, sem
):
    copies = [
        pltpu.make_async_copy(src, dst, sem.at[n])
        for n, (src, dst) in enumerate(
            ((dest_hbm, dest_ref), (delay_hbm, delay_ref), (ret_hbm, ret_ref))
        )
    ]
    for copy in copies:
        copy.start()
    names, tiles = dest_ref.shape
    shape = pick_ref.shape
    rows, cols = shape
    at = lax.broadcasted_iota(I32, shape, 0)
    col = lax.broadcasted_iota(I32, (1, cols), 1)
    tile_bits = tiles.bit_length() - 1
    group = shifted(at, 2)
    slab = shifted(col, tile_bits)
    col_delay = (slab & (HIST - 1)) + 1
    col_half = shifted(col, tile_bits + HIST.bit_length() - 1)
    spread = jnp.where(
        lax.broadcasted_iota(I32, (tiles, cols), 0) == (col & (tiles - 1)), 1.0, 0.0
    ).astype(BF16)
    of = lax.broadcasted_iota(I32, (cols, cols), 0)
    earlier = jnp.where((shifted(of, tile_bits) == slab) & (of < col), 1.0, 0.0).astype(BF16)
    placed = (col_half == (shifted(at, 1) & 1)).astype(F32)
    rank = (at & 1).astype(F32)
    copies[0].wait()
    copies[1].wait()
    dest = lax.dot(dest_ref[...].astype(F32).astype(BF16), spread, preferred_element_type=F32)
    delay = lax.dot(delay_ref[...].astype(F32).astype(BF16), spread, preferred_element_type=F32)
    dest = dest.astype(I32)
    on_time = delay.astype(I32) == col_delay
    dest_on_time = jnp.where(on_time, dest, -1)
    named = jnp.zeros(shape, F32)
    timed = jnp.zeros(shape, F32)
    for j in range(names):
        named = jnp.where(dest[j : j + 1] == group, 1.0, named)
        timed = jnp.where(dest_on_time[j : j + 1] == group, placed, timed)
    before = lax.dot(named.astype(BF16), earlier, preferred_element_type=F32)
    pick = jnp.where(before == rank, timed, 0.0).astype(BF16)
    pick_ref[...] = pick
    copies[2].wait()
    out_ref[...] = lax.dot(
        pick, halves_stacked(ret_ref[...]), preferred_element_type=F32
    ).astype(BF16)


def tables_kernel(
    pole_ref, residue_ref, reader_ref, src_ref, delay_ref, state_ref,
    hits_ref, split_ref, near_pick_ref, tail_ref, coef_ref,
):
    cap, classes, groups = reader_ref.shape
    slots = cap * groups
    group_tiles = hits_ref.shape[0]
    readers = jnp.concatenate([reader_ref[c] for c in range(cap)], axis=1)
    place = lax.broadcasted_iota(I32, (group_tiles, slots), 0)
    for k in range(classes):
        hits_ref[:, k * slots : (k + 1) * slots] = jnp.where(
            place == readers[k : k + 1], 1.0, 0.0
        ).astype(BF16)
    slot = lax.broadcasted_iota(I32, (slots, 1), 0)
    row = lax.broadcasted_iota(I32, split_ref.shape[1:], 1)
    group_bits = groups.bit_length() - 1
    start = 4 * (slot & (groups - 1)) + shifted(slot, group_bits)
    for h in range(2):
        split_ref[h] = jnp.where(row == start + 2 * h, 1.0, 0.0).astype(BF16)
    sources, tiles = src_ref.shape
    near_row = ((delay_ref[...] - 1) * tiles + src_ref[...]).astype(F32).astype(BF16)
    eye = jnp.where(
        lax.broadcasted_iota(I32, (tiles, tiles), 0) == lax.broadcasted_iota(I32, (tiles, tiles), 1),
        1.0,
        0.0,
    ).astype(BF16)
    near_col = lax.dot_general(eye, near_row, CONTRACT_LAST, preferred_element_type=F32)
    near_col = near_col.astype(I32)
    at = lax.broadcasted_iota(I32, (tiles, near_pick_ref.shape[1]), 1)
    near_pick_ref[...] = jnp.concatenate(
        [jnp.where(at == near_col[:, a : a + 1], 1.0, 0.0) for a in range(sources)], axis=0
    ).astype(BF16)
    count = state_ref.shape[0]
    scale = [residue_ref[p] for p in range(count)]
    width = coef_ref.shape[1]
    for n in range(STEPS):
        total = scale[0]
        for p in range(1, count):
            total = total + scale[p]
        coef_ref[n : n + 1, :] = jnp.full((1, width), total, F32)
        if n + 1 < STEPS:
            scale = [scale[p] * pole_ref[p] for p in range(count)]
            tail = scale[0] * state_ref[0]
            for p in range(1, count):
                tail = tail + scale[p] * state_ref[p]
            tail_ref[n] = tail
    for p in range(count):
        coef_ref[8 + p : 9 + p, :] = jnp.full((1, width), pole_ref[p], F32)


def far_terms(entries, far_ref, terms_ref, first, last):
    slots = entries.shape[0]
    for k in range(first, last):
        terms = lax.dot_general(entries, far_ref[k], CONTRACT_LAST, preferred_element_type=F32)
        terms_ref[pl.ds(k * slots, slots), :] = terms.astype(BF16)


def entries_of(in_ref, split_ref):
    incoming = in_ref[...]
    return jnp.concatenate(
        [
            lax.dot(split_ref[h], incoming, preferred_element_type=F32).astype(BF16)
            for h in range(2)
        ],
        axis=1,
    )


def near_base(step, near_pick_ref, cur_ref, near_ref, exc_ref):
    near_rows = lax.dot(near_pick_ref[...], cur_ref[...], preferred_element_type=F32).astype(BF16)
    classes = near_ref.shape[0]
    tiles = exc_ref.shape[1]
    per_class = near_rows.shape[0] // classes
    base = exc_ref[step].astype(F32)
    for k in range(classes):
        near = lax.dot_general(
            near_rows[k * per_class : (k + 1) * per_class],
            near_ref[k],
            CONTRACT_LAST,
            preferred_element_type=F32,
        )
        for m in range(per_class // tiles):
            base = base - near[m * tiles : (m + 1) * tiles]
    return base


def far_first_kernel(
    in_ref, split_ref, far_hbm, hits_ref, near_pick_ref, cur_hbm, near_ref, exc_ref,
    part_ref, base_ref, far_ref, terms_ref, cur_ref, sem,
):
    size = far_ref.shape[0] // FAR_PIECES
    copies = [
        pltpu.make_async_copy(
            far_hbm.at[pl.ds(n * size, size)], far_ref.at[pl.ds(n * size, size)], sem.at[n]
        )
        for n in range(FAR_PIECES)
    ]
    current = pltpu.make_async_copy(cur_hbm, cur_ref, sem.at[FAR_PIECES])
    current.start()
    for copy in copies:
        copy.start()
    entries = entries_of(in_ref, split_ref)
    current.wait()
    base_ref[...] = near_base(0, near_pick_ref, cur_ref, near_ref, exc_ref)
    for n in range(FAR_PIECES):
        copies[n].wait()
        far_terms(entries, far_ref, terms_ref, n * size, (n + 1) * size)
    part_ref[...] = lax.dot(
        hits_ref[...], terms_ref[...], preferred_element_type=F32
    ).astype(BF16)


def far_kernel(
    step, in_ref, split_ref, far_ref, hits_ref, near_pick_ref, cur_ref, near_ref, exc_ref,
    part_ref, base_ref, terms_ref,
):
    far_terms(entries_of(in_ref, split_ref), far_ref, terms_ref, 0, far_ref.shape[0])
    base_ref[...] = near_base(step, near_pick_ref, cur_ref, near_ref, exc_ref)
    part_ref[...] = lax.dot(
        hits_ref[...], terms_ref[...], preferred_element_type=F32
    ).astype(BF16)


def solve(parts_ref, base_ref, inverse_ref):
    far_field = parts_ref[0].astype(F32)
    for o in range(1, parts_ref.shape[0]):
        far_field = far_field + parts_ref[o].astype(F32)
    right_side = (base_ref[...] - far_field).astype(BF16)
    tiles = right_side.shape[0]
    row = lax.broadcasted_iota(I32, right_side.shape, 0)
    current = jnp.zeros(right_side.shape, F32)
    for t in range(tiles):
        current = jnp.where(
            row == t, lax.dot(right_side, inverse_ref[t], preferred_element_type=F32), current
        )
    return current.astype(BF16)


def step_kernel(
    step, coef_ref, parts_ref, base_ref, inverse_ref, tail_ref, cur_ref, ret_ref, pick_ref,
    cur_out, send_ref, ret_out=None,
):
    current = solve(parts_ref, base_ref, inverse_ref)
    tiles = current.shape[0]
    wide = current.astype(F32)
    retarded = wide * (1.0 + coef_ref[0:1, :]) + tail_ref[step]
    for back in range(1, step + 1):
        past = cur_ref[pl.ds((back - 1) * tiles, tiles), :]
        retarded = retarded + coef_ref[back : back + 1, :] * past.astype(F32)
    kept = cur_ref.shape[0] - tiles
    cur_out[...] = jnp.concatenate([current, cur_ref[:kept, :]], axis=0)
    history = jnp.concatenate([retarded.astype(BF16), ret_ref[:kept, :]], axis=0)
    if ret_out is not None:
        ret_out[...] = history
    send_ref[...] = lax.dot(
        pick_ref[...], halves_stacked(history), preferred_element_type=F32
    ).astype(BF16)


def last_kernel(coef_ref, parts_ref, base_ref, inverse_ref, cur_ref, state_ref, cur_out, state_out):
    current = solve(parts_ref, base_ref, inverse_ref)
    tiles = current.shape[0]
    past = [cur_ref[pl.ds((STEPS - 2 - n) * tiles, tiles), :] for n in range(STEPS - 1)] + [current]
    for n in range(STEPS):
        cur_out[n] = past[n]
    wide = [c.astype(F32) for c in past]
    for p in range(state_ref.shape[0]):
        pole = coef_ref[8 + p : 9 + p, :]
        state = state_ref[p]
        for n in range(STEPS):
            state = pole * state + wide[n]
        state_out[p] = state


def in_hbm(x):
    return pltpu.with_memory_space_constraint(x, pltpu.HBM)


def call(kernel, name, outs, specs, scratch=()):
    return pl.pallas_call(
        kernel,
        name=name,
        out_shape=outs,
        in_specs=specs,
        out_specs=jax.tree.map(lambda _: VMEM, outs),
        scratch_shapes=scratch,
        compiler_params=pltpu.CompilerParams(vmem_limit_bytes=8 << 20),
    )


def body(
    excitation,
    cur_hist,
    ret_hist,
    pole_state,
    self_inverse,
    near_mats,
    far_mats,
    poles,
    residues,
    near_src,
    near_delay,
    far_dest,
    far_delay,
    far_reader,
):
    groups = far_reader.shape[1]
    cap = far_reader.shape[3]
    classes = far_reader.shape[4]
    tiles = excitation.shape[1]
    width = excitation.shape[2]
    owners = lax.axis_size("own")
    group_tiles = tiles * owners
    slots = groups * cap
    past = HIST * tiles
    shape = jax.ShapeDtypeStruct

    history = ret_hist.reshape(past, width)
    names = far_dest.shape[1]
    pick, outgoing = call(
        first_kernel,
        "first",
        (shape((2 * slots, 2 * past), BF16), shape((2 * slots, LANES), BF16)),
        [HBM] * 3,
        [
            pltpu.VMEM((names, tiles), I32),
            pltpu.VMEM((names, tiles), I32),
            pltpu.VMEM((past, width), BF16),
            pltpu.SemaphoreType.DMA((3,)),
        ],
    )(in_hbm(far_dest.T), in_hbm(far_delay.T), in_hbm(history))

    sources = near_src.shape[0] * near_src.shape[2]
    poles_count = poles.shape[0]
    reader_hits, split, near_pick, tail, coef = call(
        tables_kernel,
        "tables",
        (
            shape((group_tiles, classes * slots), BF16),
            shape((2, slots, 2 * slots), BF16),
            shape((sources * tiles, past), BF16),
            shape((STEPS - 1, tiles, width), F32),
            shape((8 + poles_count, width), F32),
        ),
        [SMEM] * 2 + [VMEM] * 4,
    )(
        in_hbm(poles),
        in_hbm(residues),
        far_reader[0, :, 0].transpose(1, 2, 0),
        near_src.transpose(0, 2, 1).reshape(sources, tiles),
        near_delay.transpose(0, 2, 1).reshape(sources, tiles),
        pole_state,
    )
    inverse = self_inverse.swapaxes(1, 2)

    current = cur_hist.reshape(past, width)
    retarded = history
    for step in range(STEPS):
        incoming = lax.all_to_all(
            outgoing.reshape(groups, 2 * cap, LANES), "grp", split_axis=0, concat_axis=0, tiled=True
        ).reshape(2 * slots, LANES)
        if step == 0:
            incoming, inverse, tail, coef, reader_hits, near_pick, split = (
                lax.optimization_barrier(
                    (incoming, inverse, tail, coef, reader_hits, near_pick, split)
                )
            )
        outs = (shape((group_tiles, width), BF16), shape((tiles, width), F32))
        terms = pltpu.VMEM((classes * slots, width), BF16)
        if step == 0:
            part, base, far_kept = call(
                far_first_kernel,
                "far",
                outs + (shape(far_mats.shape, BF16),),
                [VMEM] * 2 + [HBM] + [VMEM] * 2 + [HBM] + [VMEM] * 2,
                [
                    terms,
                    pltpu.VMEM((past, width), BF16),
                    pltpu.SemaphoreType.DMA((FAR_PIECES + 1,)),
                ],
            )(
                incoming, split, in_hbm(far_mats), reader_hits, near_pick, in_hbm(current),
                near_mats, excitation,
            )
        else:
            part, base = call(
                functools.partial(far_kernel, step), "far", outs, [VMEM] * 8, [terms]
            )(incoming, split, far_kept, reader_hits, near_pick, current, near_mats, excitation)
        parts = lax.all_to_all(
            part.reshape(owners, tiles, width), "own", split_axis=0, concat_axis=0, tiled=True
        )
        if step + 1 < STEPS:
            outs = (shape((past, width), BF16), shape((2 * slots, LANES), BF16))
            if step + 2 < STEPS:
                outs = outs + (shape((past, width), BF16),)
            made = call(
                functools.partial(step_kernel, step), "step", outs, [VMEM] * 8
            )(coef, parts, base, inverse, tail, current, retarded, pick)
            current, outgoing = made[:2]
            retarded = made[-1]
    return call(
        last_kernel,
        "last",
        (shape((STEPS, tiles, width), BF16), shape(pole_state.shape, F32)),
        [VMEM] * 6,
    )(coef, parts, base, inverse, current, pole_state)


def solution(mesh):
    in_specs = (
        P(None, ("grp", "own"), None),
        P(None, ("grp", "own"), None),
        P(None, ("grp", "own"), None),
        P(None, ("grp", "own"), None),
        P(("grp", "own"), None, None),
        P(),
        P(),
        P(),
        P(),
        P(None, ("grp", "own"), None),
        P(None, ("grp", "own"), None),
        P(("grp", "own"), None),
        P(("grp", "own"), None),
        P("grp", None, "own", None, None),
    )
    out_specs = (P(None, ("grp", "own"), None), P(None, ("grp", "own"), None))
    return jax.shard_map(body, mesh=mesh, in_specs=in_specs, out_specs=out_specs, check_vma=False)
```

time: 147 us -> 139 us (0.946)
  local copies, waits for them, and re-layouts: 8.5 us -> 2.98 us
  blocking collectives: 96.6 us -> 92.8 us
  waiting for transfers between devices: 6.31 us -> 9.98 us
  other arithmetic: 2.99 us -> 0 us
    unnamed x22 -> x17, local copies, waits for them, and re-layouts: 7.61 us -> 2.98 us
    all_to_all x1, waiting for transfers between devices: 6.31 us -> 9.98 us  [body(): lax.all_to_all(outgoing.reshape(groups, 2 * cap, LANES), 'grp', split_axi...]
    all_to_all x3, blocking collectives: 56.9 us -> 53.4 us  [body(): lax.all_to_all(outgoing.reshape(groups, 2 * cap, LANES), 'grp', split_axi...]
    pallas_call x7 -> x8, Pallas kernels: 9.44 us -> 9.62 us  [the longest x3 4.31 us: body(): call(functools.partial(far_kernel, step), 'far', outs, [VMEM] * 8, [terms])]
  transfers between devices with their start and end apart: 1 -> 1, of which waited for: 1 -> 1; matrix products, arithmetic and copies ran while one was open for 5% -> 2% of each run, Pallas kernels for 0% -> 1%
where the time goes in v3:
time: 139 us; the launch traced here: 138 us
  blocking collectives  92.8 us (67%)
  starting transfers between devices  19.1 us (14%)
  Pallas kernels  12.5 us (9%)
  waiting for transfers between devices  9.98 us (7%)
  local copies, waits for them, and re-layouts  2.98 us (2%)
    all_to_all x3, blocking collectives, body(): lax.all_to_all(outgoing.reshape(groups, 2 * cap, LANES), 'grp', split_axi...  53.4 us
    all_to_all x4, blocking collectives, body(): lax.all_to_all(part.reshape(owners, tiles, width), 'own', split_axis=0, c...  39.4 us
    all_to_all x1, starting transfers between devices, body(): lax.all_to_all(outgoing.reshape(groups, 2 * cap, LANES), 'grp', split_axi...  19.1 us
    all_to_all x1, waiting for transfers between devices, body(): lax.all_to_all(outgoing.reshape(groups, 2 * cap, LANES), 'grp', split_axi...  9.98 us
    pallas_call x3, Pallas kernels, body(): call(functools.partial(far_kernel, step), 'far', outs, [VMEM] * 8, [terms])  4.31 us
    unnamed x17, local copies, waits for them, and re-layouts  2.98 us
  transfers between devices with their start and end apart: 1, of which 1 were waited for; matrix products, arithmetic and copies ran while one was open for 2% of the time, Pallas kernels for 1%

profile of v3, /device:TPU:1, one launch (start us, length us, event | category | flops | bytes accessed | tf_op | source)
XLA Modules:
  0.0 138.3 jit_solution(4812220862008308271)
XLA Ops:
  0.6 1.8 %first.1 = (bf16[256,128]{1,0:T(8,128)(2,1)S(1)}, bf16[256,128]{1,0:T(8,128)(2,1)}) custom-call(s32[4,16]{1,0:T(4,128)} %bitcast.48, s32[4,16]{1,0:T(4,128)} %bitcast.49, bf16[64,256]{1,0:T(8,128)(2,1)} %bitcast.36), custom_call_target="tpu_custom_call" | custom-call | tf_op jit(solution)/shard_map/first/pallas_call | solution.py:299
  2.4 19.1 %all-to-all-start = ((bf16[64,4,128]{2,1,0:T(4,128)(2,1)}), bf16[64,4,128]{2,1,0:T(4,128)(2,1)S(1)}, u32[]{:S(2)}, u32[]{:S(2)}) async-start(bf16[64,4,128]{2,1,0:T(4,128)(2,1)} %bitcast.3), calls=%async_computation | async-start | bytes 131072 | tf_op jit(solution)/shard_map/all_to_all | solution.py:338
  21.6 0.0 copy-start.1
  21.6 0.0 copy-start.5
  21.6 0.0 copy-start.6
  21.6 0.0 copy-start.7
  21.6 0.0 copy-start
  21.6 0.0 copy-start.2
  21.6 2.9 %copy.16 = bf16[16,256,256]{1,2,0:T(8,128)(2,1)S(1)} copy(bf16[16,256,256]{2,1,0:T(8,128)(2,1)} %param.18) | data formatting | bytes 4194304 | tf_op args[4]
  24.6 0.0 copy-done.1
  24.6 0.0 copy-done.5
  24.6 0.0 copy-done.6
  24.6 0.0 copy-done.7
  24.6 1.0 tables.1
  25.6 10.0 %all-to-all-done = bf16[64,4,128]{2,1,0:T(4,128)(2,1)S(1)} async-done(((bf16[64,4,128]{2,1,0:T(4,128)(2,1)}), bf16[64,4,128]{2,1,0:T(4,128)(2,1)S(1)}, u32[]{:S(2)}, u32[]{:S(2)}) %all-to-all-start) | async-done | bytes 65568 | tf_op jit(solution)/shard_map/all_to_all | solution.py:338
  35.6 0.0 copy-done
  35.6 2.7 %far.4 = (bf16[128,256]{1,0:T(8,128)(2,1)S(1)}, f32[16,256]{1,0:T(8,128)S(1)}, bf16[16,256,256]{2,1,0:T(8,128)(2,1)S(1)}) custom-call(bf16[256,128]{1,0:T(8,128)(2,1)S(1)} %bitcast.30, bf16[2,128,256]{2,1,0:T(8,128)(2,1)S(1)} %get-tuple-element.41.split_ref, bf16[16,256,256]{2,1,0:T(8,128)(2,1)} %far_hbm.1, ...), custom_call_target="tpu_custom_call" | custom-call | tf_op jit(solution)/shard_map/far/pallas_call | solution.py:350
  38.3 11.3 %all_to_all.40.parts_ref = bf16[8,16,256]{2,1,0:T(8,128)(2,1)S(1)} all-to-all(bf16[8,16,256]{2,1,0:T(8,128)(2,1)S(1)} %bitcast.42), channel_id=1, replica_groups=mesh['grp'=64,'own'=8] {'own'}, dimensions={0} | all-to-all | bytes 131072 | tf_op jit(solution)/shard_map/all_to_all | solution.py:368
  49.6 0.0 copy-done.3
  49.6 0.5 step.3
  50.1 17.8 %all_to_all.41 = bf16[64,4,128]{2,1,0:T(4,128)(2,1)S(1)} all-to-all(bf16[64,4,128]{2,1,0:T(4,128)(2,1)S(1)} %bitcast.41), channel_id=1, replica_groups=mesh['grp'=64,'own'=8] {'grp'}, dimensions={0} | all-to-all | bytes 131072 | tf_op jit(solution)/shard_map/all_to_all | solution.py:338
  67.9 1.4 %far.5 = (bf16[128,256]{1,0:T(8,128)(2,1)S(1)}, f32[16,256]{1,0:T(8,128)S(1)}) custom-call(bf16[256,128]{1,0:T(8,128)(2,1)S(1)} %bitcast.32, bf16[2,128,256]{2,1,0:T(8,128)(2,1)S(1)} %get-tuple-element.41.split_ref, bf16[16,256,256]{2,1,0:T(8,128)(2,1)S(1)} %get-tuple-element.50.far_ref, bf16[128,2048]{1,0:T(8,128)(2,1)S(1)} %get-tuple-element.42.hits_ref, ...), custom_call_target="tpu_custom_call" | custom-call | tf_op jit(solution)/shard_map/far/pallas_call | solution.py:365
  69.4 9.2 %all_to_all.42.parts_ref = bf16[8,16,256]{2,1,0:T(8,128)(2,1)S(1)} all-to-all(bf16[8,16,256]{2,1,0:T(8,128)(2,1)S(1)} %bitcast.43), channel_id=1, replica_groups=mesh['grp'=64,'own'=8] {'own'}, dimensions={0} | all-to-all | bytes 131072 | tf_op jit(solution)/shard_map/all_to_all | solution.py:368
  78.6 0.5 step.4
  79.2 17.8 %all_to_all.43 = bf16[64,4,128]{2,1,0:T(4,128)(2,1)S(1)} all-to-all(bf16[64,4,128]{2,1,0:T(4,128)(2,1)S(1)} %bitcast.39), channel_id=1, replica_groups=mesh['grp'=64,'own'=8] {'grp'}, dimensions={0} | all-to-all | bytes 131072 | tf_op jit(solution)/shard_map/all_to_all | solution.py:338
  97.0 1.4 %far.6 = (bf16[128,256]{1,0:T(8,128)(2,1)S(1)}, f32[16,256]{1,0:T(8,128)S(1)}) custom-call(bf16[256,128]{1,0:T(8,128)(2,1)S(1)} %bitcast.33, bf16[2,128,256]{2,1,0:T(8,128)(2,1)S(1)} %get-tuple-element.41.split_ref, bf16[16,256,256]{2,1,0:T(8,128)(2,1)S(1)} %get-tuple-element.50.far_ref, bf16[128,2048]{1,0:T(8,128)(2,1)S(1)} %get-tuple-element.42.hits_ref, ...), custom_call_target="tpu_custom_call" | custom-call | tf_op jit(solution)/shard_map/far/pallas_call | solution.py:365
  98.4 9.5 %all_to_all.44.parts_ref = bf16[8,16,256]{2,1,0:T(8,128)(2,1)S(1)} all-to-all(bf16[8,16,256]{2,1,0:T(8,128)(2,1)S(1)} %bitcast.44), channel_id=1, replica_groups=mesh['grp'=64,'own'=8] {'own'}, dimensions={0} | all-to-all | bytes 131072 | tf_op jit(solution)/shard_map/all_to_all | solution.py:368
  107.9 0.5 step.5
  108.4 17.8 %all_to_all.45 = bf16[64,4,128]{2,1,0:T(4,128)(2,1)S(1)} all-to-all(bf16[64,4,128]{2,1,0:T(4,128)(2,1)S(1)} %bitcast.38), channel_id=1, replica_groups=mesh['grp'=64,'own'=8] {'grp'}, dimensions={0} | all-to-all | bytes 131072 | tf_op jit(solution)/shard_map/all_to_all | solution.py:338
  126.2 1.4 %far.7 = (bf16[128,256]{1,0:T(8,128)(2,1)S(1)}, f32[16,256]{1,0:T(8,128)S(1)}) custom-call(bf16[256,128]{1,0:T(8,128)(2,1)S(1)} %bitcast.31, bf16[2,128,256]{2,1,0:T(8,128)(2,1)S(1)} %get-tuple-element.41.split_ref, bf16[16,256,256]{2,1,0:T(8,128)(2,1)S(1)} %get-tuple-element.50.far_ref, bf16[128,2048]{1,0:T(8,128)(2,1)S(1)} %get-tuple-element.42.hits_ref, ...), custom_call_target="tpu_custom_call" | custom-call | tf_op jit(solution)/shard_map/far/pallas_call | solution.py:365
  127.7 9.5 %all_to_all.46.parts_ref = bf16[8,16,256]{2,1,0:T(8,128)(2,1)S(1)} all-to-all(bf16[8,16,256]{2,1,0:T(8,128)(2,1)S(1)} %bitcast.40), channel_id=1, replica_groups=mesh['grp'=64,'own'=8] {'own'}, dimensions={0} | all-to-all | bytes 131072 | tf_op jit(solution)/shard_map/all_to_all | solution.py:368
  137.1 1.1 last.1
  (4 shorter events, 0.0 us)
Async XLA Ops:
  2.4 33.1 %all-to-all-start = ((bf16[64,4,128]{2,1,0:T(4,128)(2,1)}), bf16[64,4,128]{2,1,0:T(4,128)(2,1)S(1)}, u32[]{:S(2)}, u32[]{:S(2)}) async-start(bf16[64,4,128]{2,1,0:T(4,128)(2,1)} %bitcast.3), calls=%async_computation | async-start | bytes 131072 | tf_op jit(solution)/shard_map/all_to_all | solution.py:338
  21.6 3.0 %copy-start.1 = (f32[16,16,256]{2,1,0:T(8,128)S(1)}, f32[16,16,256]{2,1,0:T(8,128)}, u32[]{:S(2)}) copy-start(f32[16,16,256]{2,1,0:T(8,128)} %state_ref.3) | copy-start | bytes 786436
  21.6 3.0 %copy-start.5 = (s32[1,64,1,2,16]{1,4,3,2,0:T(8,128)S(1)}, s32[1,64,1,2,16]{1,4,3,2,0:T(8,128)}, u32[]{:S(2)}) copy-start(s32[1,64,1,2,16]{1,4,3,2,0:T(8,128)} %param.27) | copy-start | bytes 24580
  21.6 3.0 %copy-start.6 = (s32[2,16,2]{1,2,0:T(2,128)S(1)}, s32[2,16,2]{1,2,0:T(2,128)}, u32[]{:S(2)}) copy-start(s32[2,16,2]{1,2,0:T(2,128)} %param.23) | copy-start | bytes 772
  21.6 3.0 %copy-start.7 = (s32[2,16,2]{1,2,0:T(2,128)S(1)}, s32[2,16,2]{1,2,0:T(2,128)}, u32[]{:S(2)}) copy-start(s32[2,16,2]{1,2,0:T(2,128)} %param.24) | copy-start | bytes 772
  21.6 14.0 %copy-start = (bf16[2,256,256]{2,1,0:T(8,128)(2,1)S(1)}, bf16[2,256,256]{2,1,0:T(8,128)(2,1)}, u32[]{:S(2)}) copy-start(bf16[2,256,256]{2,1,0:T(8,128)(2,1)} %near_ref.7) | copy-start | bytes 786436
  21.6 14.0 %copy-start.2 = (bf16[4,16,256]{2,1,0:T(8,128)(2,1)S(1)}, bf16[4,16,256]{2,1,0:T(8,128)(2,1)}, u32[]{:S(2)}) copy-start(bf16[4,16,256]{2,1,0:T(8,128)(2,1)} %exc_ref.7) | copy-start | bytes 98308
  35.6 14.0 %copy-start.3 = (bf16[4,16,256]{2,1,0:T(8,128)(2,1)S(1)}, bf16[4,16,256]{2,1,0:T(8,128)(2,1)}, u32[]{:S(2)}) copy-start(bf16[4,16,256]{2,1,0:T(8,128)(2,1)} %param.15) | copy-start | bytes 98308
  35.6 14.0 %copy-start.4 = (bf16[4,16,256]{2,1,0:T(8,128)(2,1)S(1)}, bf16[4,16,256]{2,1,0:T(8,128)(2,1)}, u32[]{:S(2)}) copy-start(bf16[4,16,256]{2,1,0:T(8,128)(2,1)} %param.16) | copy-start | bytes 98308

commit v4 on v3

--- a/solution.py
+++ b/solution.py
@@ -13,11 +13,9 @@
 BF16 = jnp.bfloat16
 I32 = jnp.int32
 LANES = 128
-FAR_PIECES = 4
 CONTRACT_LAST = (((1,), (1,)), ((), ()))
 VMEM = pl.BlockSpec(memory_space=pltpu.VMEM)
 HBM = pl.BlockSpec(memory_space=pltpu.HBM)
-SMEM = pl.BlockSpec(memory_space=pltpu.SMEM)
 
 
 def halves_stacked(rows):
@@ -28,17 +26,17 @@
     return lax.shift_right_logical(x, jnp.full(x.shape, bits, x.dtype))
 
 
+def fetch(sem, *pairs):
+    copies = [pltpu.make_async_copy(src, dst, sem.at[n]) for n, (src, dst) in enumerate(pairs)]
+    for copy in copies:
+        copy.start()
+    return copies
+
+
 def first_kernel(
     dest_hbm, delay_hbm, ret_hbm, pick_ref, out_ref, dest_ref, delay_ref, ret_ref, sem
 ):
-    copies = [
-        pltpu.make_async_copy(src, dst, sem.at[n])
-        for n, (src, dst) in enumerate(
-            ((dest_hbm, dest_ref), (delay_hbm, delay_ref), (ret_hbm, ret_ref))
-        )
-    ]
-    for copy in copies:
-        copy.start()
+    copies = fetch(sem, (dest_hbm, dest_ref), (delay_hbm, delay_ref), (ret_hbm, ret_ref))
     names, tiles = dest_ref.shape
     shape = pick_ref.shape
     rows, cols = shape
@@ -78,24 +76,38 @@
 
 
 def tables_kernel(
-    pole_ref, residue_ref, reader_ref, src_ref, delay_ref, state_ref,
-    hits_ref, split_ref, near_pick_ref, tail_ref, coef_ref,
-):
+    pole_hbm, residue_hbm, reader_hbm, src_hbm, delay_hbm, state_hbm, far_hbm,
+    hits_ref, split_ref, near_pick_ref, tail_ref, coef_ref, far_ref,
+    pole_ref, residue_ref, reader_ref, src_ref, delay_ref, state_ref, sem,
+):
+    reader_copy, src_copy, delay_copy, pole_copy, residue_copy, state_copy, far_copy = fetch(
+        sem,
+        (reader_hbm, reader_ref),
+        (src_hbm, src_ref),
+        (delay_hbm, delay_ref),
+        (pole_hbm, pole_ref),
+        (residue_hbm, residue_ref),
+        (state_hbm, state_ref),
+        (far_hbm, far_ref),
+    )
     cap, classes, groups = reader_ref.shape
     slots = cap * groups
     group_tiles = hits_ref.shape[0]
+    slot = lax.broadcasted_iota(I32, (slots, 1), 0)
+    row = lax.broadcasted_iota(I32, split_ref.shape[1:], 1)
+    group_bits = groups.bit_length() - 1
+    start = 4 * (slot & (groups - 1)) + shifted(slot, group_bits)
+    for h in range(2):
+        split_ref[h] = jnp.where(row == start + 2 * h, 1.0, 0.0).astype(BF16)
+    reader_copy.wait()
     readers = jnp.concatenate([reader_ref[c] for c in range(cap)], axis=1)
     place = lax.broadcasted_iota(I32, (group_tiles, slots), 0)
     for k in range(classes):
         hits_ref[:, k * slots : (k + 1) * slots] = jnp.where(
             place == readers[k : k + 1], 1.0, 0.0
         ).astype(BF16)
-    slot = lax.broadcasted_iota(I32, (slots, 1), 0)
-    row = lax.broadcasted_iota(I32, split_ref.shape[1:], 1)
-    group_bits = groups.bit_length() - 1
-    start = 4 * (slot & (groups - 1)) + shifted(slot, group_bits)
-    for h in range(2):
-        split_ref[h] = jnp.where(row == start + 2 * h, 1.0, 0.0).astype(BF16)
+    src_copy.wait()
+    delay_copy.wait()
     sources, tiles = src_ref.shape
     near_row = ((delay_ref[...] - 1) * tiles + src_ref[...]).astype(F32).astype(BF16)
     eye = jnp.where(
@@ -109,6 +121,9 @@
     near_pick_ref[...] = jnp.concatenate(
         [jnp.where(at == near_col[:, a : a + 1], 1.0, 0.0) for a in range(sources)], axis=0
     ).astype(BF16)
+    pole_copy.wait()
+    residue_copy.wait()
+    state_copy.wait()
     count = state_ref.shape[0]
     scale = [residue_ref[p] for p in range(count)]
     width = coef_ref.shape[1]
@@ -125,6 +140,7 @@
             tail_ref[n] = tail
     for p in range(count):
         coef_ref[8 + p : 9 + p, :] = jnp.full((1, width), pole_ref[p], F32)
+    far_copy.wait()
 
 
 def far_terms(entries, far_ref, terms_ref, first, last):
@@ -164,29 +180,20 @@
 
 
 def far_first_kernel(
-    in_ref, split_ref, far_hbm, hits_ref, near_pick_ref, cur_hbm, near_ref, exc_ref,
-    part_ref, base_ref, far_ref, terms_ref, cur_ref, sem,
-):
-    size = far_ref.shape[0] // FAR_PIECES
-    copies = [
-        pltpu.make_async_copy(
-            far_hbm.at[pl.ds(n * size, size)], far_ref.at[pl.ds(n * size, size)], sem.at[n]
-        )
-        for n in range(FAR_PIECES)
-    ]
-    current = pltpu.make_async_copy(cur_hbm, cur_ref, sem.at[FAR_PIECES])
-    current.start()
+    in_ref, split_ref, far_ref, hits_ref, near_pick_ref, cur_hbm, near_hbm, exc_hbm,
+    inverse_hbm, part_ref, base_ref, inverse_ref, terms_ref, cur_ref, near_ref, exc_ref, sem,
+):
+    copies = fetch(sem, (cur_hbm, cur_ref), (near_hbm, near_ref), (exc_hbm, exc_ref))
+    inverse_copy = pltpu.make_async_copy(inverse_hbm, inverse_ref, sem.at[len(copies)])
+    inverse_copy.start()
+    far_terms(entries_of(in_ref, split_ref), far_ref, terms_ref, 0, far_ref.shape[0])
     for copy in copies:
-        copy.start()
-    entries = entries_of(in_ref, split_ref)
-    current.wait()
+        copy.wait()
     base_ref[...] = near_base(0, near_pick_ref, cur_ref, near_ref, exc_ref)
-    for n in range(FAR_PIECES):
-        copies[n].wait()
-        far_terms(entries, far_ref, terms_ref, n * size, (n + 1) * size)
     part_ref[...] = lax.dot(
         hits_ref[...], terms_ref[...], preferred_element_type=F32
     ).astype(BF16)
+    inverse_copy.wait()
 
 
 def far_kernel(
@@ -210,7 +217,11 @@
     current = jnp.zeros(right_side.shape, F32)
     for t in range(tiles):
         current = jnp.where(
-            row == t, lax.dot(right_side, inverse_ref[t], preferred_element_type=F32), current
+            row == t,
+            lax.dot_general(
+                right_side, inverse_ref[t], CONTRACT_LAST, preferred_element_type=F32
+            ),
+            current,
         )
     return current.astype(BF16)
 
@@ -311,7 +322,7 @@
 
     sources = near_src.shape[0] * near_src.shape[2]
     poles_count = poles.shape[0]
-    reader_hits, split, near_pick, tail, coef = call(
+    reader_hits, split, near_pick, tail, coef, far_kept = call(
         tables_kernel,
         "tables",
         (
@@ -320,17 +331,27 @@
             shape((sources * tiles, past), BF16),
             shape((STEPS - 1, tiles, width), F32),
             shape((8 + poles_count, width), F32),
+            shape(far_mats.shape, BF16),
         ),
-        [SMEM] * 2 + [VMEM] * 4,
+        [HBM] * 7,
+        [
+            pltpu.SMEM((poles_count,), F32),
+            pltpu.SMEM((poles_count,), F32),
+            pltpu.VMEM((cap, classes, groups), I32),
+            pltpu.VMEM((sources, tiles), I32),
+            pltpu.VMEM((sources, tiles), I32),
+            pltpu.VMEM(pole_state.shape, F32),
+            pltpu.SemaphoreType.DMA((7,)),
+        ],
     )(
         in_hbm(poles),
         in_hbm(residues),
-        far_reader[0, :, 0].transpose(1, 2, 0),
-        near_src.transpose(0, 2, 1).reshape(sources, tiles),
-        near_delay.transpose(0, 2, 1).reshape(sources, tiles),
-        pole_state,
+        in_hbm(far_reader[0, :, 0].transpose(1, 2, 0)),
+        in_hbm(near_src.transpose(0, 2, 1).reshape(sources, tiles)),
+        in_hbm(near_delay.transpose(0, 2, 1).reshape(sources, tiles)),
+        in_hbm(pole_state),
+        in_hbm(far_mats),
     )
-    inverse = self_inverse.swapaxes(1, 2)
 
     current = cur_hist.reshape(past, width)
     retarded = history
@@ -339,27 +360,29 @@
             outgoing.reshape(groups, 2 * cap, LANES), "grp", split_axis=0, concat_axis=0, tiled=True
         ).reshape(2 * slots, LANES)
         if step == 0:
-            incoming, inverse, tail, coef, reader_hits, near_pick, split = (
+            incoming, tail, coef, reader_hits, near_pick, split, far_kept = (
                 lax.optimization_barrier(
-                    (incoming, inverse, tail, coef, reader_hits, near_pick, split)
+                    (incoming, tail, coef, reader_hits, near_pick, split, far_kept)
                 )
             )
         outs = (shape((group_tiles, width), BF16), shape((tiles, width), F32))
         terms = pltpu.VMEM((classes * slots, width), BF16)
         if step == 0:
-            part, base, far_kept = call(
+            part, base, inverse = call(
                 far_first_kernel,
                 "far",
-                outs + (shape(far_mats.shape, BF16),),
-                [VMEM] * 2 + [HBM] + [VMEM] * 2 + [HBM] + [VMEM] * 2,
+                outs + (shape(self_inverse.shape, BF16),),
+                [VMEM] * 5 + [HBM] * 4,
                 [
                     terms,
                     pltpu.VMEM((past, width), BF16),
-                    pltpu.SemaphoreType.DMA((FAR_PIECES + 1,)),
+                    pltpu.VMEM(near_mats.shape, BF16),
+                    pltpu.VMEM(excitation.shape, BF16),
+                    pltpu.SemaphoreType.DMA((4,)),
                 ],
             )(
-                incoming, split, in_hbm(far_mats), reader_hits, near_pick, in_hbm(current),
-                near_mats, excitation,
+                incoming, split, far_kept, reader_hits, near_pick, in_hbm(current),
+                in_hbm(near_mats), in_hbm(excitation), in_hbm(self_inverse),
             )
         else:
             part, base = call(

time: 139 us -> 140 us (level)
  local copies, waits for them, and re-layouts: 2.98 us -> 0.03 us
  waiting for transfers between devices: 9.98 us -> 12.2 us
  Pallas kernels: 12.5 us -> 14.3 us
    unnamed x17 -> x10, local copies, waits for them, and re-layouts: 2.98 us -> 0.03 us
    all_to_all x1, waiting for transfers between devices: 9.98 us -> 12.2 us  [body(): lax.all_to_all(outgoing.reshape(groups, 2 * cap, LANES), 'grp', split_axi...]
  transfers between devices with their start and end apart: 1 -> 1, of which waited for: 1 -> 1; matrix products, arithmetic and copies ran while one was open for 2% -> 0% of each run, Pallas kernels for 1% -> 1%
where the time goes in v4:
time: 140 us
  blocking collectives  93.3 us (67%)
  starting transfers between devices  19.1 us (14%)
  Pallas kernels  14.3 us (10%)
  waiting for transfers between devices  12.2 us (9%)
    all_to_all x3, blocking collectives, body(): lax.all_to_all(outgoing.reshape(groups, 2 * cap, LANES), 'grp', split_axi...  53.6 us
    all_to_all x4, blocking collectives, body(): lax.all_to_all(part.reshape(owners, tiles, width), 'own', split_axis=0, c...  39.8 us
    all_to_all x1, starting transfers between devices, body(): lax.all_to_all(outgoing.reshape(groups, 2 * cap, LANES), 'grp', split_axi...  19.1 us
    all_to_all x1, waiting for transfers between devices, body(): lax.all_to_all(outgoing.reshape(groups, 2 * cap, LANES), 'grp', split_axi...  12.2 us
    pallas_call x3, Pallas kernels, body(): call(functools.partial(far_kernel, step), 'far', outs, [VMEM] * 8, [terms])  4.27 us
  transfers between devices with their start and end apart: 1, of which 1 were waited for; matrix products, arithmetic and copies ran while one was open for 0% of the time, Pallas kernels for 1%

profile of v4, /device:TPU:1, one launch (start us, length us, event | category | flops | bytes accessed | tf_op | source)
XLA Modules:
  0.0 139.7 jit_solution(13882929659264716158)
XLA Ops:
  0.6 1.8 %first.1 = (bf16[256,128]{1,0:T(8,128)(2,1)S(1)}, bf16[256,128]{1,0:T(8,128)(2,1)}) custom-call(s32[4,16]{1,0:T(4,128)} %bitcast.41, s32[4,16]{1,0:T(4,128)} %bitcast.42, bf16[64,256]{1,0:T(8,128)(2,1)} %bitcast.31), custom_call_target="tpu_custom_call" | custom-call | tf_op jit(solution)/shard_map/first/pallas_call | solution.py:310
  2.4 19.1 %all-to-all-start = ((bf16[64,4,128]{2,1,0:T(4,128)(2,1)}), bf16[64,4,128]{2,1,0:T(4,128)(2,1)S(1)}, u32[]{:S(2)}, u32[]{:S(2)}) async-start(bf16[64,4,128]{2,1,0:T(4,128)(2,1)} %bitcast.3), calls=%async_computation | async-start | bytes 131072 | tf_op jit(solution)/shard_map/all_to_all | solution.py:359
  21.6 1.8 %tables.1 = (bf16[128,2048]{1,0:T(8,128)(2,1)S(1)}, bf16[2,128,256]{2,1,0:T(8,128)(2,1)S(1)}, bf16[64,64]{1,0:T(8,128)(2,1)S(1)}, f32[3,16,256]{2,1,0:T(8,128)S(...) custom-call(f32[16]{0:T(128)} %pole_hbm.1, f32[16]{0:T(128)} %residue_hbm.1, s32[2,16,64]{2,1,0:T(8,128)} %bitcast.40, ...), custom_call_target="tpu_custom_call" | custom-call | tf_op jit(solution)/shard_map/tables/pallas_call | solution.py:325
  23.4 12.2 %all-to-all-done = bf16[64,4,128]{2,1,0:T(4,128)(2,1)S(1)} async-done(((bf16[64,4,128]{2,1,0:T(4,128)(2,1)}), bf16[64,4,128]{2,1,0:T(4,128)(2,1)S(1)}, u32[]{:S(2)}, u32[]{:S(2)}) %all-to-all-start) | async-done | bytes 65568 | tf_op jit(solution)/shard_map/all_to_all | solution.py:359
  35.6 0.0 copy-start.3
  35.6 0.0 copy-start.4
  35.6 2.6 %far.4 = (bf16[128,256]{1,0:T(8,128)(2,1)S(1)}, f32[16,256]{1,0:T(8,128)S(1)}, bf16[16,256,256]{2,1,0:T(8,128)(2,1)S(1)}) custom-call(bf16[256,128]{1,0:T(8,128)(2,1)S(1)} %bitcast.25, bf16[2,128,256]{2,1,0:T(8,128)(2,1)S(1)} %get-tuple-element.43.split_ref, bf16[16,256,256]{2,1,0:T(8,128)(2,1)S(1)} %get-tuple-element.44.far_ref, ...), custom_call_target="tpu_custom_call" | custom-call | tf_op jit(solution)/shard_map/far/pallas_call | solution.py:371
  38.2 0.0 copy-start
  38.2 0.0 copy-start.2
  38.2 11.4 %all_to_all.40.parts_ref = bf16[8,16,256]{2,1,0:T(8,128)(2,1)S(1)} all-to-all(bf16[8,16,256]{2,1,0:T(8,128)(2,1)S(1)} %bitcast.37), channel_id=1, replica_groups=mesh['grp'=64,'own'=8] {'own'}, dimensions={0} | all-to-all | bytes 131072 | tf_op jit(solution)/shard_map/all_to_all | solution.py:391
  49.6 0.0 copy-done.3
  49.6 0.0 copy-done.4
  49.6 0.8 step.3
  50.4 17.8 %all_to_all.41 = bf16[64,4,128]{2,1,0:T(4,128)(2,1)S(1)} all-to-all(bf16[64,4,128]{2,1,0:T(4,128)(2,1)S(1)} %bitcast.36), channel_id=1, replica_groups=mesh['grp'=64,'own'=8] {'grp'}, dimensions={0} | all-to-all | bytes 131072 | tf_op jit(solution)/shard_map/all_to_all | solution.py:359
  68.2 0.0 copy-done
  68.2 0.0 copy-done.2
  68.2 1.4 %far.5 = (bf16[128,256]{1,0:T(8,128)(2,1)S(1)}, f32[16,256]{1,0:T(8,128)S(1)}) custom-call(bf16[256,128]{1,0:T(8,128)(2,1)S(1)} %bitcast.27, bf16[2,128,256]{2,1,0:T(8,128)(2,1)S(1)} %get-tuple-element.43.split_ref, bf16[16,256,256]{2,1,0:T(8,128)(2,1)S(1)} %get-tuple-element.44.far_ref, bf16[128,2048]{1,0:T(8,128)(2,1)S(1)} %get-tuple-element.45.hits_ref, ...), custom_call_target="tpu_custom_call" | custom-call | tf_op jit(solution)/shard_map/far/pallas_call | solution.py:388
  69.7 9.5 %all_to_all.42.parts_ref = bf16[8,16,256]{2,1,0:T(8,128)(2,1)S(1)} all-to-all(bf16[8,16,256]{2,1,0:T(8,128)(2,1)S(1)} %bitcast.38), channel_id=1, replica_groups=mesh['grp'=64,'own'=8] {'own'}, dimensions={0} | all-to-all | bytes 131072 | tf_op jit(solution)/shard_map/all_to_all | solution.py:391
  79.1 0.8 step.4
  80.0 17.8 %all_to_all.43 = bf16[64,4,128]{2,1,0:T(4,128)(2,1)S(1)} all-to-all(bf16[64,4,128]{2,1,0:T(4,128)(2,1)S(1)} %bitcast.34), channel_id=1, replica_groups=mesh['grp'=64,'own'=8] {'grp'}, dimensions={0} | all-to-all | bytes 131072 | tf_op jit(solution)/shard_map/all_to_all | solution.py:359
  97.8 1.4 %far.6 = (bf16[128,256]{1,0:T(8,128)(2,1)S(1)}, f32[16,256]{1,0:T(8,128)S(1)}) custom-call(bf16[256,128]{1,0:T(8,128)(2,1)S(1)} %bitcast.28, bf16[2,128,256]{2,1,0:T(8,128)(2,1)S(1)} %get-tuple-element.43.split_ref, bf16[16,256,256]{2,1,0:T(8,128)(2,1)S(1)} %get-tuple-element.44.far_ref, bf16[128,2048]{1,0:T(8,128)(2,1)S(1)} %get-tuple-element.45.hits_ref, ...), custom_call_target="tpu_custom_call" | custom-call | tf_op jit(solution)/shard_map/far/pallas_call | solution.py:388
  99.2 9.5 %all_to_all.44.parts_ref = bf16[8,16,256]{2,1,0:T(8,128)(2,1)S(1)} all-to-all(bf16[8,16,256]{2,1,0:T(8,128)(2,1)S(1)} %bitcast.39), channel_id=1, replica_groups=mesh['grp'=64,'own'=8] {'own'}, dimensions={0} | all-to-all | bytes 131072 | tf_op jit(solution)/shard_map/all_to_all | solution.py:391
  108.7 0.8 step.5
  109.5 0.0 copy-start.1
  109.5 17.9 %all_to_all.45 = bf16[64,4,128]{2,1,0:T(4,128)(2,1)S(1)} all-to-all(bf16[64,4,128]{2,1,0:T(4,128)(2,1)S(1)} %bitcast.33), channel_id=1, replica_groups=mesh['grp'=64,'own'=8] {'grp'}, dimensions={0} | all-to-all | bytes 131072 | tf_op jit(solution)/shard_map/all_to_all | solution.py:359
  127.4 1.4 %far.7 = (bf16[128,256]{1,0:T(8,128)(2,1)S(1)}, f32[16,256]{1,0:T(8,128)S(1)}) custom-call(bf16[256,128]{1,0:T(8,128)(2,1)S(1)} %bitcast.26, bf16[2,128,256]{2,1,0:T(8,128)(2,1)S(1)} %get-tuple-element.43.split_ref, bf16[16,256,256]{2,1,0:T(8,128)(2,1)S(1)} %get-tuple-element.44.far_ref, bf16[128,2048]{1,0:T(8,128)(2,1)S(1)} %get-tuple-element.45.hits_ref, ...), custom_call_target="tpu_custom_call" | custom-call | tf_op jit(solution)/shard_map/far/pallas_call | solution.py:388
  128.9 9.5 %all_to_all.46.parts_ref = bf16[8,16,256]{2,1,0:T(8,128)(2,1)S(1)} all-to-all(bf16[8,16,256]{2,1,0:T(8,128)(2,1)S(1)} %bitcast.35), channel_id=1, replica_groups=mesh['grp'=64,'own'=8] {'own'}, dimensions={0} | all-to-all | bytes 131072 | tf_op jit(solution)/shard_map/all_to_all | solution.py:391
  138.3 0.0 copy-done.1
  138.3 1.4 last.1
Async XLA Ops:
  2.4 33.1 %all-to-all-start = ((bf16[64,4,128]{2,1,0:T(4,128)(2,1)}), bf16[64,4,128]{2,1,0:T(4,128)(2,1)S(1)}, u32[]{:S(2)}, u32[]{:S(2)}) async-start(bf16[64,4,128]{2,1,0:T(4,128)(2,1)} %bitcast.3), calls=%async_computation | async-start | bytes 131072 | tf_op jit(solution)/shard_map/all_to_all | solution.py:359
  35.6 14.0 %copy-start.3 = (bf16[4,16,256]{2,1,0:T(8,128)(2,1)S(1)}, bf16[4,16,256]{2,1,0:T(8,128)(2,1)}, u32[]{:S(2)}) copy-start(bf16[4,16,256]{2,1,0:T(8,128)(2,1)} %param.15) | copy-start | bytes 98308
  35.6 14.0 %copy-start.4 = (bf16[4,16,256]{2,1,0:T(8,128)(2,1)S(1)}, bf16[4,16,256]{2,1,0:T(8,128)(2,1)}, u32[]{:S(2)}) copy-start(bf16[4,16,256]{2,1,0:T(8,128)(2,1)} %param.16) | copy-start | bytes 98308
  38.2 30.0 %copy-start = (bf16[2,256,256]{2,1,0:T(8,128)(2,1)S(1)}, bf16[2,256,256]{2,1,0:T(8,128)(2,1)}, u32[]{:S(2)}) copy-start(bf16[2,256,256]{2,1,0:T(8,128)(2,1)} %near_ref.5) | copy-start | bytes 786436
  38.2 30.0 %copy-start.2 = (bf16[4,16,256]{2,1,0:T(8,128)(2,1)S(1)}, bf16[4,16,256]{2,1,0:T(8,128)(2,1)}, u32[]{:S(2)}) copy-start(bf16[4,16,256]{2,1,0:T(8,128)(2,1)} %exc_ref.5) | copy-start | bytes 98308
  109.5 28.8 %copy-start.1 = (f32[16,16,256]{2,1,0:T(8,128)S(1)}, f32[16,16,256]{2,1,0:T(8,128)}, u32[]{:S(2)}) copy-start(f32[16,16,256]{2,1,0:T(8,128)} %state_ref.1) | copy-start | bytes 786436

commit v5 on v4

--- a/solution.py
+++ b/solution.py
@@ -13,6 +13,7 @@
 BF16 = jnp.bfloat16
 I32 = jnp.int32
 LANES = 128
+FAR_PIECES = 4
 CONTRACT_LAST = (((1,), (1,)), ((), ()))
 VMEM = pl.BlockSpec(memory_space=pltpu.VMEM)
 HBM = pl.BlockSpec(memory_space=pltpu.HBM)
@@ -77,10 +78,12 @@
 
 def tables_kernel(
     pole_hbm, residue_hbm, reader_hbm, src_hbm, delay_hbm, state_hbm, far_hbm,
-    hits_ref, split_ref, near_pick_ref, tail_ref, coef_ref, far_ref,
-    pole_ref, residue_ref, reader_ref, src_ref, delay_ref, state_ref, sem,
+    hits_ref, split_ref, near_pick_ref, tail_ref, coef_ref, *rest,
 ):
-    reader_copy, src_copy, delay_copy, pole_copy, residue_copy, state_copy, far_copy = fetch(
+    turned = rest[:FAR_PIECES]
+    pole_ref, residue_ref, reader_ref, src_ref, delay_ref, state_ref, far_ref, sem = rest[FAR_PIECES:]
+    size = far_ref.shape[0] // FAR_PIECES
+    copies = fetch(
         sem,
         (reader_hbm, reader_ref),
         (src_hbm, src_ref),
@@ -88,8 +91,12 @@
         (pole_hbm, pole_ref),
         (residue_hbm, residue_ref),
         (state_hbm, state_ref),
-        (far_hbm, far_ref),
+        *(
+            (far_hbm.at[pl.ds(n * size, size)], far_ref.at[pl.ds(n * size, size)])
+            for n in range(FAR_PIECES)
+        ),
     )
+    reader_copy, src_copy, delay_copy, pole_copy, residue_copy, state_copy = copies[:6]
     cap, classes, groups = reader_ref.shape
     slots = cap * groups
     group_tiles = hits_ref.shape[0]
@@ -140,14 +147,20 @@
             tail_ref[n] = tail
     for p in range(count):
         coef_ref[8 + p : 9 + p, :] = jnp.full((1, width), pole_ref[p], F32)
-    far_copy.wait()
-
-
-def far_terms(entries, far_ref, terms_ref, first, last):
+    for n in range(FAR_PIECES):
+        copies[6 + n].wait()
+        for k in range(size):
+            turned[n][k] = far_ref[n * size + k].T
+
+
+def far_terms(entries, turned, terms_ref):
     slots = entries.shape[0]
-    for k in range(first, last):
-        terms = lax.dot_general(entries, far_ref[k], CONTRACT_LAST, preferred_element_type=F32)
-        terms_ref[pl.ds(k * slots, slots), :] = terms.astype(BF16)
+    at = 0
+    for piece in turned:
+        for k in range(piece.shape[0]):
+            terms = lax.dot(entries, piece[k], preferred_element_type=F32)
+            terms_ref[pl.ds(at, slots), :] = terms.astype(BF16)
+            at += slots
 
 
 def entries_of(in_ref, split_ref):
@@ -179,35 +192,31 @@
     return base
 
 
-def far_first_kernel(
-    in_ref, split_ref, far_ref, hits_ref, near_pick_ref, cur_hbm, near_hbm, exc_hbm,
-    inverse_hbm, part_ref, base_ref, inverse_ref, terms_ref, cur_ref, near_ref, exc_ref, sem,
-):
+def far_first_kernel(in_ref, split_ref, hits_ref, near_pick_ref, *rest):
+    turned = rest[:FAR_PIECES]
+    cur_hbm, near_hbm, exc_hbm, part_ref, base_ref = rest[FAR_PIECES : FAR_PIECES + 5]
+    terms_ref, cur_ref, near_ref, exc_ref, sem = rest[FAR_PIECES + 5 :]
     copies = fetch(sem, (cur_hbm, cur_ref), (near_hbm, near_ref), (exc_hbm, exc_ref))
-    inverse_copy = pltpu.make_async_copy(inverse_hbm, inverse_ref, sem.at[len(copies)])
-    inverse_copy.start()
-    far_terms(entries_of(in_ref, split_ref), far_ref, terms_ref, 0, far_ref.shape[0])
+    far_terms(entries_of(in_ref, split_ref), turned, terms_ref)
     for copy in copies:
         copy.wait()
     base_ref[...] = near_base(0, near_pick_ref, cur_ref, near_ref, exc_ref)
     part_ref[...] = lax.dot(
         hits_ref[...], terms_ref[...], preferred_element_type=F32
     ).astype(BF16)
-    inverse_copy.wait()
-
-
-def far_kernel(
-    step, in_ref, split_ref, far_ref, hits_ref, near_pick_ref, cur_ref, near_ref, exc_ref,
-    part_ref, base_ref, terms_ref,
-):
-    far_terms(entries_of(in_ref, split_ref), far_ref, terms_ref, 0, far_ref.shape[0])
+
+
+def far_kernel(step, in_ref, split_ref, hits_ref, near_pick_ref, *rest):
+    turned = rest[:FAR_PIECES]
+    cur_ref, near_ref, exc_ref, part_ref, base_ref, terms_ref = rest[FAR_PIECES:]
+    far_terms(entries_of(in_ref, split_ref), turned, terms_ref)
     base_ref[...] = near_base(step, near_pick_ref, cur_ref, near_ref, exc_ref)
     part_ref[...] = lax.dot(
         hits_ref[...], terms_ref[...], preferred_element_type=F32
     ).astype(BF16)
 
 
-def solve(parts_ref, base_ref, inverse_ref):
+def solve(parts_ref, base_ref, inverse_ref, turned_ref=None):
     far_field = parts_ref[0].astype(F32)
     for o in range(1, parts_ref.shape[0]):
         far_field = far_field + parts_ref[o].astype(F32)
@@ -216,21 +225,21 @@
     row = lax.broadcasted_iota(I32, right_side.shape, 0)
     current = jnp.zeros(right_side.shape, F32)
     for t in range(tiles):
+        turned = inverse_ref[t]
+        if turned_ref is not None:
+            turned = turned.T
+            turned_ref[t] = turned
         current = jnp.where(
-            row == t,
-            lax.dot_general(
-                right_side, inverse_ref[t], CONTRACT_LAST, preferred_element_type=F32
-            ),
-            current,
+            row == t, lax.dot(right_side, turned, preferred_element_type=F32), current
         )
     return current.astype(BF16)
 
 
 def step_kernel(
     step, coef_ref, parts_ref, base_ref, inverse_ref, tail_ref, cur_ref, ret_ref, pick_ref,
-    cur_out, send_ref, ret_out=None,
+    cur_out, send_ref, ret_out=None, turned_ref=None,
 ):
-    current = solve(parts_ref, base_ref, inverse_ref)
+    current = solve(parts_ref, base_ref, inverse_ref, turned_ref)
     tiles = current.shape[0]
     wide = current.astype(F32)
     retarded = wide * (1.0 + coef_ref[0:1, :]) + tail_ref[step]
@@ -322,7 +331,7 @@
 
     sources = near_src.shape[0] * near_src.shape[2]
     poles_count = poles.shape[0]
-    reader_hits, split, near_pick, tail, coef, far_kept = call(
+    reader_hits, split, near_pick, tail, coef, *turned = call(
         tables_kernel,
         "tables",
         (
@@ -331,7 +340,7 @@
             shape((sources * tiles, past), BF16),
             shape((STEPS - 1, tiles, width), F32),
             shape((8 + poles_count, width), F32),
-            shape(far_mats.shape, BF16),
+            *[shape((classes // FAR_PIECES, width, width), BF16)] * FAR_PIECES,
         ),
         [HBM] * 7,
         [
@@ -341,7 +350,8 @@
             pltpu.VMEM((sources, tiles), I32),
             pltpu.VMEM((sources, tiles), I32),
             pltpu.VMEM(pole_state.shape, F32),
-            pltpu.SemaphoreType.DMA((7,)),
+            pltpu.VMEM(far_mats.shape, BF16),
+            pltpu.SemaphoreType.DMA((6 + FAR_PIECES,)),
         ],
     )(
         in_hbm(poles),
@@ -354,40 +364,43 @@
     )
 
     current = cur_hist.reshape(past, width)
+    inverse = self_inverse
     retarded = history
     for step in range(STEPS):
         incoming = lax.all_to_all(
             outgoing.reshape(groups, 2 * cap, LANES), "grp", split_axis=0, concat_axis=0, tiled=True
         ).reshape(2 * slots, LANES)
         if step == 0:
-            incoming, tail, coef, reader_hits, near_pick, split, far_kept = (
+            incoming, tail, coef, reader_hits, near_pick, split, *turned = (
                 lax.optimization_barrier(
-                    (incoming, tail, coef, reader_hits, near_pick, split, far_kept)
+                    (incoming, tail, coef, reader_hits, near_pick, split, *turned)
                 )
             )
         outs = (shape((group_tiles, width), BF16), shape((tiles, width), F32))
         terms = pltpu.VMEM((classes * slots, width), BF16)
+        kept = (incoming, split, reader_hits, near_pick, *turned)
         if step == 0:
-            part, base, inverse = call(
+            part, base = call(
                 far_first_kernel,
                 "far",
-                outs + (shape(self_inverse.shape, BF16),),
-                [VMEM] * 5 + [HBM] * 4,
+                outs,
+                [VMEM] * len(kept) + [HBM] * 3,
                 [
                     terms,
                     pltpu.VMEM((past, width), BF16),
                     pltpu.VMEM(near_mats.shape, BF16),
                     pltpu.VMEM(excitation.shape, BF16),
-                    pltpu.SemaphoreType.DMA((4,)),
+                    pltpu.SemaphoreType.DMA((3,)),
                 ],
-            )(
-                incoming, split, far_kept, reader_hits, near_pick, in_hbm(current),
-                in_hbm(near_mats), in_hbm(excitation), in_hbm(self_inverse),
-            )
+            )(*kept, in_hbm(current), in_hbm(near_mats), in_hbm(excitation))
         else:
             part, base = call(
-                functools.partial(far_kernel, step), "far", outs, [VMEM] * 8, [terms]
-            )(incoming, split, far_kept, reader_hits, near_pick, current, near_mats, excitation)
+                functools.partial(far_kernel, step),
+                "far",
+                outs,
+                [VMEM] * (len(kept) + 3),
+                [terms],
+            )(*kept, current, near_mats, excitation)
         parts = lax.all_to_all(
             part.reshape(owners, tiles, width), "own", split_axis=0, concat_axis=0, tiled=True
         )
@@ -395,11 +408,16 @@
             outs = (shape((past, width), BF16), shape((2 * slots, LANES), BF16))
             if step + 2 < STEPS:
                 outs = outs + (shape((past, width), BF16),)
-            made = call(
-                functools.partial(step_kernel, step), "step", outs, [VMEM] * 8
-            )(coef, parts, base, inverse, tail, current, retarded, pick)
+            if step == 0:
+                outs = outs + (shape(self_inverse.shape, BF16),)
+            made = call(functools.partial(step_kernel, step), "step", outs, [VMEM] * 8)(
+                coef, parts, base, inverse, tail, current, retarded, pick
+            )
             current, outgoing = made[:2]
-            retarded = made[-1]
+            if step + 2 < STEPS:
+                retarded = made[2]
+            if step == 0:
+                inverse = made[3]
     return call(
         last_kernel,
         "last",

time: 140 us -> 137 us (0.979)
  Pallas kernels: 14.3 us -> 11.5 us
    pallas_call x4, Pallas kernels: 6.88 us -> 4.53 us  [the longest x3 2.48 us: body(): call(functools.partial(far_kernel, step), 'far', outs, [VMEM] * (len(kept...]
  transfers between devices with their start and end apart: 1 -> 1, of which waited for: 1 -> 1; matrix products, arithmetic and copies ran while one was open for 0% -> 0% of each run, Pallas kernels for 1% -> 2%
where the time goes in v5:
time: 137 us
  blocking collectives  93.3 us (68%)
  starting transfers between devices  19.1 us (14%)
  waiting for transfers between devices  11.9 us (9%)
  Pallas kernels  11.5 us (8%)
    all_to_all x3, blocking collectives, body(): lax.all_to_all(outgoing.reshape(groups, 2 * cap, LANES), 'grp', split_axi...  53.6 us
    all_to_all x4, blocking collectives, body(): lax.all_to_all(part.reshape(owners, tiles, width), 'own', split_axis=0, c...  39.8 us
    all_to_all x1, starting transfers between devices, body(): lax.all_to_all(outgoing.reshape(groups, 2 * cap, LANES), 'grp', split_axi...  19.1 us
    all_to_all x1, waiting for transfers between devices, body(): lax.all_to_all(outgoing.reshape(groups, 2 * cap, LANES), 'grp', split_axi...  11.9 us
  transfers between devices with their start and end apart: 1, of which 1 were waited for; matrix products, arithmetic and copies ran while one was open for 0% of the time, Pallas kernels for 2%

profile of v5, /device:TPU:1, one launch (start us, length us, event | category | flops | bytes accessed | tf_op | source)
XLA Modules:
  0.0 136.6 jit_solution(16340109899249994868)
XLA Ops:
  0.6 1.8 %first.1 = (bf16[256,128]{1,0:T(8,128)(2,1)S(1)}, bf16[256,128]{1,0:T(8,128)(2,1)}) custom-call(s32[4,16]{1,0:T(4,128)} %bitcast.41, s32[4,16]{1,0:T(4,128)} %bitcast.42, bf16[64,256]{1,0:T(8,128)(2,1)} %bitcast.31), custom_call_target="tpu_custom_call" | custom-call | tf_op jit(solution)/shard_map/first/pallas_call | solution.py:319
  2.4 19.1 %all-to-all-start = ((bf16[64,4,128]{2,1,0:T(4,128)(2,1)}), bf16[64,4,128]{2,1,0:T(4,128)(2,1)S(1)}, u32[]{:S(2)}, u32[]{:S(2)}) async-start(bf16[64,4,128]{2,1,0:T(4,128)(2,1)} %bitcast.3), calls=%async_computation | async-start | bytes 131072 | tf_op jit(solution)/shard_map/all_to_all | solution.py:370
  21.6 2.1 %tables.1 = (bf16[128,2048]{1,0:T(8,128)(2,1)S(1)}, bf16[2,128,256]{2,1,0:T(8,128)(2,1)S(1)}, bf16[64,64]{1,0:T(8,128)(2,1)S(1)}, f32[3,16,256]{2,1,0:T(8,128)S(...) custom-call(f32[16]{0:T(128)} %pole_hbm.1, ...), custom_call_target="tpu_custom_call" | custom-call | tf_op jit(solution)/shard_map/tables/pallas_call | solution.py:334
  23.7 0.0 copy-start.4
  23.7 0.0 copy-start.5
  23.7 11.9 %all-to-all-done = bf16[64,4,128]{2,1,0:T(4,128)(2,1)S(1)} async-done(((bf16[64,4,128]{2,1,0:T(4,128)(2,1)}), bf16[64,4,128]{2,1,0:T(4,128)(2,1)S(1)}, u32[]{:S(2)}, u32[]{:S(2)}) %all-to-all-start) | async-done | bytes 65568 | tf_op jit(solution)/shard_map/all_to_all | solution.py:370
  35.6 0.0 copy-start.1
  35.6 2.0 %far.4 = (bf16[128,256]{1,0:T(8,128)(2,1)S(1)}, f32[16,256]{1,0:T(8,128)S(1)}) custom-call(bf16[256,128]{1,0:T(8,128)(2,1)S(1)} %bitcast.25, bf16[2,128,256]{2,1,0:T(8,128)(2,1)S(1)} %get-tuple-element.52.split_ref, bf16[128,2048]{1,0:T(8,128)(2,1)S(1)} %get-tuple-element.53.hits_ref, bf16[64,64]{1,0:T(8,128)(2,1)S(1)} %get-tuple-element.54.near_pick_ref, ...), custom_call_target="tpu_custom_call" | custom-call | tf_op jit(solution)/shard_map/far/pallas_call | solution.py:383
  37.6 0.0 copy-start
  37.6 0.0 copy-start.3
  37.7 11.4 %all_to_all.40.parts_ref = bf16[8,16,256]{2,1,0:T(8,128)(2,1)S(1)} all-to-all(bf16[8,16,256]{2,1,0:T(8,128)(2,1)S(1)} %bitcast.37), channel_id=1, replica_groups=mesh['grp'=64,'own'=8] {'own'}, dimensions={0} | all-to-all | bytes 131072 | tf_op jit(solution)/shard_map/all_to_all | solution.py:404
  49.1 0.0 copy-done.4
  49.1 0.0 copy-done.5
  49.1 0.0 copy-done.1
  49.1 0.9 step.3
  49.9 17.8 %all_to_all.41 = bf16[64,4,128]{2,1,0:T(4,128)(2,1)S(1)} all-to-all(bf16[64,4,128]{2,1,0:T(4,128)(2,1)S(1)} %bitcast.36), channel_id=1, replica_groups=mesh['grp'=64,'own'=8] {'grp'}, dimensions={0} | all-to-all | bytes 131072 | tf_op jit(solution)/shard_map/all_to_all | solution.py:370
  67.7 0.0 copy-done
  67.7 0.0 copy-done.3
  67.7 0.8 far.5
  68.6 9.5 %all_to_all.42.parts_ref = bf16[8,16,256]{2,1,0:T(8,128)(2,1)S(1)} all-to-all(bf16[8,16,256]{2,1,0:T(8,128)(2,1)S(1)} %bitcast.38), channel_id=1, replica_groups=mesh['grp'=64,'own'=8] {'own'}, dimensions={0} | all-to-all | bytes 131072 | tf_op jit(solution)/shard_map/all_to_all | solution.py:404
  78.0 0.5 step.4
  78.6 17.8 %all_to_all.43 = bf16[64,4,128]{2,1,0:T(4,128)(2,1)S(1)} all-to-all(bf16[64,4,128]{2,1,0:T(4,128)(2,1)S(1)} %bitcast.35), channel_id=1, replica_groups=mesh['grp'=64,'own'=8] {'grp'}, dimensions={0} | all-to-all | bytes 131072 | tf_op jit(solution)/shard_map/all_to_all | solution.py:370
  96.4 0.8 far.6
  97.2 9.5 %all_to_all.44.parts_ref = bf16[8,16,256]{2,1,0:T(8,128)(2,1)S(1)} all-to-all(bf16[8,16,256]{2,1,0:T(8,128)(2,1)S(1)} %bitcast.39), channel_id=1, replica_groups=mesh['grp'=64,'own'=8] {'own'}, dimensions={0} | all-to-all | bytes 131072 | tf_op jit(solution)/shard_map/all_to_all | solution.py:404
  106.7 0.5 step.5
  107.2 0.0 copy-start.2
  107.2 17.9 %all_to_all.45 = bf16[64,4,128]{2,1,0:T(4,128)(2,1)S(1)} all-to-all(bf16[64,4,128]{2,1,0:T(4,128)(2,1)S(1)} %bitcast.34), channel_id=1, replica_groups=mesh['grp'=64,'own'=8] {'grp'}, dimensions={0} | all-to-all | bytes 131072 | tf_op jit(solution)/shard_map/all_to_all | solution.py:370
  125.2 0.8 far.7
  126.0 9.5 %all_to_all.46.parts_ref = bf16[8,16,256]{2,1,0:T(8,128)(2,1)S(1)} all-to-all(bf16[8,16,256]{2,1,0:T(8,128)(2,1)S(1)} %bitcast.33), channel_id=1, replica_groups=mesh['grp'=64,'own'=8] {'own'}, dimensions={0} | all-to-all | bytes 131072 | tf_op jit(solution)/shard_map/all_to_all | solution.py:404
  135.4 0.0 copy-done.2
  135.4 1.1 last.1
Async XLA Ops:
  2.4 33.1 %all-to-all-start = ((bf16[64,4,128]{2,1,0:T(4,128)(2,1)}), bf16[64,4,128]{2,1,0:T(4,128)(2,1)S(1)}, u32[]{:S(2)}, u32[]{:S(2)}) async-start(bf16[64,4,128]{2,1,0:T(4,128)(2,1)} %bitcast.3), calls=%async_computation | async-start | bytes 131072 | tf_op jit(solution)/shard_map/all_to_all | solution.py:370
  23.7 25.4 %copy-start.4 = (bf16[4,16,256]{2,1,0:T(8,128)(2,1)S(1)}, bf16[4,16,256]{2,1,0:T(8,128)(2,1)}, u32[]{:S(2)}) copy-start(bf16[4,16,256]{2,1,0:T(8,128)(2,1)} %param.15) | copy-start | bytes 98308
  23.7 25.4 %copy-start.5 = (bf16[4,16,256]{2,1,0:T(8,128)(2,1)S(1)}, bf16[4,16,256]{2,1,0:T(8,128)(2,1)}, u32[]{:S(2)}) copy-start(bf16[4,16,256]{2,1,0:T(8,128)(2,1)} %param.16) | copy-start | bytes 98308
  35.6 13.5 %copy-start.1 = (bf16[16,256,256]{2,1,0:T(8,128)(2,1)S(1)}, bf16[16,256,256]{2,1,0:T(8,128)(2,1)}, u32[]{:S(2)}) copy-start(bf16[16,256,256]{2,1,0:T(8,128)(2,1)} %inverse_ref.1) | copy-start | bytes 6291460
  37.6 30.1 %copy-start = (bf16[2,256,256]{2,1,0:T(8,128)(2,1)S(1)}, bf16[2,256,256]{2,1,0:T(8,128)(2,1)}, u32[]{:S(2)}) copy-start(bf16[2,256,256]{2,1,0:T(8,128)(2,1)} %rest_5_.7) | copy-start | bytes 786436
  37.6 30.1 %copy-start.3 = (bf16[4,16,256]{2,1,0:T(8,128)(2,1)S(1)}, bf16[4,16,256]{2,1,0:T(8,128)(2,1)}, u32[]{:S(2)}) copy-start(bf16[4,16,256]{2,1,0:T(8,128)(2,1)} %rest_6_.7) | copy-start | bytes 98308
  107.2 28.2 %copy-start.2 = (f32[16,16,256]{2,1,0:T(8,128)S(1)}, f32[16,16,256]{2,1,0:T(8,128)}, u32[]{:S(2)}) copy-start(f32[16,16,256]{2,1,0:T(8,128)} %state_ref.1) | copy-start | bytes 786436

commit v6 on v5

--- a/solution.py
+++ b/solution.py
@@ -78,10 +78,12 @@
 
 def tables_kernel(
     pole_hbm, residue_hbm, reader_hbm, src_hbm, delay_hbm, state_hbm, far_hbm,
-    hits_ref, split_ref, near_pick_ref, tail_ref, coef_ref, *rest,
+    cur_hbm, near_hbm, exc_hbm, hits_ref, split_ref, near_pick_ref, tail_ref, coef_ref, base_ref,
+    *rest,
 ):
     turned = rest[:FAR_PIECES]
-    pole_ref, residue_ref, reader_ref, src_ref, delay_ref, state_ref, far_ref, sem = rest[FAR_PIECES:]
+    pole_ref, residue_ref, reader_ref, src_ref, delay_ref, state_ref = rest[FAR_PIECES:][:6]
+    far_ref, cur_ref, near_ref, exc_ref, sem = rest[FAR_PIECES + 6 :]
     size = far_ref.shape[0] // FAR_PIECES
     copies = fetch(
         sem,
@@ -91,6 +93,9 @@
         (pole_hbm, pole_ref),
         (residue_hbm, residue_ref),
         (state_hbm, state_ref),
+        (cur_hbm, cur_ref),
+        (near_hbm, near_ref),
+        (exc_hbm, exc_ref),
         *(
             (far_hbm.at[pl.ds(n * size, size)], far_ref.at[pl.ds(n * size, size)])
             for n in range(FAR_PIECES)
@@ -147,8 +152,11 @@
             tail_ref[n] = tail
     for p in range(count):
         coef_ref[8 + p : 9 + p, :] = jnp.full((1, width), pole_ref[p], F32)
+    for n in range(6, 9):
+        copies[n].wait()
+    base_ref[...] = near_base(0, near_pick_ref, cur_ref, near_ref, exc_ref)
     for n in range(FAR_PIECES):
-        copies[6 + n].wait()
+        copies[9 + n].wait()
         for k in range(size):
             turned[n][k] = far_ref[n * size + k].T
 
@@ -192,23 +200,16 @@
     return base
 
 
-def far_first_kernel(in_ref, split_ref, hits_ref, near_pick_ref, *rest):
-    turned = rest[:FAR_PIECES]
-    cur_hbm, near_hbm, exc_hbm, part_ref, base_ref = rest[FAR_PIECES : FAR_PIECES + 5]
-    terms_ref, cur_ref, near_ref, exc_ref, sem = rest[FAR_PIECES + 5 :]
-    copies = fetch(sem, (cur_hbm, cur_ref), (near_hbm, near_ref), (exc_hbm, exc_ref))
+def far_first_kernel(in_ref, split_ref, hits_ref, *rest):
+    *turned, part_ref, terms_ref = rest
     far_terms(entries_of(in_ref, split_ref), turned, terms_ref)
-    for copy in copies:
-        copy.wait()
-    base_ref[...] = near_base(0, near_pick_ref, cur_ref, near_ref, exc_ref)
     part_ref[...] = lax.dot(
         hits_ref[...], terms_ref[...], preferred_element_type=F32
     ).astype(BF16)
 
 
-def far_kernel(step, in_ref, split_ref, hits_ref, near_pick_ref, *rest):
-    turned = rest[:FAR_PIECES]
-    cur_ref, near_ref, exc_ref, part_ref, base_ref, terms_ref = rest[FAR_PIECES:]
+def far_kernel(step, in_ref, split_ref, hits_ref, *rest):
+    *turned, near_pick_ref, cur_ref, near_ref, exc_ref, part_ref, base_ref, terms_ref = rest
     far_terms(entries_of(in_ref, split_ref), turned, terms_ref)
     base_ref[...] = near_base(step, near_pick_ref, cur_ref, near_ref, exc_ref)
     part_ref[...] = lax.dot(
@@ -329,9 +330,10 @@
         ],
     )(in_hbm(far_dest.T), in_hbm(far_delay.T), in_hbm(history))
 
+    current = cur_hist.reshape(past, width)
     sources = near_src.shape[0] * near_src.shape[2]
     poles_count = poles.shape[0]
-    reader_hits, split, near_pick, tail, coef, *turned = call(
+    reader_hits, split, near_pick, tail, coef, base, *turned = call(
         tables_kernel,
         "tables",
         (
@@ -340,9 +342,10 @@
             shape((sources * tiles, past), BF16),
             shape((STEPS - 1, tiles, width), F32),
             shape((8 + poles_count, width), F32),
+            shape((tiles, width), F32),
             *[shape((classes // FAR_PIECES, width, width), BF16)] * FAR_PIECES,
         ),
-        [HBM] * 7,
+        [HBM] * 10,
         [
             pltpu.SMEM((poles_count,), F32),
             pltpu.SMEM((poles_count,), F32),
@@ -351,7 +354,10 @@
             pltpu.VMEM((sources, tiles), I32),
             pltpu.VMEM(pole_state.shape, F32),
             pltpu.VMEM(far_mats.shape, BF16),
-            pltpu.SemaphoreType.DMA((6 + FAR_PIECES,)),
+            pltpu.VMEM((past, width), BF16),
+            pltpu.VMEM(near_mats.shape, BF16),
+            pltpu.VMEM(excitation.shape, BF16),
+            pltpu.SemaphoreType.DMA((9 + FAR_PIECES,)),
         ],
     )(
         in_hbm(poles),
@@ -361,9 +367,11 @@
         in_hbm(near_delay.transpose(0, 2, 1).reshape(sources, tiles)),
         in_hbm(pole_state),
         in_hbm(far_mats),
+        in_hbm(current),
+        in_hbm(near_mats),
+        in_hbm(excitation),
     )
 
-    current = cur_hist.reshape(past, width)
     inverse = self_inverse
     retarded = history
     for step in range(STEPS):
@@ -371,36 +379,24 @@
             outgoing.reshape(groups, 2 * cap, LANES), "grp", split_axis=0, concat_axis=0, tiled=True
         ).reshape(2 * slots, LANES)
         if step == 0:
-            incoming, tail, coef, reader_hits, near_pick, split, *turned = (
+            incoming, tail, coef, base, reader_hits, near_pick, split, *turned = (
                 lax.optimization_barrier(
-                    (incoming, tail, coef, reader_hits, near_pick, split, *turned)
+                    (incoming, tail, coef, base, reader_hits, near_pick, split, *turned)
                 )
             )
-        outs = (shape((group_tiles, width), BF16), shape((tiles, width), F32))
+        sums = shape((group_tiles, width), BF16)
         terms = pltpu.VMEM((classes * slots, width), BF16)
-        kept = (incoming, split, reader_hits, near_pick, *turned)
+        kept = (incoming, split, reader_hits, *turned)
         if step == 0:
-            part, base = call(
-                far_first_kernel,
-                "far",
-                outs,
-                [VMEM] * len(kept) + [HBM] * 3,
-                [
-                    terms,
-                    pltpu.VMEM((past, width), BF16),
-                    pltpu.VMEM(near_mats.shape, BF16),
-                    pltpu.VMEM(excitation.shape, BF16),
-                    pltpu.SemaphoreType.DMA((3,)),
-                ],
-            )(*kept, in_hbm(current), in_hbm(near_mats), in_hbm(excitation))
+            part = call(far_first_kernel, "far", sums, [VMEM] * len(kept), [terms])(*kept)
         else:
             part, base = call(
                 functools.partial(far_kernel, step),
                 "far",
-                outs,
-                [VMEM] * (len(kept) + 3),
+                (sums, shape((tiles, width), F32)),
+                [VMEM] * (len(kept) + 4),
                 [terms],
-            )(*kept, current, near_mats, excitation)
+            )(*kept, near_pick, current, near_mats, excitation)
         parts = lax.all_to_all(
             part.reshape(owners, tiles, width), "own", split_axis=0, concat_axis=0, tiled=True
         )

time: 137 us -> 136 us (level)
  no operation moved by 1% of the time
where the time goes in v6:
time: 136 us; the launch traced here: 135 us
  blocking collectives  93.2 us (69%)
  starting transfers between devices  19.1 us (14%)
  waiting for transfers between devices  11.6 us (9%)
  Pallas kernels  10.6 us (8%)
    all_to_all x3, blocking collectives, body(): lax.all_to_all(outgoing.reshape(groups, 2 * cap, LANES), 'grp', split_axi...  53.6 us
    all_to_all x4, blocking collectives, body(): lax.all_to_all(part.reshape(owners, tiles, width), 'own', split_axis=0, c...  39.6 us
    all_to_all x1, starting transfers between devices, body(): lax.all_to_all(outgoing.reshape(groups, 2 * cap, LANES), 'grp', split_axi...  19.1 us
    all_to_all x1, waiting for transfers between devices, body(): lax.all_to_all(outgoing.reshape(groups, 2 * cap, LANES), 'grp', split_axi...  11.6 us
  transfers between devices with their start and end apart: 1, of which 1 were waited for; matrix products, arithmetic and copies ran while one was open for 0% of the time, Pallas kernels for 2%

profile of v6, /device:TPU:1, one launch (start us, length us, event | category | flops | bytes accessed | tf_op | source)
XLA Modules:
  0.0 135.2 jit_solution(13429353593087029556)
XLA Ops:
  0.6 1.8 %first.1 = (bf16[256,128]{1,0:T(8,128)(2,1)S(1)}, bf16[256,128]{1,0:T(8,128)(2,1)}) custom-call(s32[4,16]{1,0:T(4,128)} %bitcast.43, s32[4,16]{1,0:T(4,128)} %bitcast.44, bf16[64,256]{1,0:T(8,128)(2,1)} %bitcast.32), custom_call_target="tpu_custom_call" | custom-call | tf_op jit(solution)/shard_map/first/pallas_call | solution.py:320
  2.4 19.1 %all-to-all-start = ((bf16[64,4,128]{2,1,0:T(4,128)(2,1)}), bf16[64,4,128]{2,1,0:T(4,128)(2,1)S(1)}, u32[]{:S(2)}, u32[]{:S(2)}) async-start(bf16[64,4,128]{2,1,0:T(4,128)(2,1)} %bitcast.3), calls=%async_computation | async-start | bytes 131072 | tf_op jit(solution)/shard_map/all_to_all | solution.py:378
  21.6 2.4 %tables.1 = (bf16[128,2048]{1,0:T(8,128)(2,1)S(1)}, bf16[2,128,256]{2,1,0:T(8,128)(2,1)S(1)}, bf16[64,64]{1,0:T(8,128)(2,1)S(1)}, f32[3,16,256]{2,1,0:T(8,128)S(...) custom-call(f32[16]{0:T(128)} %pole_hbm.1, ...), custom_call_target="tpu_custom_call" | custom-call | tf_op jit(solution)/shard_map/tables/pallas_call | solution.py:336
  24.0 0.0 copy-start.4
  24.0 0.0 copy-start.5
  24.0 11.6 %all-to-all-done = bf16[64,4,128]{2,1,0:T(4,128)(2,1)S(1)} async-done(((bf16[64,4,128]{2,1,0:T(4,128)(2,1)}), bf16[64,4,128]{2,1,0:T(4,128)(2,1)S(1)}, u32[]{:S(2)}, u32[]{:S(2)}) %all-to-all-start) | async-done | bytes 65568 | tf_op jit(solution)/shard_map/all_to_all | solution.py:378
  35.6 0.0 copy-start.1
  35.6 0.0 copy-start
  35.6 0.0 copy-start.3
  35.6 0.8 far.4
  36.4 11.3 %all_to_all.40.parts_ref = bf16[8,16,256]{2,1,0:T(8,128)(2,1)S(1)} all-to-all(bf16[8,16,256]{2,1,0:T(8,128)(2,1)S(1)} %bitcast.29), channel_id=1, replica_groups=mesh['grp'=64,'own'=8] {'own'}, dimensions={0} | all-to-all | bytes 131072 | tf_op jit(solution)/shard_map/all_to_all | solution.py:400
  47.7 0.0 copy-done.4
  47.7 0.0 copy-done.5
  47.7 0.0 copy-done.1
  47.7 0.9 step.3
  48.6 17.8 %all_to_all.41 = bf16[64,4,128]{2,1,0:T(4,128)(2,1)S(1)} all-to-all(bf16[64,4,128]{2,1,0:T(4,128)(2,1)S(1)} %bitcast.37), channel_id=1, replica_groups=mesh['grp'=64,'own'=8] {'grp'}, dimensions={0} | all-to-all | bytes 131072 | tf_op jit(solution)/shard_map/all_to_all | solution.py:378
  66.4 0.0 copy-done
  66.4 0.0 copy-done.3
  66.4 0.8 far.5
  67.2 9.5 %all_to_all.42.parts_ref = bf16[8,16,256]{2,1,0:T(8,128)(2,1)S(1)} all-to-all(bf16[8,16,256]{2,1,0:T(8,128)(2,1)S(1)} %bitcast.38), channel_id=1, replica_groups=mesh['grp'=64,'own'=8] {'own'}, dimensions={0} | all-to-all | bytes 131072 | tf_op jit(solution)/shard_map/all_to_all | solution.py:400
  76.7 0.5 step.4
  77.2 17.8 %all_to_all.43 = bf16[64,4,128]{2,1,0:T(4,128)(2,1)S(1)} all-to-all(bf16[64,4,128]{2,1,0:T(4,128)(2,1)S(1)} %bitcast.36), channel_id=1, replica_groups=mesh['grp'=64,'own'=8] {'grp'}, dimensions={0} | all-to-all | bytes 131072 | tf_op jit(solution)/shard_map/all_to_all | solution.py:378
  95.0 0.8 far.6
  95.8 9.5 %all_to_all.44.parts_ref = bf16[8,16,256]{2,1,0:T(8,128)(2,1)S(1)} all-to-all(bf16[8,16,256]{2,1,0:T(8,128)(2,1)S(1)} %bitcast.39), channel_id=1, replica_groups=mesh['grp'=64,'own'=8] {'own'}, dimensions={0} | all-to-all | bytes 131072 | tf_op jit(solution)/shard_map/all_to_all | solution.py:400
  105.3 0.5 step.5
  105.8 0.0 copy-start.2
  105.9 17.9 %all_to_all.45 = bf16[64,4,128]{2,1,0:T(4,128)(2,1)S(1)} all-to-all(bf16[64,4,128]{2,1,0:T(4,128)(2,1)S(1)} %bitcast.35), channel_id=1, replica_groups=mesh['grp'=64,'own'=8] {'grp'}, dimensions={0} | all-to-all | bytes 131072 | tf_op jit(solution)/shard_map/all_to_all | solution.py:378
  123.8 0.8 far.7
  124.6 9.5 %all_to_all.46.parts_ref = bf16[8,16,256]{2,1,0:T(8,128)(2,1)S(1)} all-to-all(bf16[8,16,256]{2,1,0:T(8,128)(2,1)S(1)} %bitcast.34), channel_id=1, replica_groups=mesh['grp'=64,'own'=8] {'own'}, dimensions={0} | all-to-all | bytes 131072 | tf_op jit(solution)/shard_map/all_to_all | solution.py:400
  134.1 0.0 copy-done.2
  134.1 1.1 last.1
Async XLA Ops:
  2.4 33.1 %all-to-all-start = ((bf16[64,4,128]{2,1,0:T(4,128)(2,1)}), bf16[64,4,128]{2,1,0:T(4,128)(2,1)S(1)}, u32[]{:S(2)}, u32[]{:S(2)}) async-start(bf16[64,4,128]{2,1,0:T(4,128)(2,1)} %bitcast.3), calls=%async_computation | async-start | bytes 131072 | tf_op jit(solution)/shard_map/all_to_all | solution.py:378
  24.0 23.7 %copy-start.4 = (bf16[4,16,256]{2,1,0:T(8,128)(2,1)S(1)}, bf16[4,16,256]{2,1,0:T(8,128)(2,1)}, u32[]{:S(2)}) copy-start(bf16[4,16,256]{2,1,0:T(8,128)(2,1)} %param.15) | copy-start | bytes 98308
  24.0 23.7 %copy-start.5 = (bf16[4,16,256]{2,1,0:T(8,128)(2,1)S(1)}, bf16[4,16,256]{2,1,0:T(8,128)(2,1)}, u32[]{:S(2)}) copy-start(bf16[4,16,256]{2,1,0:T(8,128)(2,1)} %param.16) | copy-start | bytes 98308
  35.6 12.1 %copy-start.1 = (bf16[16,256,256]{2,1,0:T(8,128)(2,1)S(1)}, bf16[16,256,256]{2,1,0:T(8,128)(2,1)}, u32[]{:S(2)}) copy-start(bf16[16,256,256]{2,1,0:T(8,128)(2,1)} %inverse_ref.1) | copy-start | bytes 6291460
  35.6 30.8 %copy-start = (bf16[2,256,256]{2,1,0:T(8,128)(2,1)S(1)}, bf16[2,256,256]{2,1,0:T(8,128)(2,1)}, u32[]{:S(2)}) copy-start(bf16[2,256,256]{2,1,0:T(8,128)(2,1)} %rest_6_.5) | copy-start | bytes 786436
  35.6 30.8 %copy-start.3 = (bf16[4,16,256]{2,1,0:T(8,128)(2,1)S(1)}, bf16[4,16,256]{2,1,0:T(8,128)(2,1)}, u32[]{:S(2)}) copy-start(bf16[4,16,256]{2,1,0:T(8,128)(2,1)} %rest_7_.5) | copy-start | bytes 98308
  105.8 28.2 %copy-start.2 = (f32[16,16,256]{2,1,0:T(8,128)S(1)}, f32[16,16,256]{2,1,0:T(8,128)}, u32[]{:S(2)}) copy-start(f32[16,16,256]{2,1,0:T(8,128)} %state_ref.1) | copy-start | bytes 786436

commit v7 on v6

--- a/solution.py
+++ b/solution.py
@@ -14,6 +14,7 @@
 I32 = jnp.int32
 LANES = 128
 FAR_PIECES = 4
+OUT_PIECES = 2
 CONTRACT_LAST = (((1,), (1,)), ((), ()))
 VMEM = pl.BlockSpec(memory_space=pltpu.VMEM)
 HBM = pl.BlockSpec(memory_space=pltpu.HBM)
@@ -79,11 +80,11 @@
 def tables_kernel(
     pole_hbm, residue_hbm, reader_hbm, src_hbm, delay_hbm, state_hbm, far_hbm,
     cur_hbm, near_hbm, exc_hbm, hits_ref, split_ref, near_pick_ref, tail_ref, coef_ref, base_ref,
-    *rest,
+    near_ref, *rest,
 ):
     turned = rest[:FAR_PIECES]
     pole_ref, residue_ref, reader_ref, src_ref, delay_ref, state_ref = rest[FAR_PIECES:][:6]
-    far_ref, cur_ref, near_ref, exc_ref, sem = rest[FAR_PIECES + 6 :]
+    far_ref, cur_ref, near_in_ref, exc_ref, sem = rest[FAR_PIECES + 6 :]
     size = far_ref.shape[0] // FAR_PIECES
     copies = fetch(
         sem,
@@ -94,7 +95,7 @@
         (residue_hbm, residue_ref),
         (state_hbm, state_ref),
         (cur_hbm, cur_ref),
-        (near_hbm, near_ref),
+        (near_hbm, near_in_ref),
         (exc_hbm, exc_ref),
         *(
             (far_hbm.at[pl.ds(n * size, size)], far_ref.at[pl.ds(n * size, size)])
@@ -106,11 +107,13 @@
     slots = cap * groups
     group_tiles = hits_ref.shape[0]
     slot = lax.broadcasted_iota(I32, (slots, 1), 0)
-    row = lax.broadcasted_iota(I32, split_ref.shape[1:], 1)
+    row = lax.broadcasted_iota(I32, (slots, 2 * slots), 1)
     group_bits = groups.bit_length() - 1
     start = 4 * (slot & (groups - 1)) + shifted(slot, group_bits)
     for h in range(2):
-        split_ref[h] = jnp.where(row == start + 2 * h, 1.0, 0.0).astype(BF16)
+        split_ref[h * slots : (h + 1) * slots, :] = jnp.where(
+            row == start + 2 * h, 1.0, 0.0
+        ).astype(BF16)
     reader_copy.wait()
     readers = jnp.concatenate([reader_ref[c] for c in range(cap)], axis=1)
     place = lax.broadcasted_iota(I32, (group_tiles, slots), 0)
@@ -154,6 +157,8 @@
         coef_ref[8 + p : 9 + p, :] = jnp.full((1, width), pole_ref[p], F32)
     for n in range(6, 9):
         copies[n].wait()
+    for k in range(near_ref.shape[0]):
+        near_ref[k] = near_in_ref[k].T
     base_ref[...] = near_base(0, near_pick_ref, cur_ref, near_ref, exc_ref)
     for n in range(FAR_PIECES):
         copies[9 + n].wait()
@@ -172,14 +177,9 @@
 
 
 def entries_of(in_ref, split_ref):
-    incoming = in_ref[...]
-    return jnp.concatenate(
-        [
-            lax.dot(split_ref[h], incoming, preferred_element_type=F32).astype(BF16)
-            for h in range(2)
-        ],
-        axis=1,
-    )
+    halves = lax.dot(split_ref[...], in_ref[...], preferred_element_type=F32).astype(BF16)
+    slots = halves.shape[0] // 2
+    return jnp.concatenate([halves[:slots], halves[slots:]], axis=1)
 
 
 def near_base(step, near_pick_ref, cur_ref, near_ref, exc_ref):
@@ -189,10 +189,9 @@
     per_class = near_rows.shape[0] // classes
     base = exc_ref[step].astype(F32)
     for k in range(classes):
-        near = lax.dot_general(
+        near = lax.dot(
             near_rows[k * per_class : (k + 1) * per_class],
             near_ref[k],
-            CONTRACT_LAST,
             preferred_element_type=F32,
         )
         for m in range(per_class // tiles):
@@ -257,32 +256,46 @@
     ).astype(BF16)
 
 
-def last_kernel(coef_ref, parts_ref, base_ref, inverse_ref, cur_ref, state_ref, cur_out, state_out):
+def last_kernel(
+    coef_ref, parts_ref, base_ref, inverse_ref, cur_ref, state_ref, cur_out, state_out,
+    now_ref, made_ref, sem,
+):
+    tiles = now_ref.shape[0]
+    olds = [cur_ref.at[pl.ds((STEPS - 2 - n) * tiles, tiles)] for n in range(STEPS - 1)]
+    copies = fetch(sem, *((old, cur_out.at[n]) for n, old in enumerate(olds)))
     current = solve(parts_ref, base_ref, inverse_ref)
-    tiles = current.shape[0]
-    past = [cur_ref[pl.ds((STEPS - 2 - n) * tiles, tiles), :] for n in range(STEPS - 1)] + [current]
-    for n in range(STEPS):
-        cur_out[n] = past[n]
-    wide = [c.astype(F32) for c in past]
-    for p in range(state_ref.shape[0]):
-        pole = coef_ref[8 + p : 9 + p, :]
-        state = state_ref[p]
-        for n in range(STEPS):
-            state = pole * state + wide[n]
-        state_out[p] = state
+    now_ref[...] = current
+    copies.append(pltpu.make_async_copy(now_ref, cur_out.at[STEPS - 1], sem.at[STEPS - 1]))
+    copies[-1].start()
+    wide = [old[...].astype(F32) for old in olds] + [current.astype(F32)]
+    size = state_ref.shape[0] // OUT_PIECES
+    for piece in range(OUT_PIECES):
+        for p in range(piece * size, (piece + 1) * size):
+            pole = coef_ref[8 + p : 9 + p, :]
+            state = state_ref[p]
+            for n in range(STEPS):
+                state = pole * state + wide[n]
+            made_ref[p] = state
+        rows = pl.ds(piece * size, size)
+        copies.append(
+            pltpu.make_async_copy(made_ref.at[rows], state_out.at[rows], sem.at[STEPS + piece])
+        )
+        copies[-1].start()
+    for copy in copies:
+        copy.wait()
 
 
 def in_hbm(x):
     return pltpu.with_memory_space_constraint(x, pltpu.HBM)
 
 
-def call(kernel, name, outs, specs, scratch=()):
+def call(kernel, name, outs, specs, scratch=(), out_spec=VMEM):
     return pl.pallas_call(
         kernel,
         name=name,
         out_shape=outs,
         in_specs=specs,
-        out_specs=jax.tree.map(lambda _: VMEM, outs),
+        out_specs=jax.tree.map(lambda _: out_spec, outs),
         scratch_shapes=scratch,
         compiler_params=pltpu.CompilerParams(vmem_limit_bytes=8 << 20),
     )
@@ -333,16 +346,17 @@
     current = cur_hist.reshape(past, width)
     sources = near_src.shape[0] * near_src.shape[2]
     poles_count = poles.shape[0]
-    reader_hits, split, near_pick, tail, coef, base, *turned = call(
+    reader_hits, split, near_pick, tail, coef, base, near, *turned = call(
         tables_kernel,
         "tables",
         (
             shape((group_tiles, classes * slots), BF16),
-            shape((2, slots, 2 * slots), BF16),
+            shape((2 * slots, 2 * slots), BF16),
             shape((sources * tiles, past), BF16),
             shape((STEPS - 1, tiles, width), F32),
             shape((8 + poles_count, width), F32),
             shape((tiles, width), F32),
+            shape(near_mats.shape, BF16),
             *[shape((classes // FAR_PIECES, width, width), BF16)] * FAR_PIECES,
         ),
         [HBM] * 10,
@@ -379,9 +393,9 @@
             outgoing.reshape(groups, 2 * cap, LANES), "grp", split_axis=0, concat_axis=0, tiled=True
         ).reshape(2 * slots, LANES)
         if step == 0:
-            incoming, tail, coef, base, reader_hits, near_pick, split, *turned = (
+            incoming, tail, coef, base, near, reader_hits, near_pick, split, *turned = (
                 lax.optimization_barrier(
-                    (incoming, tail, coef, base, reader_hits, near_pick, split, *turned)
+                    (incoming, tail, coef, base, near, reader_hits, near_pick, split, *turned)
                 )
             )
         sums = shape((group_tiles, width), BF16)
@@ -396,7 +410,7 @@
                 (sums, shape((tiles, width), F32)),
                 [VMEM] * (len(kept) + 4),
                 [terms],
-            )(*kept, near_pick, current, near_mats, excitation)
+            )(*kept, near_pick, current, near, excitation)
         parts = lax.all_to_all(
             part.reshape(owners, tiles, width), "own", split_axis=0, concat_axis=0, tiled=True
         )
@@ -419,6 +433,12 @@
         "last",
         (shape((STEPS, tiles, width), BF16), shape(pole_state.shape, F32)),
         [VMEM] * 6,
+        [
+            pltpu.VMEM((tiles, width), BF16),
+            pltpu.VMEM(pole_state.shape, F32),
+            pltpu.SemaphoreType.DMA((STEPS + OUT_PIECES,)),
+        ],
+        HBM,
     )(coef, parts, base, inverse, current, pole_state)
 
 

time: 136 us -> 137 us (level)
  no operation moved by 1% of the time
where the time goes in v7:
time: 137 us; the launch traced here: 136 us
  blocking collectives  93.2 us (68%)
  starting transfers between devices  19.1 us (14%)
  waiting for transfers between devices  11.6 us (8%)
  Pallas kernels  11.5 us (8%)
    all_to_all x3, blocking collectives, body(): lax.all_to_all(outgoing.reshape(groups, 2 * cap, LANES), 'grp', split_axi...  53.6 us
    all_to_all x4, blocking collectives, body(): lax.all_to_all(part.reshape(owners, tiles, width), 'own', split_axis=0, c...  39.6 us
    all_to_all x1, starting transfers between devices, body(): lax.all_to_all(outgoing.reshape(groups, 2 * cap, LANES), 'grp', split_axi...  19.1 us
    all_to_all x1, waiting for transfers between devices, body(): lax.all_to_all(outgoing.reshape(groups, 2 * cap, LANES), 'grp', split_axi...  11.6 us
    pallas_call x3, Pallas kernels, body(): call(functools.partial(far_kernel, step), 'far', (sums, shape((tiles, wid...  3.34 us
  transfers between devices with their start and end apart: 1, of which 1 were waited for; matrix products, arithmetic and copies ran while one was open for 0% of the time, Pallas kernels for 2%

profile of v7, /device:TPU:1, one launch (start us, length us, event | category | flops | bytes accessed | tf_op | source)
XLA Modules:
  0.0 136.1 jit_solution(16629212350889036869)
XLA Ops:
  0.6 1.8 %first.1 = (bf16[256,128]{1,0:T(8,128)(2,1)S(1)}, bf16[256,128]{1,0:T(8,128)(2,1)}) custom-call(s32[4,16]{1,0:T(4,128)} %bitcast.43, s32[4,16]{1,0:T(4,128)} %bitcast.44, bf16[64,256]{1,0:T(8,128)(2,1)} %bitcast.32), custom_call_target="tpu_custom_call" | custom-call | tf_op jit(solution)/shard_map/first/pallas_call | solution.py:333
  2.4 19.1 %all-to-all-start = ((bf16[64,4,128]{2,1,0:T(4,128)(2,1)}), bf16[64,4,128]{2,1,0:T(4,128)(2,1)S(1)}, u32[]{:S(2)}, u32[]{:S(2)}) async-start(bf16[64,4,128]{2,1,0:T(4,128)(2,1)} %bitcast.3), calls=%async_computation | async-start | bytes 131072 | tf_op jit(solution)/shard_map/all_to_all | solution.py:392
  21.6 2.4 %tables.1 = (bf16[128,2048]{1,0:T(8,128)(2,1)S(1)}, bf16[256,256]{1,0:T(8,128)(2,1)S(1)}, bf16[64,64]{1,0:T(8,128)(2,1)S(1)}, f32[3,16,256]{2,1,0:T(8,128)S(1)},...) custom-call(f32[16]{0:T(128)} %pole_hbm.1, ...), custom_call_target="tpu_custom_call" | custom-call | tf_op jit(solution)/shard_map/tables/pallas_call | solution.py:349
  24.0 0.0 copy-start.3
  24.0 0.0 copy-start.4
  24.0 11.6 %all-to-all-done = bf16[64,4,128]{2,1,0:T(4,128)(2,1)S(1)} async-done(((bf16[64,4,128]{2,1,0:T(4,128)(2,1)}), bf16[64,4,128]{2,1,0:T(4,128)(2,1)S(1)}, u32[]{:S(2)}, u32[]{:S(2)}) %all-to-all-start) | async-done | bytes 65568 | tf_op jit(solution)/shard_map/all_to_all | solution.py:392
  35.6 0.0 copy-start
  35.6 0.0 copy-start.2
  35.6 0.8 far.4
  36.4 11.3 %all_to_all.40.parts_ref = bf16[8,16,256]{2,1,0:T(8,128)(2,1)S(1)} all-to-all(bf16[8,16,256]{2,1,0:T(8,128)(2,1)S(1)} %bitcast.29), channel_id=1, replica_groups=mesh['grp'=64,'own'=8] {'own'}, dimensions={0} | all-to-all | bytes 131072 | tf_op jit(solution)/shard_map/all_to_all | solution.py:414
  47.7 0.0 copy-done.3
  47.7 0.0 copy-done.4
  47.7 0.0 copy-done
  47.7 0.9 step.3
  48.6 17.8 %all_to_all.41 = bf16[64,4,128]{2,1,0:T(4,128)(2,1)S(1)} all-to-all(bf16[64,4,128]{2,1,0:T(4,128)(2,1)S(1)} %bitcast.37), channel_id=1, replica_groups=mesh['grp'=64,'own'=8] {'grp'}, dimensions={0} | all-to-all | bytes 131072 | tf_op jit(solution)/shard_map/all_to_all | solution.py:392
  66.4 0.0 copy-done.2
  66.4 1.1 far.5
  67.5 9.5 %all_to_all.42.parts_ref = bf16[8,16,256]{2,1,0:T(8,128)(2,1)S(1)} all-to-all(bf16[8,16,256]{2,1,0:T(8,128)(2,1)S(1)} %bitcast.38), channel_id=1, replica_groups=mesh['grp'=64,'own'=8] {'own'}, dimensions={0} | all-to-all | bytes 131072 | tf_op jit(solution)/shard_map/all_to_all | solution.py:414
  77.0 0.5 step.4
  77.5 17.8 %all_to_all.43 = bf16[64,4,128]{2,1,0:T(4,128)(2,1)S(1)} all-to-all(bf16[64,4,128]{2,1,0:T(4,128)(2,1)S(1)} %bitcast.36), channel_id=1, replica_groups=mesh['grp'=64,'own'=8] {'grp'}, dimensions={0} | all-to-all | bytes 131072 | tf_op jit(solution)/shard_map/all_to_all | solution.py:392
  95.3 1.1 far.6
  96.4 9.5 %all_to_all.44.parts_ref = bf16[8,16,256]{2,1,0:T(8,128)(2,1)S(1)} all-to-all(bf16[8,16,256]{2,1,0:T(8,128)(2,1)S(1)} %bitcast.39), channel_id=1, replica_groups=mesh['grp'=64,'own'=8] {'own'}, dimensions={0} | all-to-all | bytes 131072 | tf_op jit(solution)/shard_map/all_to_all | solution.py:414
  105.9 0.5 step.5
  106.4 0.0 copy-start.1
  106.4 17.9 %all_to_all.45 = bf16[64,4,128]{2,1,0:T(4,128)(2,1)S(1)} all-to-all(bf16[64,4,128]{2,1,0:T(4,128)(2,1)S(1)} %bitcast.35), channel_id=1, replica_groups=mesh['grp'=64,'own'=8] {'grp'}, dimensions={0} | all-to-all | bytes 131072 | tf_op jit(solution)/shard_map/all_to_all | solution.py:392
  124.4 1.1 far.7
  125.5 9.5 %all_to_all.46.parts_ref = bf16[8,16,256]{2,1,0:T(8,128)(2,1)S(1)} all-to-all(bf16[8,16,256]{2,1,0:T(8,128)(2,1)S(1)} %bitcast.34), channel_id=1, replica_groups=mesh['grp'=64,'own'=8] {'own'}, dimensions={0} | all-to-all | bytes 131072 | tf_op jit(solution)/shard_map/all_to_all | solution.py:414
  135.0 0.0 copy-done.1
  135.0 1.1 last.1
Async XLA Ops:
  2.4 33.1 %all-to-all-start = ((bf16[64,4,128]{2,1,0:T(4,128)(2,1)}), bf16[64,4,128]{2,1,0:T(4,128)(2,1)S(1)}, u32[]{:S(2)}, u32[]{:S(2)}) async-start(bf16[64,4,128]{2,1,0:T(4,128)(2,1)} %bitcast.3), calls=%async_computation | async-start | bytes 131072 | tf_op jit(solution)/shard_map/all_to_all | solution.py:392
  24.0 23.7 %copy-start.3 = (bf16[4,16,256]{2,1,0:T(8,128)(2,1)S(1)}, bf16[4,16,256]{2,1,0:T(8,128)(2,1)}, u32[]{:S(2)}) copy-start(bf16[4,16,256]{2,1,0:T(8,128)(2,1)} %param.15) | copy-start | bytes 98308
  24.0 23.7 %copy-start.4 = (bf16[4,16,256]{2,1,0:T(8,128)(2,1)S(1)}, bf16[4,16,256]{2,1,0:T(8,128)(2,1)}, u32[]{:S(2)}) copy-start(bf16[4,16,256]{2,1,0:T(8,128)(2,1)} %param.16) | copy-start | bytes 98308
  35.6 12.1 %copy-start = (bf16[16,256,256]{2,1,0:T(8,128)(2,1)S(1)}, bf16[16,256,256]{2,1,0:T(8,128)(2,1)}, u32[]{:S(2)}) copy-start(bf16[16,256,256]{2,1,0:T(8,128)(2,1)} %inverse_ref.1) | copy-start | bytes 6291460
  35.6 30.8 %copy-start.2 = (bf16[4,16,256]{2,1,0:T(8,128)(2,1)S(1)}, bf16[4,16,256]{2,1,0:T(8,128)(2,1)}, u32[]{:S(2)}) copy-start(bf16[4,16,256]{2,1,0:T(8,128)(2,1)} %rest_7_.5) | copy-start | bytes 98308
  106.4 28.5 %copy-start.1 = (f32[16,16,256]{2,1,0:T(8,128)S(1)}, f32[16,16,256]{2,1,0:T(8,128)}, u32[]{:S(2)}) copy-start(f32[16,16,256]{2,1,0:T(8,128)} %state_ref.1) | copy-start | bytes 786436

commit v8 on v6

--- a/solution.py
+++ b/solution.py
@@ -106,11 +106,13 @@
     slots = cap * groups
     group_tiles = hits_ref.shape[0]
     slot = lax.broadcasted_iota(I32, (slots, 1), 0)
-    row = lax.broadcasted_iota(I32, split_ref.shape[1:], 1)
+    row = lax.broadcasted_iota(I32, (slots, 2 * slots), 1)
     group_bits = groups.bit_length() - 1
     start = 4 * (slot & (groups - 1)) + shifted(slot, group_bits)
     for h in range(2):
-        split_ref[h] = jnp.where(row == start + 2 * h, 1.0, 0.0).astype(BF16)
+        split_ref[h * slots : (h + 1) * slots, :] = jnp.where(
+            row == start + 2 * h, 1.0, 0.0
+        ).astype(BF16)
     reader_copy.wait()
     readers = jnp.concatenate([reader_ref[c] for c in range(cap)], axis=1)
     place = lax.broadcasted_iota(I32, (group_tiles, slots), 0)
@@ -172,14 +174,9 @@
 
 
 def entries_of(in_ref, split_ref):
-    incoming = in_ref[...]
-    return jnp.concatenate(
-        [
-            lax.dot(split_ref[h], incoming, preferred_element_type=F32).astype(BF16)
-            for h in range(2)
-        ],
-        axis=1,
-    )
+    halves = lax.dot(split_ref[...], in_ref[...], preferred_element_type=F32).astype(BF16)
+    slots = halves.shape[0] // 2
+    return jnp.concatenate([halves[:slots], halves[slots:]], axis=1)
 
 
 def near_base(step, near_pick_ref, cur_ref, near_ref, exc_ref):
@@ -210,8 +207,9 @@
 
 def far_kernel(step, in_ref, split_ref, hits_ref, *rest):
     *turned, near_pick_ref, cur_ref, near_ref, exc_ref, part_ref, base_ref, terms_ref = rest
-    far_terms(entries_of(in_ref, split_ref), turned, terms_ref)
+    entries = entries_of(in_ref, split_ref)
     base_ref[...] = near_base(step, near_pick_ref, cur_ref, near_ref, exc_ref)
+    far_terms(entries, turned, terms_ref)
     part_ref[...] = lax.dot(
         hits_ref[...], terms_ref[...], preferred_element_type=F32
     ).astype(BF16)
@@ -338,7 +336,7 @@
         "tables",
         (
             shape((group_tiles, classes * slots), BF16),
-            shape((2, slots, 2 * slots), BF16),
+            shape((2 * slots, 2 * slots), BF16),
             shape((sources * tiles, past), BF16),
             shape((STEPS - 1, tiles, width), F32),
             shape((8 + poles_count, width), F32),

time: 136 us -> 136 us (level)
  no operation moved by 1% of the time
where the time goes in v8:
time: 136 us; the launch traced here: 135 us
  blocking collectives  93.2 us (69%)
  starting transfers between devices  19.1 us (14%)
  waiting for transfers between devices  11.6 us (9%)
  Pallas kernels  10.5 us (8%)
    all_to_all x3, blocking collectives, body(): lax.all_to_all(outgoing.reshape(groups, 2 * cap, LANES), 'grp', split_axi...  53.6 us
    all_to_all x4, blocking collectives, body(): lax.all_to_all(part.reshape(owners, tiles, width), 'own', split_axis=0, c...  39.6 us
    all_to_all x1, starting transfers between devices, body(): lax.all_to_all(outgoing.reshape(groups, 2 * cap, LANES), 'grp', split_axi...  19.1 us
    all_to_all x1, waiting for transfers between devices, body(): lax.all_to_all(outgoing.reshape(groups, 2 * cap, LANES), 'grp', split_axi...  11.6 us
  transfers between devices with their start and end apart: 1, of which 1 were waited for; matrix products, arithmetic and copies ran while one was open for 0% of the time, Pallas kernels for 2%

profile of v8, /device:TPU:1, one launch (start us, length us, event | category | flops | bytes accessed | tf_op | source)
XLA Modules:
  0.0 135.2 jit_solution(15438002110856783726)
XLA Ops:
  0.6 1.8 %first.1 = (bf16[256,128]{1,0:T(8,128)(2,1)S(1)}, bf16[256,128]{1,0:T(8,128)(2,1)}) custom-call(s32[4,16]{1,0:T(4,128)} %bitcast.43, s32[4,16]{1,0:T(4,128)} %bitcast.44, bf16[64,256]{1,0:T(8,128)(2,1)} %bitcast.32), custom_call_target="tpu_custom_call" | custom-call | tf_op jit(solution)/shard_map/first/pallas_call | solution.py:318
  2.4 19.1 %all-to-all-start = ((bf16[64,4,128]{2,1,0:T(4,128)(2,1)}), bf16[64,4,128]{2,1,0:T(4,128)(2,1)S(1)}, u32[]{:S(2)}, u32[]{:S(2)}) async-start(bf16[64,4,128]{2,1,0:T(4,128)(2,1)} %bitcast.3), calls=%async_computation | async-start | bytes 131072 | tf_op jit(solution)/shard_map/all_to_all | solution.py:376
  21.6 2.4 %tables.1 = (bf16[128,2048]{1,0:T(8,128)(2,1)S(1)}, bf16[256,256]{1,0:T(8,128)(2,1)S(1)}, bf16[64,64]{1,0:T(8,128)(2,1)S(1)}, f32[3,16,256]{2,1,0:T(8,128)S(1)},...) custom-call(f32[16]{0:T(128)} %pole_hbm.1, ...), custom_call_target="tpu_custom_call" | custom-call | tf_op jit(solution)/shard_map/tables/pallas_call | solution.py:334
  24.0 0.0 copy-start.4
  24.0 0.0 copy-start.5
  24.0 11.6 %all-to-all-done = bf16[64,4,128]{2,1,0:T(4,128)(2,1)S(1)} async-done(((bf16[64,4,128]{2,1,0:T(4,128)(2,1)}), bf16[64,4,128]{2,1,0:T(4,128)(2,1)S(1)}, u32[]{:S(2)}, u32[]{:S(2)}) %all-to-all-start) | async-done | bytes 65568 | tf_op jit(solution)/shard_map/all_to_all | solution.py:376
  35.6 0.0 copy-start.1
  35.6 0.0 copy-start
  35.6 0.0 copy-start.3
  35.6 0.8 far.4
  36.4 11.3 %all_to_all.40.parts_ref = bf16[8,16,256]{2,1,0:T(8,128)(2,1)S(1)} all-to-all(bf16[8,16,256]{2,1,0:T(8,128)(2,1)S(1)} %bitcast.29), channel_id=1, replica_groups=mesh['grp'=64,'own'=8] {'own'}, dimensions={0} | all-to-all | bytes 131072 | tf_op jit(solution)/shard_map/all_to_all | solution.py:398
  47.7 0.0 copy-done.4
  47.7 0.0 copy-done.5
  47.7 0.0 copy-done.1
  47.7 0.9 step.3
  48.6 17.8 %all_to_all.41 = bf16[64,4,128]{2,1,0:T(4,128)(2,1)S(1)} all-to-all(bf16[64,4,128]{2,1,0:T(4,128)(2,1)S(1)} %bitcast.37), channel_id=1, replica_groups=mesh['grp'=64,'own'=8] {'grp'}, dimensions={0} | all-to-all | bytes 131072 | tf_op jit(solution)/shard_map/all_to_all | solution.py:376
  66.4 0.0 copy-done
  66.4 0.0 copy-done.3
  66.4 0.8 far.5
  67.2 9.5 %all_to_all.42.parts_ref = bf16[8,16,256]{2,1,0:T(8,128)(2,1)S(1)} all-to-all(bf16[8,16,256]{2,1,0:T(8,128)(2,1)S(1)} %bitcast.38), channel_id=1, replica_groups=mesh['grp'=64,'own'=8] {'own'}, dimensions={0} | all-to-all | bytes 131072 | tf_op jit(solution)/shard_map/all_to_all | solution.py:398
  76.7 0.5 step.4
  77.2 17.8 %all_to_all.43 = bf16[64,4,128]{2,1,0:T(4,128)(2,1)S(1)} all-to-all(bf16[64,4,128]{2,1,0:T(4,128)(2,1)S(1)} %bitcast.36), channel_id=1, replica_groups=mesh['grp'=64,'own'=8] {'grp'}, dimensions={0} | all-to-all | bytes 131072 | tf_op jit(solution)/shard_map/all_to_all | solution.py:376
  95.0 0.8 far.6
  95.8 9.5 %all_to_all.44.parts_ref = bf16[8,16,256]{2,1,0:T(8,128)(2,1)S(1)} all-to-all(bf16[8,16,256]{2,1,0:T(8,128)(2,1)S(1)} %bitcast.39), channel_id=1, replica_groups=mesh['grp'=64,'own'=8] {'own'}, dimensions={0} | all-to-all | bytes 131072 | tf_op jit(solution)/shard_map/all_to_all | solution.py:398
  105.3 0.5 step.5
  105.8 0.0 copy-start.2
  105.8 17.9 %all_to_all.45 = bf16[64,4,128]{2,1,0:T(4,128)(2,1)S(1)} all-to-all(bf16[64,4,128]{2,1,0:T(4,128)(2,1)S(1)} %bitcast.35), channel_id=1, replica_groups=mesh['grp'=64,'own'=8] {'grp'}, dimensions={0} | all-to-all | bytes 131072 | tf_op jit(solution)/shard_map/all_to_all | solution.py:376
  123.8 0.8 far.7
  124.6 9.5 %all_to_all.46.parts_ref = bf16[8,16,256]{2,1,0:T(8,128)(2,1)S(1)} all-to-all(bf16[8,16,256]{2,1,0:T(8,128)(2,1)S(1)} %bitcast.34), channel_id=1, replica_groups=mesh['grp'=64,'own'=8] {'own'}, dimensions={0} | all-to-all | bytes 131072 | tf_op jit(solution)/shard_map/all_to_all | solution.py:398
  134.1 0.0 copy-done.2
  134.1 1.1 last.1
Async XLA Ops:
  2.4 33.1 %all-to-all-start = ((bf16[64,4,128]{2,1,0:T(4,128)(2,1)}), bf16[64,4,128]{2,1,0:T(4,128)(2,1)S(1)}, u32[]{:S(2)}, u32[]{:S(2)}) async-start(bf16[64,4,128]{2,1,0:T(4,128)(2,1)} %bitcast.3), calls=%async_computation | async-start | bytes 131072 | tf_op jit(solution)/shard_map/all_to_all | solution.py:376
  24.0 23.7 %copy-start.4 = (bf16[4,16,256]{2,1,0:T(8,128)(2,1)S(1)}, bf16[4,16,256]{2,1,0:T(8,128)(2,1)}, u32[]{:S(2)}) copy-start(bf16[4,16,256]{2,1,0:T(8,128)(2,1)} %param.15) | copy-start | bytes 98308
  24.0 23.7 %copy-start.5 = (bf16[4,16,256]{2,1,0:T(8,128)(2,1)S(1)}, bf16[4,16,256]{2,1,0:T(8,128)(2,1)}, u32[]{:S(2)}) copy-start(bf16[4,16,256]{2,1,0:T(8,128)(2,1)} %param.16) | copy-start | bytes 98308
  35.6 12.1 %copy-start.1 = (bf16[16,256,256]{2,1,0:T(8,128)(2,1)S(1)}, bf16[16,256,256]{2,1,0:T(8,128)(2,1)}, u32[]{:S(2)}) copy-start(bf16[16,256,256]{2,1,0:T(8,128)(2,1)} %inverse_ref.1) | copy-start | bytes 6291460
  35.6 30.8 %copy-start = (bf16[2,256,256]{2,1,0:T(8,128)(2,1)S(1)}, bf16[2,256,256]{2,1,0:T(8,128)(2,1)}, u32[]{:S(2)}) copy-start(bf16[2,256,256]{2,1,0:T(8,128)(2,1)} %rest_6_.5) | copy-start | bytes 786436
  35.6 30.8 %copy-start.3 = (bf16[4,16,256]{2,1,0:T(8,128)(2,1)S(1)}, bf16[4,16,256]{2,1,0:T(8,128)(2,1)}, u32[]{:S(2)}) copy-start(bf16[4,16,256]{2,1,0:T(8,128)(2,1)} %rest_7_.5) | copy-start | bytes 98308
  105.8 28.2 %copy-start.2 = (f32[16,16,256]{2,1,0:T(8,128)S(1)}, f32[16,16,256]{2,1,0:T(8,128)}, u32[]{:S(2)}) copy-start(f32[16,16,256]{2,1,0:T(8,128)} %state_ref.1) | copy-start | bytes 786436

commit v9 on v8

--- a/solution.py
+++ b/solution.py
@@ -228,9 +228,13 @@
         if turned_ref is not None:
             turned = turned.T
             turned_ref[t] = turned
-        current = jnp.where(
-            row == t, lax.dot(right_side, turned, preferred_element_type=F32), current
-        )
+        if turned_ref is not None and t % 2 == 0:
+            product = lax.dot_general(
+                right_side, inverse_ref[t], CONTRACT_LAST, preferred_element_type=F32
+            )
+        else:
+            product = lax.dot(right_side, turned, preferred_element_type=F32)
+        current = jnp.where(row == t, product, current)
     return current.astype(BF16)
 
 

time: 136 us -> 136 us (level)
  no operation moved by 1% of the time
where the time goes in v9:
time: 136 us; the launch traced here: 135 us
  blocking collectives  93.2 us (69%)
  starting transfers between devices  19.1 us (14%)
  waiting for transfers between devices  11.6 us (9%)
  Pallas kernels  10.4 us (8%)
    all_to_all x3, blocking collectives, body(): lax.all_to_all(outgoing.reshape(groups, 2 * cap, LANES), 'grp', split_axi...  53.5 us
    all_to_all x4, blocking collectives, body(): lax.all_to_all(part.reshape(owners, tiles, width), 'own', split_axis=0, c...  39.6 us
    all_to_all x1, starting transfers between devices, body(): lax.all_to_all(outgoing.reshape(groups, 2 * cap, LANES), 'grp', split_axi...  19.1 us
    all_to_all x1, waiting for transfers between devices, body(): lax.all_to_all(outgoing.reshape(groups, 2 * cap, LANES), 'grp', split_axi...  11.6 us
  transfers between devices with their start and end apart: 1, of which 1 were waited for; matrix products, arithmetic and copies ran while one was open for 0% of the time, Pallas kernels for 2%

profile of v9, /device:TPU:1, one launch (start us, length us, event | category | flops | bytes accessed | tf_op | source)
XLA Modules:
  0.0 135.1 jit_solution(3467792665576936578)
XLA Ops:
  0.6 1.8 %first.1 = (bf16[256,128]{1,0:T(8,128)(2,1)S(1)}, bf16[256,128]{1,0:T(8,128)(2,1)}) custom-call(s32[4,16]{1,0:T(4,128)} %bitcast.43, s32[4,16]{1,0:T(4,128)} %bitcast.44, bf16[64,256]{1,0:T(8,128)(2,1)} %bitcast.32), custom_call_target="tpu_custom_call" | custom-call | tf_op jit(solution)/shard_map/first/pallas_call | solution.py:322
  2.4 19.1 %all-to-all-start = ((bf16[64,4,128]{2,1,0:T(4,128)(2,1)}), bf16[64,4,128]{2,1,0:T(4,128)(2,1)S(1)}, u32[]{:S(2)}, u32[]{:S(2)}) async-start(bf16[64,4,128]{2,1,0:T(4,128)(2,1)} %bitcast.3), calls=%async_computation | async-start | bytes 131072 | tf_op jit(solution)/shard_map/all_to_all | solution.py:380
  21.6 2.4 %tables.1 = (bf16[128,2048]{1,0:T(8,128)(2,1)S(1)}, bf16[256,256]{1,0:T(8,128)(2,1)S(1)}, bf16[64,64]{1,0:T(8,128)(2,1)S(1)}, f32[3,16,256]{2,1,0:T(8,128)S(1)},...) custom-call(f32[16]{0:T(128)} %pole_hbm.1, ...), custom_call_target="tpu_custom_call" | custom-call | tf_op jit(solution)/shard_map/tables/pallas_call | solution.py:338
  24.0 0.0 copy-start.4
  24.0 0.0 copy-start.5
  24.0 11.6 %all-to-all-done = bf16[64,4,128]{2,1,0:T(4,128)(2,1)S(1)} async-done(((bf16[64,4,128]{2,1,0:T(4,128)(2,1)}), bf16[64,4,128]{2,1,0:T(4,128)(2,1)S(1)}, u32[]{:S(2)}, u32[]{:S(2)}) %all-to-all-start) | async-done | bytes 65568 | tf_op jit(solution)/shard_map/all_to_all | solution.py:380
  35.6 0.0 copy-start.1
  35.6 0.0 copy-start
  35.6 0.0 copy-start.3
  35.6 0.8 far.4
  36.4 11.3 %all_to_all.40.parts_ref = bf16[8,16,256]{2,1,0:T(8,128)(2,1)S(1)} all-to-all(bf16[8,16,256]{2,1,0:T(8,128)(2,1)S(1)} %bitcast.29), channel_id=1, replica_groups=mesh['grp'=64,'own'=8] {'own'}, dimensions={0} | all-to-all | bytes 131072 | tf_op jit(solution)/shard_map/all_to_all | solution.py:402
  47.7 0.0 copy-done.4
  47.7 0.0 copy-done.5
  47.7 0.0 copy-done.1
  47.7 0.8 step.3
  48.5 17.8 %all_to_all.41 = bf16[64,4,128]{2,1,0:T(4,128)(2,1)S(1)} all-to-all(bf16[64,4,128]{2,1,0:T(4,128)(2,1)S(1)} %bitcast.37), channel_id=1, replica_groups=mesh['grp'=64,'own'=8] {'grp'}, dimensions={0} | all-to-all | bytes 131072 | tf_op jit(solution)/shard_map/all_to_all | solution.py:380
  66.3 0.0 copy-done
  66.3 0.0 copy-done.3
  66.3 0.8 far.5
  67.1 9.5 %all_to_all.42.parts_ref = bf16[8,16,256]{2,1,0:T(8,128)(2,1)S(1)} all-to-all(bf16[8,16,256]{2,1,0:T(8,128)(2,1)S(1)} %bitcast.38), channel_id=1, replica_groups=mesh['grp'=64,'own'=8] {'own'}, dimensions={0} | all-to-all | bytes 131072 | tf_op jit(solution)/shard_map/all_to_all | solution.py:402
  76.5 0.5 step.4
  77.1 17.8 %all_to_all.43 = bf16[64,4,128]{2,1,0:T(4,128)(2,1)S(1)} all-to-all(bf16[64,4,128]{2,1,0:T(4,128)(2,1)S(1)} %bitcast.36), channel_id=1, replica_groups=mesh['grp'=64,'own'=8] {'grp'}, dimensions={0} | all-to-all | bytes 131072 | tf_op jit(solution)/shard_map/all_to_all | solution.py:380
  94.9 0.8 far.6
  95.7 9.5 %all_to_all.44.parts_ref = bf16[8,16,256]{2,1,0:T(8,128)(2,1)S(1)} all-to-all(bf16[8,16,256]{2,1,0:T(8,128)(2,1)S(1)} %bitcast.39), channel_id=1, replica_groups=mesh['grp'=64,'own'=8] {'own'}, dimensions={0} | all-to-all | bytes 131072 | tf_op jit(solution)/shard_map/all_to_all | solution.py:402
  105.2 0.5 step.5
  105.7 0.0 copy-start.2
  105.7 17.9 %all_to_all.45 = bf16[64,4,128]{2,1,0:T(4,128)(2,1)S(1)} all-to-all(bf16[64,4,128]{2,1,0:T(4,128)(2,1)S(1)} %bitcast.35), channel_id=1, replica_groups=mesh['grp'=64,'own'=8] {'grp'}, dimensions={0} | all-to-all | bytes 131072 | tf_op jit(solution)/shard_map/all_to_all | solution.py:380
  123.7 0.8 far.7
  124.5 9.5 %all_to_all.46.parts_ref = bf16[8,16,256]{2,1,0:T(8,128)(2,1)S(1)} all-to-all(bf16[8,16,256]{2,1,0:T(8,128)(2,1)S(1)} %bitcast.34), channel_id=1, replica_groups=mesh['grp'=64,'own'=8] {'own'}, dimensions={0} | all-to-all | bytes 131072 | tf_op jit(solution)/shard_map/all_to_all | solution.py:402
  133.9 0.0 copy-done.2
  133.9 1.1 last.1
Async XLA Ops:
  2.4 33.1 %all-to-all-start = ((bf16[64,4,128]{2,1,0:T(4,128)(2,1)}), bf16[64,4,128]{2,1,0:T(4,128)(2,1)S(1)}, u32[]{:S(2)}, u32[]{:S(2)}) async-start(bf16[64,4,128]{2,1,0:T(4,128)(2,1)} %bitcast.3), calls=%async_computation | async-start | bytes 131072 | tf_op jit(solution)/shard_map/all_to_all | solution.py:380
  24.0 23.7 %copy-start.4 = (bf16[4,16,256]{2,1,0:T(8,128)(2,1)S(1)}, bf16[4,16,256]{2,1,0:T(8,128)(2,1)}, u32[]{:S(2)}) copy-start(bf16[4,16,256]{2,1,0:T(8,128)(2,1)} %param.15) | copy-start | bytes 98308
  24.0 23.7 %copy-start.5 = (bf16[4,16,256]{2,1,0:T(8,128)(2,1)S(1)}, bf16[4,16,256]{2,1,0:T(8,128)(2,1)}, u32[]{:S(2)}) copy-start(bf16[4,16,256]{2,1,0:T(8,128)(2,1)} %param.16) | copy-start | bytes 98308
  35.6 12.1 %copy-start.1 = (bf16[16,256,256]{2,1,0:T(8,128)(2,1)S(1)}, bf16[16,256,256]{2,1,0:T(8,128)(2,1)}, u32[]{:S(2)}) copy-start(bf16[16,256,256]{2,1,0:T(8,128)(2,1)} %inverse_ref.1) | copy-start | bytes 6291460
  35.6 30.7 %copy-start = (bf16[2,256,256]{2,1,0:T(8,128)(2,1)S(1)}, bf16[2,256,256]{2,1,0:T(8,128)(2,1)}, u32[]{:S(2)}) copy-start(bf16[2,256,256]{2,1,0:T(8,128)(2,1)} %rest_6_.5) | copy-start | bytes 786436
  35.6 30.7 %copy-start.3 = (bf16[4,16,256]{2,1,0:T(8,128)(2,1)S(1)}, bf16[4,16,256]{2,1,0:T(8,128)(2,1)}, u32[]{:S(2)}) copy-start(bf16[4,16,256]{2,1,0:T(8,128)(2,1)} %rest_7_.5) | copy-start | bytes 98308
  105.7 28.2 %copy-start.2 = (f32[16,16,256]{2,1,0:T(8,128)S(1)}, f32[16,16,256]{2,1,0:T(8,128)}, u32[]{:S(2)}) copy-start(f32[16,16,256]{2,1,0:T(8,128)} %state_ref.1) | copy-start | bytes 786436

commit v10 on v9

--- a/solution.py
+++ b/solution.py
@@ -228,7 +228,7 @@
         if turned_ref is not None:
             turned = turned.T
             turned_ref[t] = turned
-        if turned_ref is not None and t % 2 == 0:
+        if turned_ref is not None and t % 4 != 3:
             product = lax.dot_general(
                 right_side, inverse_ref[t], CONTRACT_LAST, preferred_element_type=F32
             )

time: 136 us -> 136 us (level)
  no operation moved by 1% of the time
where the time goes in v10:
time: 136 us; the launch traced here: 135 us
  blocking collectives  93.2 us (69%)
  starting transfers between devices  19.1 us (14%)
  waiting for transfers between devices  11.6 us (9%)
  Pallas kernels  10.4 us (8%)
    all_to_all x3, blocking collectives, body(): lax.all_to_all(outgoing.reshape(groups, 2 * cap, LANES), 'grp', split_axi...  53.5 us
    all_to_all x4, blocking collectives, body(): lax.all_to_all(part.reshape(owners, tiles, width), 'own', split_axis=0, c...  39.6 us
    all_to_all x1, starting transfers between devices, body(): lax.all_to_all(outgoing.reshape(groups, 2 * cap, LANES), 'grp', split_axi...  19.1 us
    all_to_all x1, waiting for transfers between devices, body(): lax.all_to_all(outgoing.reshape(groups, 2 * cap, LANES), 'grp', split_axi...  11.6 us
  transfers between devices with their start and end apart: 1, of which 1 were waited for; matrix products, arithmetic and copies ran while one was open for 0% of the time, Pallas kernels for 2%

profile of v10, /device:TPU:1, one launch (start us, length us, event | category | flops | bytes accessed | tf_op | source)
XLA Modules:
  0.0 135.1 jit_solution(5557219528119744181)
XLA Ops:
  0.6 1.8 %first.1 = (bf16[256,128]{1,0:T(8,128)(2,1)S(1)}, bf16[256,128]{1,0:T(8,128)(2,1)}) custom-call(s32[4,16]{1,0:T(4,128)} %bitcast.43, s32[4,16]{1,0:T(4,128)} %bitcast.44, bf16[64,256]{1,0:T(8,128)(2,1)} %bitcast.32), custom_call_target="tpu_custom_call" | custom-call | tf_op jit(solution)/shard_map/first/pallas_call | solution.py:322
  2.4 19.1 %all-to-all-start = ((bf16[64,4,128]{2,1,0:T(4,128)(2,1)}), bf16[64,4,128]{2,1,0:T(4,128)(2,1)S(1)}, u32[]{:S(2)}, u32[]{:S(2)}) async-start(bf16[64,4,128]{2,1,0:T(4,128)(2,1)} %bitcast.3), calls=%async_computation | async-start | bytes 131072 | tf_op jit(solution)/shard_map/all_to_all | solution.py:380
  21.6 2.4 %tables.1 = (bf16[128,2048]{1,0:T(8,128)(2,1)S(1)}, bf16[256,256]{1,0:T(8,128)(2,1)S(1)}, bf16[64,64]{1,0:T(8,128)(2,1)S(1)}, f32[3,16,256]{2,1,0:T(8,128)S(1)},...) custom-call(f32[16]{0:T(128)} %pole_hbm.1, ...), custom_call_target="tpu_custom_call" | custom-call | tf_op jit(solution)/shard_map/tables/pallas_call | solution.py:338
  24.0 0.0 copy-start.4
  24.0 0.0 copy-start.5
  24.0 11.6 %all-to-all-done = bf16[64,4,128]{2,1,0:T(4,128)(2,1)S(1)} async-done(((bf16[64,4,128]{2,1,0:T(4,128)(2,1)}), bf16[64,4,128]{2,1,0:T(4,128)(2,1)S(1)}, u32[]{:S(2)}, u32[]{:S(2)}) %all-to-all-start) | async-done | bytes 65568 | tf_op jit(solution)/shard_map/all_to_all | solution.py:380
  35.6 0.0 copy-start.1
  35.6 0.0 copy-start
  35.6 0.0 copy-start.3
  35.6 0.8 far.4
  36.4 11.3 %all_to_all.40.parts_ref = bf16[8,16,256]{2,1,0:T(8,128)(2,1)S(1)} all-to-all(bf16[8,16,256]{2,1,0:T(8,128)(2,1)S(1)} %bitcast.29), channel_id=1, replica_groups=mesh['grp'=64,'own'=8] {'own'}, dimensions={0} | all-to-all | bytes 131072 | tf_op jit(solution)/shard_map/all_to_all | solution.py:402
  47.7 0.0 copy-done.4
  47.7 0.0 copy-done.5
  47.7 0.0 copy-done.1
  47.7 0.8 step.3
  48.5 17.8 %all_to_all.41 = bf16[64,4,128]{2,1,0:T(4,128)(2,1)S(1)} all-to-all(bf16[64,4,128]{2,1,0:T(4,128)(2,1)S(1)} %bitcast.37), channel_id=1, replica_groups=mesh['grp'=64,'own'=8] {'grp'}, dimensions={0} | all-to-all | bytes 131072 | tf_op jit(solution)/shard_map/all_to_all | solution.py:380
  66.3 0.0 copy-done
  66.3 0.0 copy-done.3
  66.3 0.8 far.5
  67.1 9.5 %all_to_all.42.parts_ref = bf16[8,16,256]{2,1,0:T(8,128)(2,1)S(1)} all-to-all(bf16[8,16,256]{2,1,0:T(8,128)(2,1)S(1)} %bitcast.38), channel_id=1, replica_groups=mesh['grp'=64,'own'=8] {'own'}, dimensions={0} | all-to-all | bytes 131072 | tf_op jit(solution)/shard_map/all_to_all | solution.py:402
  76.5 0.5 step.4
  77.1 17.8 %all_to_all.43 = bf16[64,4,128]{2,1,0:T(4,128)(2,1)S(1)} all-to-all(bf16[64,4,128]{2,1,0:T(4,128)(2,1)S(1)} %bitcast.36), channel_id=1, replica_groups=mesh['grp'=64,'own'=8] {'grp'}, dimensions={0} | all-to-all | bytes 131072 | tf_op jit(solution)/shard_map/all_to_all | solution.py:380
  94.9 0.8 far.6
  95.7 9.5 %all_to_all.44.parts_ref = bf16[8,16,256]{2,1,0:T(8,128)(2,1)S(1)} all-to-all(bf16[8,16,256]{2,1,0:T(8,128)(2,1)S(1)} %bitcast.39), channel_id=1, replica_groups=mesh['grp'=64,'own'=8] {'own'}, dimensions={0} | all-to-all | bytes 131072 | tf_op jit(solution)/shard_map/all_to_all | solution.py:402
  105.2 0.5 step.5
  105.7 0.0 copy-start.2
  105.7 17.9 %all_to_all.45 = bf16[64,4,128]{2,1,0:T(4,128)(2,1)S(1)} all-to-all(bf16[64,4,128]{2,1,0:T(4,128)(2,1)S(1)} %bitcast.35), channel_id=1, replica_groups=mesh['grp'=64,'own'=8] {'grp'}, dimensions={0} | all-to-all | bytes 131072 | tf_op jit(solution)/shard_map/all_to_all | solution.py:380
  123.7 0.8 far.7
  124.5 9.5 %all_to_all.46.parts_ref = bf16[8,16,256]{2,1,0:T(8,128)(2,1)S(1)} all-to-all(bf16[8,16,256]{2,1,0:T(8,128)(2,1)S(1)} %bitcast.34), channel_id=1, replica_groups=mesh['grp'=64,'own'=8] {'own'}, dimensions={0} | all-to-all | bytes 131072 | tf_op jit(solution)/shard_map/all_to_all | solution.py:402
  133.9 0.0 copy-done.2
  133.9 1.1 last.1
Async XLA Ops:
  2.4 33.1 %all-to-all-start = ((bf16[64,4,128]{2,1,0:T(4,128)(2,1)}), bf16[64,4,128]{2,1,0:T(4,128)(2,1)S(1)}, u32[]{:S(2)}, u32[]{:S(2)}) async-start(bf16[64,4,128]{2,1,0:T(4,128)(2,1)} %bitcast.3), calls=%async_computation | async-start | bytes 131072 | tf_op jit(solution)/shard_map/all_to_all | solution.py:380
  24.0 23.7 %copy-start.4 = (bf16[4,16,256]{2,1,0:T(8,128)(2,1)S(1)}, bf16[4,16,256]{2,1,0:T(8,128)(2,1)}, u32[]{:S(2)}) copy-start(bf16[4,16,256]{2,1,0:T(8,128)(2,1)} %param.15) | copy-start | bytes 98308
  24.0 23.7 %copy-start.5 = (bf16[4,16,256]{2,1,0:T(8,128)(2,1)S(1)}, bf16[4,16,256]{2,1,0:T(8,128)(2,1)}, u32[]{:S(2)}) copy-start(bf16[4,16,256]{2,1,0:T(8,128)(2,1)} %param.16) | copy-start | bytes 98308
  35.6 12.1 %copy-start.1 = (bf16[16,256,256]{2,1,0:T(8,128)(2,1)S(1)}, bf16[16,256,256]{2,1,0:T(8,128)(2,1)}, u32[]{:S(2)}) copy-start(bf16[16,256,256]{2,1,0:T(8,128)(2,1)} %inverse_ref.1) | copy-start | bytes 6291460
  35.6 30.7 %copy-start = (bf16[2,256,256]{2,1,0:T(8,128)(2,1)S(1)}, bf16[2,256,256]{2,1,0:T(8,128)(2,1)}, u32[]{:S(2)}) copy-start(bf16[2,256,256]{2,1,0:T(8,128)(2,1)} %rest_6_.5) | copy-start | bytes 786436
  35.6 30.7 %copy-start.3 = (bf16[4,16,256]{2,1,0:T(8,128)(2,1)S(1)}, bf16[4,16,256]{2,1,0:T(8,128)(2,1)}, u32[]{:S(2)}) copy-start(bf16[4,16,256]{2,1,0:T(8,128)(2,1)} %rest_7_.5) | copy-start | bytes 98308
  105.7 28.2 %copy-start.2 = (f32[16,16,256]{2,1,0:T(8,128)S(1)}, f32[16,16,256]{2,1,0:T(8,128)}, u32[]{:S(2)}) copy-start(f32[16,16,256]{2,1,0:T(8,128)} %state_ref.1) | copy-start | bytes 786436
